TPU v7x, 32 devices: a whole 2x2x4 slice. The times are simulated.
32 devices in a mesh: gx: 8 (over z, core), gz: 4 (over y, x).
Axes of the slice: x: 2, y: 2, z: 4, core: 2. Of those that a mesh axis runs over, the one named last changes fastest.
Arguments:
- fields: bfloat16 [4, 4, 512, 8192], P(None, None, 'gz', 'gx'), may hold values from -6 to 6
- strat_sq: float32 [512], P('gz'), may hold values from 0.3 to 3
Outputs:
- tendency: float32 [4, 4, 512, 8192], P(None, None, 'gz', 'gx')
All inputs are finite; a program needn't handle non-finite values.
Results may differ from a plain program's by a relative error of at most 0.0003.
Values may be sent and summed in bfloat16 or wider, within the bound.
No kernel may reach another device: no remote copies, remote signals or barrier semaphores. Data moves between devices by JAX's collectives and lax.ppermute only.
A program may use at most 128 MiB of HBM per device.

v0:
```python
import math

import jax
import jax.numpy as jnp
from jax import lax
from jax.sharding import PartitionSpec as P

NX = 8192


TWO_PI = 2.0 * math.pi
STENCIL = (4.0 / 5.0, -1.0 / 5.0, 4.0 / 105.0, -1.0 / 280.0)
HIGH = lax.Precision.HIGHEST


def extended(block, sides, width):
    for axis, dim in sides:
        count = lax.axis_size(axis)
        forward = [(i, i + 1) for i in range(count - 1)]
        backward = [(target, source) for source, target in forward]
        low = lax.ppermute(
            lax.slice_in_dim(block, block.shape[dim] - width, None, axis=dim), axis, forward
        )
        high = lax.ppermute(lax.slice_in_dim(block, 0, width, axis=dim), axis, backward)
        block = jnp.concatenate([low, block, high], axis=dim)
    return block


def vertical(padded, levels):
    result = jnp.zeros_like(padded[:, :, 4 : 4 + levels])
    for offset in range(1, 5):
        weight = STENCIL[offset - 1]
        result = result + weight * (
            padded[:, :, 4 + offset : 4 + offset + levels]
            - padded[:, :, 4 - offset : 4 - offset + levels]
        )
    return result


def tendencies(values, slope_x, slope_z, strat_col):
    speed_u = values[0]
    speed_w = values[2]
    advect = -(speed_u[None] * slope_x + speed_w[None] * slope_z)
    return jnp.stack([advect[0], advect[1], advect[2] + values[3], advect[3] - strat_col * speed_w])


def rotate(real_part, imag_part, angles, direction):
    cos_tab = jnp.cos(angles)
    sin_tab = direction * jnp.sin(angles)
    return (real_part * cos_tab - imag_part * sin_tab, real_part * sin_tab + imag_part * cos_tab)


def tables(length, direction):
    index_row = jnp.arange(length, dtype=jnp.int32)
    angles = (
        TWO_PI * (index_row[:, None] * index_row[None, :] % length).astype(jnp.float32) / length
    )
    return (jnp.cos(angles), direction * jnp.sin(angles))


def complex_apply(real_part, imag_part, cos_tab, sin_tab, form):
    out_real = jnp.einsum(form, real_part, cos_tab, precision=HIGH) - jnp.einsum(
        form, imag_part, sin_tab, precision=HIGH
    )
    out_imag = jnp.einsum(form, real_part, sin_tab, precision=HIGH) + jnp.einsum(
        form, imag_part, cos_tab, precision=HIGH
    )
    return (out_real, out_imag)


def middle(real_part, imag_part, leading, length_all):
    length = real_part.shape[-1]
    stride = length_all // length
    column = jnp.arange(length, dtype=jnp.int32)
    twist = TWO_PI * (column * leading % length_all).astype(jnp.float32) / length_all
    real_part, imag_part = rotate(real_part, imag_part, twist, -1.0)
    cos_tab, sin_tab = tables(length, -1.0)
    real_part, imag_part = complex_apply(real_part, imag_part, cos_tab, sin_tab, "...j,jk->...k")
    wave_idx = leading + stride * column
    wavenum = jnp.where(wave_idx < length_all // 2, wave_idx, wave_idx - length_all).astype(
        jnp.float32
    ) * (TWO_PI / length_all)
    wavenum = jnp.where(wave_idx == length_all // 2, jnp.zeros_like(wavenum), wavenum)
    real_part, imag_part = (-wavenum * imag_part, wavenum * real_part)
    cos_tab, sin_tab = tables(length, 1.0)
    real_part, imag_part = complex_apply(real_part, imag_part, cos_tab, sin_tab, "...j,jk->...k")
    return rotate(real_part, imag_part, twist, 1.0)


def line_slopes(gathered, devices):
    comps, lines_now, blocks, levels, width = gathered.shape
    batch = comps * lines_now
    values = gathered.astype(jnp.float32).reshape(batch, blocks, levels * width)
    cos_tab, sin_tab = tables(devices, -1.0)
    real_part = jnp.einsum("kp,bpn->kbn", cos_tab, values, precision=HIGH).reshape(
        blocks, batch, levels, width
    )
    imag_part = jnp.einsum("kp,bpn->kbn", sin_tab, values, precision=HIGH).reshape(
        blocks, batch, levels, width
    )
    leading = jnp.arange(devices, dtype=jnp.int32)[:, None, None, None]
    real_part, imag_part = middle(real_part, imag_part, leading, NX)
    cos_tab, sin_tab = tables(devices, 1.0)
    real_part = real_part.reshape(blocks, batch, levels * width)
    imag_part = imag_part.reshape(blocks, batch, levels * width)
    result = jnp.einsum("pk,kbn->pbn", cos_tab, real_part, precision=HIGH) - jnp.einsum(
        "pk,kbn->pbn", sin_tab, imag_part, precision=HIGH
    )
    return result.reshape(blocks, comps, lines_now, levels, width) / NX


def by_whole(blocked):
    devices = lax.axis_size("gx")
    gathered = lax.all_to_all(blocked, "gx", split_axis=2, concat_axis=2, tiled=True)
    result = line_slopes(gathered, devices)
    return lax.all_to_all(result, "gx", split_axis=0, concat_axis=0, tiled=True)


def body(fields, strat_sq):
    comps, lines_now, levels, width = fields.shape
    devices = lax.axis_size("gx")
    values = fields.astype(jnp.float32)
    padded = extended(fields, (("gz", 2),), 4).astype(jnp.float32)
    slope_z = vertical(padded, levels)
    blocked = fields.reshape(comps, lines_now, devices, levels // devices, width)
    returned = by_whole(blocked)
    slope_x = jnp.transpose(returned, (1, 2, 0, 3, 4)).reshape(comps, lines_now, levels, width)
    return tendencies(values, slope_x, slope_z, strat_sq[:, None])


def solution(mesh):
    placed = (P(None, None, "gz", "gx"), P("gz"))
    return jax.shard_map(
        body, mesh=mesh, in_specs=placed, out_specs=P(None, None, "gz", "gx"), check_vma=False
    )
```

profile of v0, /device:TPU:9, one launch (start us, length us, event | category | flops | bytes accessed | tf_op | source)
XLA Modules:
  0.0 708.5 jit_solution(8967977379650984319)
XLA Ops:
  0.0 5.0 copy.21
  5.0 5.6 all-to-all-start
  10.7 0.8 fusion.73
  11.4 0.1 broadcast_multiply_fusion
  11.6 16.2 %fusion.179 = f32[1024,1024,1,1]{1,0,3,2:T(8,128)} fusion(), kind=kLoop, calls=%fused_computation.54.clone.1 | loop fusion | flops 14680064 | bytes 4194304 | tf_op jit(solution)/shard_map/...j,jk->...k/dot_general | solution.py:65
  27.8 16.2 %fusion.177 = f32[1024,1024,1,1]{1,0,3,2:T(8,128)} fusion(), kind=kLoop, calls=%fused_computation.53.clone | loop fusion | flops 14680064 | bytes 4194304 | tf_op jit(solution)/shard_map/...j,jk->...k/dot_general | solution.py:62
  44.0 16.2 %fusion.181 = f32[1024,1024,1,1]{1,0,3,2:T(8,128)} fusion(), kind=kLoop, calls=%fused_computation.52.clone | loop fusion | flops 14680064 | bytes 4194304 | tf_op jit(solution)/shard_map/...j,jk->...k/dot_general | solution.py:62
  60.2 16.2 %fusion.173 = f32[1024,1024,1,1]{1,0,3,2:T(8,128)} fusion(), kind=kLoop, calls=%fused_computation.51.clone.1 | loop fusion | flops 14680064 | bytes 4194304 | tf_op jit(solution)/shard_map/...j,jk->...k/dot_general | solution.py:65
  76.4 16.3 %fusion.175 = f32[1024,1024,1,1]{1,0,3,2:T(8,128)} fusion(), kind=kLoop, calls=%fused_computation.48.clone.1 | loop fusion | flops 14680064 | bytes 4194304 | tf_op jit(solution)/shard_map/...j,jk->...k/dot_general | solution.py:62
  92.8 16.3 %fusion.30.clone.4 = f32[1024,1024,1,1]{1,0,3,2:T(8,128)} fusion(), kind=kLoop, calls=%fused_computation.47.clone.clone.clone.1 | loop fusion | flops 14680064 | bytes 4194304 | tf_op jit(solution)/shard_map/add | solution.py:50
  109.1 16.5 %fusion.171 = f32[1024,1024,1,1]{1,0,3,2:T(8,128)} fusion(), kind=kLoop, calls=%fused_computation.50.clone.clone.clone.1 | loop fusion | flops 15728640 | bytes 4194304 | tf_op jit(solution)/shard_map/...j,jk->...k/dot_general | solution.py:65
  125.6 16.9 %fusion.169 = f32[1024,1024,1,1]{1,0,3,2:T(8,128)} fusion(), kind=kLoop, calls=%fused_computation.49.clone.clone.clone.1 | loop fusion | flops 15728640 | bytes 4194304 | tf_op jit(solution)/shard_map/...j,jk->...k/dot_general | solution.py:62
  142.5 0.0 all-to-all-done
  142.5 4.9 copy.22
  147.5 3.5 fusion.81
  150.9 0.0 copy-start.12
  150.9 8.8 %multiply_subtract_fusion.1 = (f32[8,16,16,1024]{3,0,2,1:T(8,128)}, f32[8,16,16,1024]{3,0,2,1:T(8,128)}) fusion(f32[8,16,16,1024]{3,0,2,1:T(8,128)S(1)} %fusion.81, f32[8,1024]{1,0:T(8,128)S(1)} %get-tuple-element.17, f32[8,1024]{1,0:T(8,128)S(1)} %get-tuple-element.18, bf16[16,16,1024,8]{2,3,1,0:T(8,128)(2,1)S(1)} %bitcast.104), kind=kOutput, calls=%fused_computation.23 | convolution fusion | flops 213910464 | bytes 29425664 | tf_op jit(solution)/shard_map/kp,bpn->kbn/dot_general | solution.py:98
  159.7 0.0 copy-done.12
  159.7 0.0 slice-start.1
  159.7 37.0 %fusion.21 = f32[8,16,16,1024]{3,2,1,0:T(8,128)} fusion(f32[8,16,16,1024]{3,0,2,1:T(8,128)} %get-tuple-element.8, f32[1024,1024,1,1]{1,0,3,2:T(8,128)S(1)} %copy-done.12), kind=kOutput, calls=%fused_computation.34 | convolution fusion | flops 25769803776 | bytes 20971520 | tf_op jit(solution)/shard_map/...j,jk->...k/dot_general | solution.py:65
  196.7 0.0 copy-done.6
  196.7 0.0 copy-done.11
  196.7 0.0 copy-start.13
  196.7 40.4 %fusion.23 = f32[8,16,16,1024]{3,2,1,0:T(8,128)} fusion(f32[8,16,16,1024]{3,0,2,1:T(8,128)S(1)} %copy-done.6, f32[1024,1024,1,1]{1,0,3,2:T(8,128)S(1)} %copy-done.11), kind=kOutput, calls=%fused_computation.36 | convolution fusion | flops 25769803776 | bytes 20971520 | tf_op jit(solution)/shard_map/...j,jk->...k/dot_general | solution.py:62
  237.1 0.0 slice-done.1
  237.1 0.0 slice-done.2
  237.1 0.0 copy-done.13
  237.2 0.0 copy-start.10
  237.2 35.8 %subtract_multiply_fusion = f32[8,16,16,1024]{3,2,1,0:T(8,128)} fusion(f32[8,16,16,1024]{3,2,1,0:T(8,128)} %fusion.23, f32[8,1024]{1,0:T(8,128)S(1)} %get-tuple-element.15, f32[8,16,16,1024]{3,0,2,1:T(8,128)S(1)} %bitcast.107, f32[1024,1024,1,1]{1,0,3,2:T(8,128)S(1)} %copy-done.13), kind=kOutput, calls=%fused_computation.20 | convolution fusion | flops 25773998080 | bytes 29392896 | tf_op jit(solution)/shard_map/...j,jk->...k/dot_general | solution.py:62
  273.0 0.0 copy-done.10
  273.0 35.8 %fusion.11 = f32[8,16,16,1024]{3,0,2,1:T(8,128)} fusion(f32[8,16,16,1024]{3,2,1,0:T(8,128)} %subtract_multiply_fusion, f32[1024,1024,1,1]{1,0,3,2:T(8,128)S(1)} %copy-done.10), kind=kOutput, calls=%fused_computation.24 | convolution fusion | flops 25769803776 | bytes 20971520 | tf_op jit(solution)/shard_map/...j,jk->...k/dot_general | solution.py:65
  308.8 0.0 copy-done.9
  308.8 0.0 copy-done.15
  308.8 40.1 %fusion.13 = f32[8,16,16,1024]{3,0,2,1:T(8,128)} fusion(f32[8,16,16,1024]{3,2,1,0:T(8,128)S(1)} %copy-done.15, f32[1024,1024,1,1]{1,0,3,2:T(8,128)S(1)} %copy-done.9), kind=kOutput, calls=%fused_computation.26 | convolution fusion | flops 25769803776 | bytes 20971520 | tf_op jit(solution)/shard_map/...j,jk->...k/dot_general | solution.py:62
  348.9 0.0 copy-done.8
  348.9 33.1 %add_multiply_fusion = f32[8,16,16,1024]{3,2,1,0:T(8,128)S(1)} fusion(f32[8,16,16,1024]{3,2,1,0:T(8,128)} %fusion.21, f32[8,1024]{1,0:T(8,128)S(1)} %get-tuple-element.16, f32[8,16,16,1024]{3,0,2,1:T(8,128)S(1)} %copy-done.6, f32[1024,1024,1,1]{1,0,3,2:T(8,128)S(1)} %copy-done.8), kind=kOutput, calls=%fused_computation.21 | convolution fusion | flops 25773998080 | bytes 29392896 | tf_op jit(solution)/shard_map/...j,jk->...k/dot_general | solution.py:65
  382.0 0.0 copy-start.4
  382.0 3.2 copy-done.4
  385.2 0.0 copy-done.7
  385.2 40.3 %fusion.17 = f32[8,16,16,1024]{3,0,2,1:T(8,128)} fusion(f32[8,16,16,1024]{3,2,1,0:T(8,128)S(1)} %add_multiply_fusion, f32[1024,1024,1,1]{1,0,3,2:T(8,128)S(1)} %copy-done.7), kind=kOutput, calls=%fused_computation.30 | convolution fusion | flops 25769803776 | bytes 20971520 | tf_op jit(solution)/shard_map/...j,jk->...k/dot_general | solution.py:62
  425.5 0.0 copy-done.5
  425.5 37.3 %multiply_add_fusion = (f32[8,16,16,1024]{3,0,2,1:T(8,128)S(1)}, f32[8,16,16,1024]{3,0,2,1:T(8,128)S(1)}) fusion(f32[8,1024]{1,0:T(8,128)} %fusion.73, f32[8,1024]{1,0:T(8,128)S(1)} %get-tuple-element.18, f32[8,16,16,1024]{3,0,2,1:T(8,128)} %fusion.11, f32[8,16,16,1024]{3,0,2,1:T(8,128)} %fusion.17, f32[8,16,16,1024]{3,0,2,1:T(8,128)} %fusion.13, ...), kind=kOutput, calls=%fused_computation.18 | convolution fusion | flops 25786580992 | bytes 54591488 | tf_op jit(solution)/shard_map/...j,jk->...k/dot_general | solution.py:65
  462.9 10.0 %fusion.84 = f32[8,16,16384]{2,0,1:T(8,128)} fusion(f32[8,16,16384]{2,0,1:T(8,128)S(1)} %bitcast.101), kind=kOutput, calls=%fused_computation.98 | convolution fusion | flops 201327488 | bytes 16777216 | tf_op jit(solution)/shard_map/pk,kbn->pbn/dot_general | solution.py:106
  472.9 11.2 %fusion = f32[8,16,16384]{2,0,1:T(8,128)S(1)} fusion(f32[8,16,16384]{2,0,1:T(8,128)} %fusion.84, f32[8,16,16384]{2,0,1:T(8,128)S(1)} %bitcast.100), kind=kOutput, calls=%fused_computation.1 | convolution fusion | flops 205521792 | bytes 25165824 | tf_op jit(solution)/shard_map/pk,kbn->pbn/dot_general | solution.py:106
  484.1 8.2 %copy.31 = f32[8,4,4,16,1024]{4,3,2,1,0:T(8,128)} copy(f32[8,4,4,16,1024]{4,0,3,2,1:T(8,128)S(1)} %bitcast.105) | data formatting | bytes 16777216 | tf_op jit(solution)/shard_map/div | solution.py:109
  492.3 5.1 all-to-all-start.1
  497.4 1.1 fusion.148
  498.5 3.1 collective-permute-start
  501.6 1.3 collective-permute-start.1
  502.9 3.2 convert_element_type.76
  506.2 0.0 copy-start.2
  506.2 0.0 copy-start.1
  506.2 2.4 slice_bitcast_fusion
  508.5 3.2 copy-done.2
  511.7 0.0 collective-permute-done
  511.7 0.0 collective-permute-done.1
  511.7 4.2 maximum_convert_fusion
  516.0 161.7 %all-to-all-done.1 = f32[8,4,4,16,1024]{4,3,2,1,0:T(8,128)} async-done(((f32[8,4,4,16,1024]{4,3,2,1,0:T(8,128)}), f32[8,4,4,16,1024]{4,3,2,1,0:T(8,128)}, u32[]{:S(2)}, u32[]{:S(2)}) %all-to-all-start.1) | async-done | bytes 8388640 | tf_op jit(solution)/shard_map/all_to_all | solution.py:116
  677.7 8.5 %copy.32 = f32[8,4,4,16,1024]{4,3,0,2,1:T(8,128)} copy(f32[8,4,4,16,1024]{4,3,2,1,0:T(8,128)} %all-to-all-done.1) | data formatting | bytes 16777216 | tf_op jit(solution)/shard_map/all_to_all | solution.py:116
  686.2 11.6 %fusion.5 = f32[4,4,128,1024]{3,2,1,0:T(8,128)} fusion(f32[4,4,136,1024]{3,2,1,0:T(8,128)S(1)} %copy-done, f32[8,4,4,16,1024]{4,3,0,2,1:T(8,128)} %copy.32, f32[4,128,1024]{2,1,0:T(8,128)} %get-tuple-element.12, f32[4,128,1024]{2,1,0:T(8,128)} %get-tuple-element.11), kind=kLoop, calls=%fused_computation.7 | loop fusion | flops 31457280 | bytes 88080384 | tf_op jit(solution)/shard_map/neg | solution.py:43
  697.8 3.4 copy-done.3
  701.2 3.3 slice_add_fusion
  704.5 0.1 slice-done
  704.6 3.7 pad_maximum_fusion
  (18 shorter events, 0.0 us)
Async XLA Ops:
  5.0 137.5 %all-to-all-start = ((bf16[4,4,8,16,1024]{4,3,1,0,2:T(8,128)(2,1)}), bf16[4,4,8,16,1024]{4,3,1,0,2:T(8,128)(2,1)}, u32[]{:S(2)}, u32[]{:S(2)}) async-start(bf16[4,4,8,16,1024]{4,3,1,0,2:T(8,128)(2,1)} %copy.21), calls=%async_computation | async-start | bytes 8388608 | tf_op jit(solution)/shard_map/all_to_all | solution.py:114
  150.9 8.8 %copy-start.12 = (f32[1024,1024,1,1]{1,0,3,2:T(8,128)S(1)}, f32[1024,1024,1,1]{1,0,3,2:T(8,128)}, u32[]{:S(2)}) copy-start(f32[1024,1024,1,1]{1,0,3,2:T(8,128)} %fusion.179) | copy-start | bytes 12582916
  159.7 37.0 %copy-start.6 = (f32[8,16,16,1024]{3,0,2,1:T(8,128)S(1)}, f32[8,16,16,1024]{3,0,2,1:T(8,128)}, u32[]{:S(2)}) copy-start(f32[8,16,16,1024]{3,0,2,1:T(8,128)} %get-tuple-element.7) | copy-start | bytes 25165828
  159.7 37.0 %copy-start.11 = (f32[1024,1024,1,1]{1,0,3,2:T(8,128)S(1)}, f32[1024,1024,1,1]{1,0,3,2:T(8,128)}, u32[]{:S(2)}) copy-start(f32[1024,1024,1,1]{1,0,3,2:T(8,128)} %fusion.181) | copy-start | bytes 12582916
  159.7 77.4 %slice-start.1 = ((s8[8388608]{0:T(1024)(128)(4,1)}), s8[4194304]{0:T(1024)(128)(4,1)S(1)}, s32[]{:S(2)}) async-start(s8[8388608]{0:T(1024)(128)(4,1)} %bitcast.106), calls=%async_computation.3 | async-start | bytes 8388608
  196.7 40.4 %slice-start.2 = ((s8[8388608]{0:T(1024)(128)(4,1)}), s8[4194304]{0:T(1024)(128)(4,1)S(1)}, s32[]{:S(2)}) async-start(s8[8388608]{0:T(1024)(128)(4,1)} %bitcast.106), calls=%async_computation.4 | async-start | bytes 8388608
  196.7 40.4 %copy-start.13 = (f32[1024,1024,1,1]{1,0,3,2:T(8,128)S(1)}, f32[1024,1024,1,1]{1,0,3,2:T(8,128)}, u32[]{:S(2)}) copy-start(f32[1024,1024,1,1]{1,0,3,2:T(8,128)} %fusion.169) | copy-start | bytes 12582916
  237.2 35.8 %copy-start.10 = (f32[1024,1024,1,1]{1,0,3,2:T(8,128)S(1)}, f32[1024,1024,1,1]{1,0,3,2:T(8,128)}, u32[]{:S(2)}) copy-start(f32[1024,1024,1,1]{1,0,3,2:T(8,128)} %fusion.173) | copy-start | bytes 12582916
  273.0 35.8 %copy-start.9 = (f32[1024,1024,1,1]{1,0,3,2:T(8,128)S(1)}, f32[1024,1024,1,1]{1,0,3,2:T(8,128)}, u32[]{:S(2)}) copy-start(f32[1024,1024,1,1]{1,0,3,2:T(8,128)} %fusion.175) | copy-start | bytes 12582916
  273.0 35.8 %copy-start.15 = (f32[8,16,16,1024]{3,2,1,0:T(8,128)S(1)}, f32[8,16,16,1024]{3,2,1,0:T(8,128)}, u32[]{:S(2)}) copy-start(f32[8,16,16,1024]{3,2,1,0:T(8,128)} %subtract_multiply_fusion) | copy-start | bytes 25165828
  308.8 40.1 %copy-start.8 = (f32[1024,1024,1,1]{1,0,3,2:T(8,128)S(1)}, f32[1024,1024,1,1]{1,0,3,2:T(8,128)}, u32[]{:S(2)}) copy-start(f32[1024,1024,1,1]{1,0,3,2:T(8,128)} %fusion.171) | copy-start | bytes 12582916
  348.9 36.3 %copy-start.7 = (f32[1024,1024,1,1]{1,0,3,2:T(8,128)S(1)}, f32[1024,1024,1,1]{1,0,3,2:T(8,128)}, u32[]{:S(2)}) copy-start(f32[1024,1024,1,1]{1,0,3,2:T(8,128)} %fusion.177) | copy-start | bytes 12582916
  382.0 3.3 copy-start.4
  385.2 40.3 %copy-start.5 = (f32[1024,1024,1,1]{1,0,3,2:T(8,128)S(1)}, f32[1024,1024,1,1]{1,0,3,2:T(8,128)}, u32[]{:S(2)}) copy-start(f32[1024,1024,1,1]{1,0,3,2:T(8,128)} %fusion.30.clone.4) | copy-start | bytes 12582916
  492.3 185.4 %all-to-all-start.1 = ((f32[8,4,4,16,1024]{4,3,2,1,0:T(8,128)}), f32[8,4,4,16,1024]{4,3,2,1,0:T(8,128)}, u32[]{:S(2)}, u32[]{:S(2)}) async-start(f32[8,4,4,16,1024]{4,3,2,1,0:T(8,128)} %copy.31), calls=%async_computation.1 | async-start | bytes 16777216 | tf_op jit(solution)/shard_map/all_to_all | solution.py:116
  498.5 13.2 %collective-permute-start = (bf16[4,4,4,1024]{3,2,1,0:T(4,128)(2,1)S(1)}, bf16[4,4,4,1024]{3,2,1,0:T(4,128)(2,1)S(1)}, u32[]{:S(2)}, u32[]{:S(2)}) collective-permute-start(bf16[4,4,4,1024]{3,2,1,0:T(4,128)(2,1)S(1)} %get-tuple-element.13), channel_id=1, source_target_pairs={{0,1},{1,2},{2,3},{4,5},{5,6},{6,7},{8,9},{9,10},{10,11},{12,13},{... | collective-permute-start | bytes 393224 | tf_op jit(solution)/shard_map/ppermute | solution.py:21
  501.6 10.1 %collective-permute-start.1 = (bf16[4,4,4,1024]{3,2,1,0:T(4,128)(2,1)S(1)}, bf16[4,4,4,1024]{3,2,1,0:T(4,128)(2,1)S(1)}, u32[]{:S(2)}, u32[]{:S(2)}) collective-permute-start(bf16[4,4,4,1024]{3,2,1,0:T(4,128)(2,1)S(1)} %get-tuple-element.14), channel_id=1, source_target_pairs={{1,0},{2,1},{3,2},{5,4},{6,5},{7,6},{9,8},{10,9},{11,10},{13,12},{... | collective-permute-start | bytes 393224 | tf_op jit(solution)/shard_map/ppermute | solution.py:24
  506.2 5.6 copy-start.2
  506.2 5.6 copy-start.1
  677.7 8.5 %copy-start = (f32[4,4,136,1024]{3,2,1,0:T(8,128)S(1)}, f32[4,4,136,1024]{3,2,1,0:T(8,128)}, u32[]{:S(2)}) copy-start(f32[4,4,136,1024]{3,2,1,0:T(8,128)} %maximum_convert_fusion) | copy-start | bytes 26738692
  686.2 11.6 %copy-start.14 = (f32[128]{0:T(128)S(1)}, f32[128]{0:T(128)}, u32[]{:S(2)}) copy-start(f32[128]{0:T(128)} %param.3) | copy-start | bytes 1540
  697.8 3.4 copy-start.3
  701.2 3.4 slice-start
where the time goes:
time: 720 us; the launch traced here: 709 us
  matrix products  333 us (46%)
  waiting for transfers between devices  162 us (22%)
  other arithmetic  158 us (22%)
  local copies, waits for them, and re-layouts  40.2 us (6%)
  starting transfers between devices  15.1 us (2%)
    all_to_all x1, waiting for transfers between devices, by_whole(): return lax.all_to_all(result, 'gx', split_axis=0, concat_axis=0, tiled=True)  162 us
    dot_general x2, matrix products, complex_apply(): jnp.einsum(form, real_part, cos_tab, precision=HIGH)  80.7 us
    dot_general x2, matrix products, complex_apply(): jnp.einsum(form, imag_part, sin_tab, precision=HIGH)  75.9 us
    dot_general x2, matrix products, complex_apply(): jnp.einsum(form, imag_part, cos_tab, precision=HIGH)  72.8 us
    dot_general x2, matrix products, complex_apply(): jnp.einsum(form, real_part, sin_tab, precision=HIGH)  70.4 us
    dot_general x2, other arithmetic, complex_apply(): jnp.einsum(form, imag_part, sin_tab, precision=HIGH)  33.3 us
    dot_general x2, other arithmetic, complex_apply(): jnp.einsum(form, imag_part, cos_tab, precision=HIGH)  32.4 us
    dot_general x2, other arithmetic, complex_apply(): jnp.einsum(form, real_part, cos_tab, precision=HIGH)  32.4 us
  transfers between devices with their start and end apart: 4, of which 1 were waited for; matrix products, arithmetic and copies ran while one was open for 20% of the time, Pallas kernels for 0%

commit v1 on v0

v1 whole, which is shorter than its diff:
```python
import functools
import math

import jax
import jax.numpy as jnp
import numpy as np
from jax import lax
from jax.experimental import pallas as pl
from jax.experimental.pallas import tpu as pltpu
from jax.sharding import PartitionSpec as P

STENCIL = (4.0 / 5.0, -1.0 / 5.0, 4.0 / 105.0, -1.0 / 280.0)
BAND = 256
CHUNKS = 2
F32 = jnp.float32
BF16 = jnp.bfloat16


def kernel_row(length):
    index = np.arange(length)
    signed = np.where(index < length // 2, index, index - length).astype(np.float64)
    angle = np.pi * np.where(signed == 0, 1.0, signed) / length
    row = np.where(index % 2 == 0, 1.0, -1.0) * (np.pi / length) / np.tan(angle)
    row = np.where((index == 0) | (index == length // 2), 0.0, row)
    return jnp.asarray(row.astype(np.float32))[None, :]


def strip_body(pad, row_ref, high_ref, low_ref, run_ref):
    rows, length = run_ref.shape

    @pl.when(pl.program_id(0) == 0)
    def _():
        wide = jnp.broadcast_to(row_ref[...], (rows, length))
        run_ref[...] = pltpu.roll(wide, pad, 1, stride=1, stride_axis=0)

    @pl.when(pl.program_id(0) > 0)
    def _():
        run_ref[...] = pltpu.roll(run_ref[...], rows, 1)

    run = run_ref[...]
    high = run.astype(BF16)
    low = (run - high.astype(F32)).astype(BF16)
    high_ref[:, :length] = high
    low_ref[:, :length] = low
    if pad:
        high_ref[:, length:] = high[:, :pad]
        low_ref[:, length:] = low[:, :pad]


def strips(length, width):
    pad = width - BAND
    rows = 16
    shape = jax.ShapeDtypeStruct((BAND, length + pad), BF16)
    spec = pl.BlockSpec((rows, length + pad), lambda i: (i, 0))
    return pl.pallas_call(
        functools.partial(strip_body, pad),
        grid=(BAND // rows,),
        in_specs=[pl.BlockSpec((1, length), lambda i: (0, 0))],
        out_specs=[spec, spec],
        out_shape=[shape, shape],
        scratch_shapes=[pltpu.VMEM((rows, length), F32)],
        cost_estimate=pl.CostEstimate(
            flops=4 * BAND * length, bytes_accessed=4 * BAND * length, transcendentals=0
        ),
    )(kernel_row(length))


def panel(strip_ref, first, width, columns):
    runs = [
        strip_ref[:, pl.ds(pl.multiple_of(first + width - BAND - BAND * i, BAND), columns)]
        for i in range(width // BAND)
    ]
    return runs[0] if len(runs) == 1 else jnp.concatenate(runs, axis=0)


def dot(left, right):
    return jnp.dot(left, right, preferred_element_type=F32)


def far_body(devices, lines_ref, high_ref, low_ref, out_ref):
    total_rows, width = lines_ref.shape
    rows = total_rows // devices
    columns = out_ref.shape[1]
    column = pl.program_id(0) * columns
    total = None
    for step in range(1, devices):
        cut = (devices - step) * rows
        moved = jnp.concatenate([lines_ref[cut:, :], lines_ref[:cut, :]], axis=0)
        first = step * width + column
        for strip_ref in (high_ref, low_ref):
            part = dot(moved, panel(strip_ref, first, width, columns))
            total = part if total is None else total + part
    out_ref[...] = total.astype(BF16)


def far_slopes(lines, high, low):
    devices, rows, width = lines.shape
    total_rows = devices * rows
    columns = BAND
    out = pl.pallas_call(
        functools.partial(far_body, devices),
        grid=(width // columns,),
        in_specs=[
            pl.BlockSpec((total_rows, width), lambda j: (0, 0)),
            pl.BlockSpec(high.shape, lambda j: (0, 0)),
            pl.BlockSpec(low.shape, lambda j: (0, 0)),
        ],
        out_specs=pl.BlockSpec((total_rows, columns), lambda j: (0, j)),
        out_shape=jax.ShapeDtypeStruct((total_rows, width), BF16),
        compiler_params=pltpu.CompilerParams(vmem_limit_bytes=48 * 2**20),
        cost_estimate=pl.CostEstimate(
            flops=4 * total_rows * (devices - 1) * width * width,
            bytes_accessed=4 * total_rows * width + 4 * high.size,
            transcendentals=0,
        ),
    )(lines.reshape(total_rows, width), high, low)
    return out.reshape(devices, rows, width)


def local_body(field_ref, u_ref, w_ref, b_ref, below_ref, above_ref, strat_ref, high_ref, low_ref, out_ref, pad_ref):
    comp = pl.program_id(1)
    levels, width = out_ref.shape
    pad_ref[8 : 8 + levels, :] = field_ref[...].astype(F32)
    pad_ref[4:8, :] = below_ref[...].astype(F32)
    pad_ref[8 + levels : 12 + levels, :] = above_ref[...].astype(F32)
    is_w = (comp == 2).astype(F32)
    is_b = (comp == 3).astype(F32)
    strat = strat_ref[...] * is_b
    columns = BAND
    for j in range(width // columns):
        here = slice(j * columns, (j + 1) * columns)
        near = dot(field_ref[...], panel(high_ref, j * columns, width, columns)) + dot(
            field_ref[...], panel(low_ref, j * columns, width, columns)
        )
        slope_z = None
        for offset in range(1, 5):
            term = STENCIL[offset - 1] * (
                pad_ref[8 + offset : 8 + offset + levels, here]
                - pad_ref[8 - offset : 8 - offset + levels, here]
            )
            slope_z = term if slope_z is None else slope_z + term
        speed_w = w_ref[:, here].astype(F32)
        out_ref[:, here] = (
            is_w * b_ref[:, here].astype(F32)
            - strat * speed_w
            - (u_ref[:, here].astype(F32) * near + speed_w * slope_z)
        )


def local_part(fields, below, above, strat_col, high, low):
    comps, lines, levels, width = fields.shape

    def block(comp):
        return pl.BlockSpec(
            (None, None, levels, width),
            (lambda l, c: (c, l, 0, 0)) if comp is None else (lambda l, c: (comp, l, 0, 0)),
        )

    halo = pl.BlockSpec((None, None, 4, width), lambda l, c: (c, l, 0, 0))
    whole = pl.BlockSpec(high.shape, lambda l, c: (0, 0))
    return pl.pallas_call(
        local_body,
        grid=(lines, comps),
        in_specs=[
            block(None),
            block(0),
            block(2),
            block(3),
            halo,
            halo,
            pl.BlockSpec((levels, 1), lambda l, c: (0, 0)),
            whole,
            whole,
        ],
        out_specs=block(None),
        out_shape=jax.ShapeDtypeStruct(fields.shape, F32),
        scratch_shapes=[pltpu.VMEM((levels + 16, width), F32)],
        compiler_params=pltpu.CompilerParams(vmem_limit_bytes=56 * 2**20),
        cost_estimate=pl.CostEstimate(
            flops=4 * fields.size * width, bytes_accessed=8 * fields.size, transcendentals=0
        ),
    )(fields, fields, fields, fields, below, above, strat_col, high, low)


def update_body(part_ref, u_ref, far_ref, out_ref):
    out_ref[...] = part_ref[...] - u_ref[...].astype(F32) * far_ref[...].astype(F32)


def update(part, fields, far, comp):
    comps, lines, levels, width = fields.shape
    spec = pl.BlockSpec((None, None, levels, width), lambda l, c: (comp + c, l, 0, 0))
    return pl.pallas_call(
        update_body,
        grid=(lines, far.shape[0]),
        in_specs=[
            spec,
            pl.BlockSpec((None, None, levels, width), lambda l, c: (0, l, 0, 0)),
            pl.BlockSpec((None, None, levels, width), lambda l, c: (c, l, 0, 0)),
        ],
        out_specs=spec,
        out_shape=jax.ShapeDtypeStruct(part.shape, F32),
        input_output_aliases={0: 0},
        cost_estimate=pl.CostEstimate(
            flops=2 * far.size, bytes_accessed=12 * far.size, transcendentals=0
        ),
    )(part, fields, far)


def halos(fields):
    count = lax.axis_size("gz")
    forward = [(i, i + 1) for i in range(count - 1)]
    backward = [(target, source) for source, target in forward]
    levels = fields.shape[2]
    below = lax.ppermute(fields[:, :, levels - 4 :], "gz", forward)
    above = lax.ppermute(fields[:, :, :4], "gz", backward)
    return below, above


def body(fields, strat_sq):
    comps, lines, levels, width = fields.shape
    devices = lax.axis_size("gx")
    group = comps // CHUNKS
    shape = (devices, group * lines * levels // devices, width)
    gathered = [
        lax.all_to_all(
            fields[c : c + group].reshape(shape), "gx", split_axis=0, concat_axis=0, tiled=True
        )
        for c in range(0, comps, group)
    ]
    below, above = halos(fields)
    high, low = strips(devices * width, width)
    part = local_part(fields, below, above, strat_sq[:, None], high, low)
    for i in range(CHUNKS):
        far = far_slopes(gathered[i], high, low)
        back = lax.all_to_all(far, "gx", split_axis=0, concat_axis=0, tiled=True)
        part = update(part, fields, back.reshape(group, lines, levels, width), i * group)
    return part


def solution(mesh):
    placed = (P(None, None, "gz", "gx"), P("gz"))
    return jax.shard_map(
        body, mesh=mesh, in_specs=placed, out_specs=P(None, None, "gz", "gx"), check_vma=False
    )
```

time: 720 us -> 228 us (0.32)
  the two profiles are of different devices: /device:TPU:9 before, /device:TPU:0 now
where the time goes in v1:
time: 228 us; the launch traced here: 227 us
  Pallas kernels  122 us (54%)
  blocking collectives  55.3 us (24%)
  waiting for transfers between devices  21.6 us (9%)
  starting transfers between devices  17.5 us (8%)
  local copies, waits for them, and re-layouts  10.8 us (5%)
    pallas_call x2, Pallas kernels, far_slopes(): pl.pallas_call(functools.partial(far_body, devices), grid=(width // colum...  70.5 us
    all_to_all x1, blocking collectives, body(): lax.all_to_all(fields[c:c + group].reshape(shape), 'gx', split_axis=0, co...  55.3 us
    pallas_call x1, Pallas kernels, local_part(): pl.pallas_call(local_body, grid=(lines, comps), in_specs=[block(None), bl...  26.2 us
    all_to_all x2, waiting for transfers between devices, body(): back = lax.all_to_all(far, 'gx', split_axis=0, concat_axis=0, tiled=True)  18 us
    pallas_call x2, Pallas kernels, update(): pl.pallas_call(update_body, grid=(lines, far.shape[0]), in_specs=[spec, p...  15 us
    pallas_call x1, Pallas kernels, strips(): pl.pallas_call(functools.partial(strip_body, pad), grid=(BAND // rows,),...  9.89 us
    all_to_all x2, starting transfers between devices, body(): back = lax.all_to_all(far, 'gx', split_axis=0, concat_axis=0, tiled=True)  8.09 us
    unnamed x12, local copies, waits for them, and re-layouts  4.88 us
  transfers between devices with their start and end apart: 5, of which 5 were waited for; matrix products, arithmetic and copies ran while one was open for 1% of the time, Pallas kernels for 50%

profile of v1, /device:TPU:0, one launch (start us, length us, event | category | flops | bytes accessed | tf_op | source)
XLA Modules:
  0.0 226.9 jit_solution(321254244724725306)
XLA Ops:
  0.0 4.0 %fusion = (bf16[2,4,128,1024]{3,2,1,0:T(8,128)(2,1)}, bf16[2,4,128,1024]{3,2,1,0:T(8,128)(2,1)S(1)}) fusion(bf16[4,4,128,1024]{3,2,1,0:T(8,128)(2,1)} %u_ref.5), kind=kLoop, calls=%fused_computation | loop fusion | bytes 8388608 | tf_op jit(solution)/shard_map/slice | solution.py:226
  4.0 55.3 %all_to_all.20 = bf16[8,128,1024]{2,1,0:T(8,128)(2,1)} all-to-all(bf16[8,128,1024]{2,1,0:T(8,128)(2,1)S(1)} %bitcast.13), channel_id=1, replica_groups=mesh['gx'=8,'gz'=4] {'gx'}, dimensions={0} | all-to-all | bytes 4194304 | tf_op jit(solution)/shard_map/all_to_all | solution.py:225
  59.3 3.6 %all-to-all-start.2 = ((bf16[8,128,1024]{2,1,0:T(8,128)(2,1)}), bf16[8,128,1024]{2,1,0:T(8,128)(2,1)S(1)}, u32[]{:S(2)}, u32[]{:S(2)}) async-start(bf16[8,128,1024]{2,1,0:T(8,128)(2,1)} %bitcast.12), calls=%async_computation.2 | async-start | bytes 4194304 | tf_op jit(solution)/shard_map/all_to_all | solution.py:225
  62.9 9.9 %shard_map.37 = (bf16[256,8960]{1,0:T(8,128)(2,1)}, bf16[256,8960]{1,0:T(8,128)(2,1)}) custom-call(f32[1,8192]{1,0:T(1,128)} %constant.3.row_ref), custom_call_target="tpu_custom_call" | custom-call | flops 8388608 | bytes 8388608 | tf_op jit(solution)/shard_map/pallas_call | solution.py:55
  72.8 0.0 copy-start
  72.8 1.6 copy-done
  74.4 34.9 %shard_map.39 = bf16[1024,1024]{1,0:T(8,128)(2,1)S(1)} custom-call(bf16[1024,1024]{1,0:T(8,128)(2,1)S(1)} %bitcast.10, bf16[256,8960]{1,0:T(8,128)(2,1)} %get-tuple-element.7.high_ref, bf16[256,8960]{1,0:T(8,128)(2,1)} %get-tuple-element.8.low_ref), custom_call_target="tpu_custom_call" | custom-call | flops 30064771072 | bytes 13369344 | tf_op jit(solution)/shard_map/pallas_call | solution.py:100
  109.3 0.0 copy-start.1
  109.3 1.3 copy-done.1
  110.6 1.3 all-to-all-done.2
  111.9 4.4 %all-to-all-start.1 = ((bf16[8,128,1024]{2,1,0:T(8,128)(2,1)}), bf16[8,128,1024]{2,1,0:T(8,128)(2,1)}, u32[]{:S(2)}, u32[]{:S(2)}) async-start(bf16[8,128,1024]{2,1,0:T(8,128)(2,1)} %bitcast.11), calls=%async_computation.1 | async-start | bytes 4194304 | tf_op jit(solution)/shard_map/all_to_all | solution.py:235
  116.3 35.6 %shard_map.41 = bf16[1024,1024]{1,0:T(8,128)(2,1)} custom-call(bf16[1024,1024]{1,0:T(8,128)(2,1)S(1)} %bitcast.9, bf16[256,8960]{1,0:T(8,128)(2,1)} %get-tuple-element.7.high_ref, bf16[256,8960]{1,0:T(8,128)(2,1)} %get-tuple-element.8.low_ref), custom_call_target="tpu_custom_call" | custom-call | flops 30064771072 | bytes 13369344 | tf_op jit(solution)/shard_map/pallas_call | solution.py:100
  151.8 13.5 %all-to-all-done.1 = bf16[8,128,1024]{2,1,0:T(8,128)(2,1)} async-done(((bf16[8,128,1024]{2,1,0:T(8,128)(2,1)}), bf16[8,128,1024]{2,1,0:T(8,128)(2,1)}, u32[]{:S(2)}, u32[]{:S(2)}) %all-to-all-start.1) | async-done | bytes 2097184 | tf_op jit(solution)/shard_map/all_to_all | solution.py:235
  165.3 0.0 copy-start.5
  165.3 3.7 %all-to-all-start.3 = ((bf16[8,128,1024]{2,1,0:T(8,128)(2,1)}), bf16[8,128,1024]{2,1,0:T(8,128)(2,1)S(1)}, u32[]{:S(2)}, u32[]{:S(2)}) async-start(bf16[8,128,1024]{2,1,0:T(8,128)(2,1)} %bitcast.7), calls=%async_computation.3 | async-start | bytes 4194304 | tf_op jit(solution)/shard_map/all_to_all | solution.py:235
  169.1 1.1 fusion.1
  170.2 1.3 collective-permute-start.1
  171.5 4.6 %collective-permute-start = (bf16[4,4,4,1024]{3,2,1,0:T(4,128)(2,1)S(1)}, bf16[4,4,4,1024]{3,2,1,0:T(4,128)(2,1)S(1)}, u32[]{:S(2)}, u32[]{:S(2)}) collective-permute-start(bf16[4,4,4,1024]{3,2,1,0:T(4,128)(2,1)S(1)} %get-tuple-element.12), channel_id=1, source_target_pairs={{0,1},{1,2},{2,3},{4,5},{5,6},{6,7},{8,9},{9,10},{10,11},{12,13},{... | collective-permute-start | bytes 393224 | tf_op jit(solution)/shard_map/ppermute | solution.py:214
  176.1 0.0 copy-done.5
  176.1 0.7 copy.6.strat_ref
  176.8 1.1 collective-permute-done.1.above_ref
  177.9 0.0 copy-start.3
  177.9 1.2 collective-permute-done.below_ref
  179.1 0.0 copy-done.3
  179.1 0.0 copy-start.4
  179.1 0.7 copy-done.4
  179.8 26.2 %shard_map.38.part_ref = f32[4,4,128,1024]{3,2,1,0:T(8,128)} custom-call(bf16[4,4,128,1024]{3,2,1,0:T(8,128)(2,1)} %u_ref.5, bf16[4,4,128,1024]{3,2,1,0:T(8,128)(2,1)} %u_ref.5, bf16[4,4,128,1024]{3,2,1,0:T(8,128)(2,1)} %u_ref.5, bf16[4,4,128,1024]{3,2,1,0:T(8,128)(2,1)} %u_ref.5, bf16[4,4,4,1024]{3,2,1,0:T(4,128)(2,1)} %copy-done.4, ...), custom_call_target="tpu_custom_call" | custom-call | flops 8589934592 | bytes 16777216 | tf_op jit(solution)/shard_map/pallas_call | solution.py:161
  206.0 7.5 %shard_map.40.part_ref = f32[4,4,128,1024]{3,2,1,0:T(8,128)} custom-call(f32[4,4,128,1024]{3,2,1,0:T(8,128)} %shard_map.38.part_ref, bf16[4,4,128,1024]{3,2,1,0:T(8,128)(2,1)} %u_ref.5, bf16[2,4,128,1024]{3,2,1,0:T(8,128)(2,1)} %bitcast.4.far_ref), custom_call_target="tpu_custom_call", output_to_operand_aliasing={{}: (0, {})} | custom-call | flops 2097152 | bytes 12582912 | tf_op jit(solution)/shard_map/pallas_call | solution.py:192
  213.5 4.6 %all-to-all-done.3 = bf16[8,128,1024]{2,1,0:T(8,128)(2,1)S(1)} async-done(((bf16[8,128,1024]{2,1,0:T(8,128)(2,1)}), bf16[8,128,1024]{2,1,0:T(8,128)(2,1)S(1)}, u32[]{:S(2)}, u32[]{:S(2)}) %all-to-all-start.3) | async-done | bytes 2097184 | tf_op jit(solution)/shard_map/all_to_all | solution.py:235
  218.1 0.0 copy-start.2
  218.1 1.3 copy-done.2
  219.4 7.5 %shard_map.42 = f32[4,4,128,1024]{3,2,1,0:T(8,128)} custom-call(f32[4,4,128,1024]{3,2,1,0:T(8,128)} %shard_map.40.part_ref, bf16[4,4,128,1024]{3,2,1,0:T(8,128)(2,1)} %u_ref.5, bf16[2,4,128,1024]{3,2,1,0:T(8,128)(2,1)} %bitcast.14), custom_call_target="tpu_custom_call", output_to_operand_aliasing={{}: (0, {})} | custom-call | flops 2097152 | bytes 12582912 | tf_op jit(solution)/shard_map/pallas_call | solution.py:192
Async XLA Ops:
  59.3 52.6 %all-to-all-start.2 = ((bf16[8,128,1024]{2,1,0:T(8,128)(2,1)}), bf16[8,128,1024]{2,1,0:T(8,128)(2,1)S(1)}, u32[]{:S(2)}, u32[]{:S(2)}) async-start(bf16[8,128,1024]{2,1,0:T(8,128)(2,1)} %bitcast.12), calls=%async_computation.2 | async-start | bytes 4194304 | tf_op jit(solution)/shard_map/all_to_all | solution.py:225
  72.8 1.6 copy-start
  109.3 1.3 copy-start.1
  111.9 53.4 %all-to-all-start.1 = ((bf16[8,128,1024]{2,1,0:T(8,128)(2,1)}), bf16[8,128,1024]{2,1,0:T(8,128)(2,1)}, u32[]{:S(2)}, u32[]{:S(2)}) async-start(bf16[8,128,1024]{2,1,0:T(8,128)(2,1)} %bitcast.11), calls=%async_computation.1 | async-start | bytes 4194304 | tf_op jit(solution)/shard_map/all_to_all | solution.py:235
  165.3 10.8 %copy-start.5 = (f32[128]{0:T(128)S(1)}, f32[128]{0:T(128)}, u32[]{:S(2)}) copy-start(f32[128]{0:T(128)} %param.4) | copy-start | bytes 1540
  165.3 52.7 %all-to-all-start.3 = ((bf16[8,128,1024]{2,1,0:T(8,128)(2,1)}), bf16[8,128,1024]{2,1,0:T(8,128)(2,1)S(1)}, u32[]{:S(2)}, u32[]{:S(2)}) async-start(bf16[8,128,1024]{2,1,0:T(8,128)(2,1)} %bitcast.7), calls=%async_computation.3 | async-start | bytes 4194304 | tf_op jit(solution)/shard_map/all_to_all | solution.py:235
  170.2 7.7 %collective-permute-start.1 = (bf16[4,4,4,1024]{3,2,1,0:T(4,128)(2,1)S(1)}, bf16[4,4,4,1024]{3,2,1,0:T(4,128)(2,1)S(1)}, u32[]{:S(2)}, u32[]{:S(2)}) collective-permute-start(bf16[4,4,4,1024]{3,2,1,0:T(4,128)(2,1)S(1)} %get-tuple-element.11), channel_id=1, source_target_pairs={{1,0},{2,1},{3,2},{5,4},{6,5},{7,6},{9,8},{10,9},{11,10},{13,12},{... | collective-permute-start | bytes 393224 | tf_op jit(solution)/shard_map/ppermute | solution.py:215
  171.5 7.6 %collective-permute-start = (bf16[4,4,4,1024]{3,2,1,0:T(4,128)(2,1)S(1)}, bf16[4,4,4,1024]{3,2,1,0:T(4,128)(2,1)S(1)}, u32[]{:S(2)}, u32[]{:S(2)}) collective-permute-start(bf16[4,4,4,1024]{3,2,1,0:T(4,128)(2,1)S(1)} %get-tuple-element.12), channel_id=1, source_target_pairs={{0,1},{1,2},{2,3},{4,5},{5,6},{6,7},{8,9},{9,10},{10,11},{12,13},{... | collective-permute-start | bytes 393224 | tf_op jit(solution)/shard_map/ppermute | solution.py:214
  177.9 1.2 copy-start.3
  179.1 0.7 copy-start.4
  218.1 1.3 copy-start.2

commit v2 on v1

--- a/solution.py
+++ b/solution.py
@@ -11,7 +11,8 @@
 
 STENCIL = (4.0 / 5.0, -1.0 / 5.0, 4.0 / 105.0, -1.0 / 280.0)
 BAND = 256
-CHUNKS = 2
+UPDATE_CUTS = (4, 6)
+UPDATE_VMEM = 60 * 2**20
 F32 = jnp.float32
 BF16 = jnp.bfloat16
 
@@ -77,11 +78,9 @@
     return jnp.dot(left, right, preferred_element_type=F32)
 
 
-def far_body(devices, lines_ref, high_ref, low_ref, out_ref):
+def far_sum(devices, column, columns, lines_ref, high_ref, low_ref):
     total_rows, width = lines_ref.shape
     rows = total_rows // devices
-    columns = out_ref.shape[1]
-    column = pl.program_id(0) * columns
     total = None
     for step in range(1, devices):
         cut = (devices - step) * rows
@@ -90,31 +89,52 @@
         for strip_ref in (high_ref, low_ref):
             part = dot(moved, panel(strip_ref, first, width, columns))
             total = part if total is None else total + part
-    out_ref[...] = total.astype(BF16)
-
-
-def far_slopes(lines, high, low):
+    return total.astype(BF16)
+
+
+def far_body(devices, me_ref, lines_ref, high_ref, low_ref, out_ref):
+    columns = out_ref.shape[1]
+    out_ref[...] = far_sum(
+        devices, pl.program_id(0) * columns, columns, lines_ref, high_ref, low_ref
+    )
+
+
+def far_blocks_body(devices, me_ref, lines_ref, high_ref, low_ref, *refs):
+    outs, all_ref = refs[:-1], refs[-1]
+    rows, columns = outs[0].shape
+    all_ref[...] = far_sum(
+        devices, pl.program_id(0) * columns, columns, lines_ref, high_ref, low_ref
+    )
+    for k in range(devices):
+        start = pl.multiple_of((me_ref[0] + devices - k) % devices * rows, rows)
+        outs[k][...] = all_ref[pl.ds(start, rows), :]
+
+
+def far_slopes(lines, high, low, me, split):
     devices, rows, width = lines.shape
     total_rows = devices * rows
     columns = BAND
+    whole = pl.BlockSpec((total_rows, width), lambda j, m: (0, 0))
+    strip = pl.BlockSpec(high.shape, lambda j, m: (0, 0), pipeline_mode=pl.Buffered(1))
+    held, count = (rows, devices) if split else (total_rows, 1)
     out = pl.pallas_call(
-        functools.partial(far_body, devices),
-        grid=(width // columns,),
-        in_specs=[
-            pl.BlockSpec((total_rows, width), lambda j: (0, 0)),
-            pl.BlockSpec(high.shape, lambda j: (0, 0)),
-            pl.BlockSpec(low.shape, lambda j: (0, 0)),
-        ],
-        out_specs=pl.BlockSpec((total_rows, columns), lambda j: (0, j)),
-        out_shape=jax.ShapeDtypeStruct((total_rows, width), BF16),
-        compiler_params=pltpu.CompilerParams(vmem_limit_bytes=48 * 2**20),
+        functools.partial(far_blocks_body if split else far_body, devices),
+        grid_spec=pltpu.PrefetchScalarGridSpec(
+            num_scalar_prefetch=1,
+            grid=(width // columns,),
+            in_specs=[whole, strip, strip],
+            out_specs=[pl.BlockSpec((held, columns), lambda j, m: (0, j))] * count,
+            scratch_shapes=[pltpu.VMEM((total_rows, columns), BF16)] if split else [],
+        ),
+        out_shape=[jax.ShapeDtypeStruct((held, width), BF16)] * count,
+        compiler_params=pltpu.CompilerParams(vmem_limit_bytes=28 * 2**20),
         cost_estimate=pl.CostEstimate(
             flops=4 * total_rows * (devices - 1) * width * width,
             bytes_accessed=4 * total_rows * width + 4 * high.size,
             transcendentals=0,
         ),
-    )(lines.reshape(total_rows, width), high, low)
-    return out.reshape(devices, rows, width)
+    )(me, lines.reshape(total_rows, width), high, low)
+    return out if split else out[0].reshape(devices, rows, width)
 
 
 def local_body(field_ref, u_ref, w_ref, b_ref, below_ref, above_ref, strat_ref, high_ref, low_ref, out_ref, pad_ref):
@@ -157,7 +177,7 @@
         )
 
     halo = pl.BlockSpec((None, None, 4, width), lambda l, c: (c, l, 0, 0))
-    whole = pl.BlockSpec(high.shape, lambda l, c: (0, 0))
+    whole = pl.BlockSpec(high.shape, lambda l, c: (0, 0), pipeline_mode=pl.Buffered(1))
     return pl.pallas_call(
         local_body,
         grid=(lines, comps),
@@ -175,7 +195,7 @@
         out_specs=block(None),
         out_shape=jax.ShapeDtypeStruct(fields.shape, F32),
         scratch_shapes=[pltpu.VMEM((levels + 16, width), F32)],
-        compiler_params=pltpu.CompilerParams(vmem_limit_bytes=56 * 2**20),
+        compiler_params=pltpu.CompilerParams(vmem_limit_bytes=28 * 2**20),
         cost_estimate=pl.CostEstimate(
             flops=4 * fields.size * width, bytes_accessed=8 * fields.size, transcendentals=0
         ),
@@ -200,10 +220,61 @@
         out_specs=spec,
         out_shape=jax.ShapeDtypeStruct(part.shape, F32),
         input_output_aliases={0: 0},
+        compiler_params=pltpu.CompilerParams(vmem_limit_bytes=UPDATE_VMEM),
         cost_estimate=pl.CostEstimate(
             flops=2 * far.size, bytes_accessed=12 * far.size, transcendentals=0
         ),
     )(part, fields, far)
+
+
+def update_blocks_body(offsets, me_ref, part_ref, u_ref, *refs):
+    fars, out_ref = refs[:-1], refs[-1]
+    for i, far_ref in enumerate(fars):
+
+        @pl.when(pl.program_id(0) == i)
+        def _(far_ref=far_ref):
+            out_ref[...] = part_ref[...] - u_ref[...].astype(F32) * far_ref[...].astype(F32)
+
+
+def update_blocks(part, fields, base, offsets, fars, me, devices, lines_levels):
+    rows, width = fars[0].shape
+    u_blocks = lines_levels // rows
+
+    def owner(i, m):
+        offset = offsets[-1]
+        for index in range(len(offsets) - 1):
+            offset = jnp.where(i == index, offsets[index], offset)
+        return (m[0] + offset) % devices
+
+    spec = pl.BlockSpec((rows, width), lambda i, m: (base + owner(i, m), 0))
+    return pl.pallas_call(
+        functools.partial(update_blocks_body, offsets),
+        grid_spec=pltpu.PrefetchScalarGridSpec(
+            num_scalar_prefetch=1,
+            grid=(len(offsets),),
+            in_specs=[spec, pl.BlockSpec((rows, width), lambda i, m: (owner(i, m) % u_blocks, 0))]
+            + [pl.BlockSpec((rows, width), lambda i, m: (0, 0))] * len(offsets),
+            out_specs=spec,
+        ),
+        out_shape=jax.ShapeDtypeStruct(part.shape, F32),
+        input_output_aliases={1: 0},
+        compiler_params=pltpu.CompilerParams(vmem_limit_bytes=UPDATE_VMEM),
+        cost_estimate=pl.CostEstimate(
+            flops=2 * len(offsets) * rows * width,
+            bytes_accessed=12 * len(offsets) * rows * width,
+            transcendentals=0,
+        ),
+    )(me, part, fields, *fars)
+
+
+def order_of(devices):
+    return sorted(range(1, devices), key=lambda k: abs(2 * k - devices))
+
+
+def groups_of(devices, cuts):
+    order = [0] + order_of(devices)
+    marks = [0] + [devices * cut // 8 for cut in cuts] + [devices]
+    return [order[a:b] for a, b in zip(marks, marks[1:])]
 
 
 def halos(fields):
@@ -219,22 +290,35 @@
 def body(fields, strat_sq):
     comps, lines, levels, width = fields.shape
     devices = lax.axis_size("gx")
-    group = comps // CHUNKS
+    group = comps // 2
     shape = (devices, group * lines * levels // devices, width)
-    gathered = [
-        lax.all_to_all(
-            fields[c : c + group].reshape(shape), "gx", split_axis=0, concat_axis=0, tiled=True
-        )
-        for c in range(0, comps, group)
-    ]
+    me = lax.axis_index("gx").astype(jnp.int32)[None]
+
+    def exchange(whole):
+        return lax.all_to_all(whole, "gx", split_axis=0, concat_axis=0, tiled=True)
+
+    def ahead(block, k):
+        return lax.ppermute(block, "gx", [(i, (i + k) % devices) for i in range(devices)])
+
+    first = exchange(fields[:group].reshape(shape))
     below, above = halos(fields)
     high, low = strips(devices * width, width)
     part = local_part(fields, below, above, strat_sq[:, None], high, low)
-    for i in range(CHUNKS):
-        far = far_slopes(gathered[i], high, low)
-        back = lax.all_to_all(far, "gx", split_axis=0, concat_axis=0, tiled=True)
-        part = update(part, fields, back.reshape(group, lines, levels, width), i * group)
-    return part
+    source, part = lax.optimization_barrier((fields, part))
+    second = exchange(source[group:].reshape(shape))
+    back = exchange(far_slopes(first, high, low, me, False))
+    outs = far_slopes(second, high, low, me, True)
+    fars = {0: outs[0]}
+    for k in order_of(devices):
+        fars[k] = ahead(outs[k], devices - k)
+    part = update(part, fields, back.reshape(group, lines, levels, width), 0)
+    flat = fields.reshape(comps * lines * levels, width)
+    part = part.reshape(flat.shape)
+    for offsets in groups_of(devices, UPDATE_CUTS):
+        part = update_blocks(
+            part, flat, devices, offsets, [fars[k] for k in offsets], me, devices, lines * levels
+        )
+    return part.reshape(fields.shape)
 
 
 def solution(mesh):

time: 228 us -> 216 us (0.947)
  the two profiles are of different devices: /device:TPU:0 before, /device:TPU:9 now
where the time goes in v2:
time: 216 us; the launch traced here: 212 us
  Pallas kernels  113 us (52%)
  starting transfers between devices  39.1 us (18%)
  waiting for transfers between devices  35.2 us (16%)
  local copies, waits for them, and re-layouts  24.5 us (11%)
    pallas_call x2, Pallas kernels, far_slopes(): pl.pallas_call(functools.partial(far_blocks_body if split else far_body,...  64.9 us
    ppermute x7, waiting for transfers between devices, ahead(): lax.ppermute(block, 'gx', [(i, (i + k) % devices) for i in range(devices)])  26.1 us
    pallas_call x1, Pallas kernels, local_part(): pl.pallas_call(local_body, grid=(lines, comps), in_specs=[block(None), bl...  21.7 us
    all_to_all x3, starting transfers between devices, exchange(): return lax.all_to_all(whole, 'gx', split_axis=0, concat_axis=0, tiled=True)  20.6 us
    unnamed x24, local copies, waits for them, and re-layouts  18.7 us
    ppermute x7, starting transfers between devices, ahead(): lax.ppermute(block, 'gx', [(i, (i + k) % devices) for i in range(devices)])  14 us
    pallas_call x1, Pallas kernels, strips(): pl.pallas_call(functools.partial(strip_body, pad), grid=(BAND // rows,),...  9.86 us
    pallas_call x3, Pallas kernels, update_blocks(): pl.pallas_call(functools.partial(update_blocks_body, offsets), grid_spec=...  9.14 us
  transfers between devices with their start and end apart: 12, of which 2 were waited for; matrix products, arithmetic and copies ran while one was open for 1% of the time, Pallas kernels for 52%

profile of v2, /device:TPU:9, one launch (start us, length us, event | category | flops | bytes accessed | tf_op | source)
XLA Modules:
  0.0 211.9 jit_solution(2245670489262329185)
XLA Ops:
  0.0 0.0 copy-start.11
  0.0 3.1 %slice.14 = bf16[2,4,128,1024]{3,2,1,0:T(8,128)(2,1)} slice(bf16[4,4,128,1024]{3,2,1,0:T(8,128)(2,1)} %u_ref.3), slice={[0:2], [0:4], [0:128], [0:1024]} | slice | bytes 4194304 | tf_op jit(solution)/shard_map/slice | solution.py:303
  3.1 5.6 %all-to-all-start = ((bf16[8,128,1024]{2,1,0:T(8,128)(2,1)}), bf16[8,128,1024]{2,1,0:T(8,128)(2,1)S(1)}, u32[]{:S(2)}, u32[]{:S(2)}) async-start(bf16[8,128,1024]{2,1,0:T(8,128)(2,1)} %bitcast.16), calls=%async_computation | async-start | bytes 4194304 | tf_op jit(solution)/shard_map/all_to_all | solution.py:298
  8.7 1.1 fusion
  9.9 3.1 %collective-permute-start = (bf16[4,4,4,1024]{3,2,1,0:T(4,128)(2,1)S(1)}, bf16[4,4,4,1024]{3,2,1,0:T(4,128)(2,1)S(1)}, u32[]{:S(2)}, u32[]{:S(2)}) collective-permute-start(bf16[4,4,4,1024]{3,2,1,0:T(4,128)(2,1)S(1)} %get-tuple-element.30), channel_id=1, source_target_pairs={{0,1},{1,2},{2,3},{4,5},{5,6},{6,7},{8,9},{9,10},{10,11},{12,13},{... | collective-permute-start | bytes 393224 | tf_op jit(solution)/shard_map/ppermute | solution.py:285
  13.0 1.3 collective-permute-start.1
  14.3 0.0 copy-done.11
  14.3 0.1 copy.8.strat_ref
  14.4 9.9 %shard_map.37 = (bf16[256,8960]{1,0:T(8,128)(2,1)}, bf16[256,8960]{1,0:T(8,128)(2,1)}) custom-call(f32[1,8192]{1,0:T(1,128)} %constant.9.row_ref), custom_call_target="tpu_custom_call" | custom-call | flops 8388608 | bytes 8388608 | tf_op jit(solution)/shard_map/pallas_call | solution.py:56
  24.3 0.0 collective-permute-done.below_ref
  24.3 0.0 collective-permute-done.1.above_ref
  24.3 0.0 copy-start
  24.3 2.2 %copy-done = bf16[4,4,128,1024]{3,2,1,0:T(8,128)(2,1)S(1)} copy-done((bf16[4,4,128,1024]{3,2,1,0:T(8,128)(2,1)S(1)}, bf16[4,4,128,1024]{3,2,1,0:T(8,128)(2,1)}, u32[]{:S(2)}) %copy-start) | copy-done | bytes 4194328
  26.5 0.0 copy-start.1
  26.5 2.3 %copy-done.1 = bf16[256,8960]{1,0:T(8,128)(2,1)S(1)} copy-done((bf16[256,8960]{1,0:T(8,128)(2,1)S(1)}, bf16[256,8960]{1,0:T(8,128)(2,1)}, u32[]{:S(2)}) %copy-start.1) | copy-done | bytes 4587544
  28.8 0.0 copy-start.4
  28.8 2.3 %copy-done.4 = bf16[256,8960]{1,0:T(8,128)(2,1)S(1)} copy-done((bf16[256,8960]{1,0:T(8,128)(2,1)S(1)}, bf16[256,8960]{1,0:T(8,128)(2,1)}, u32[]{:S(2)}) %copy-start.4) | copy-done | bytes 4587544
  31.1 21.7 %shard_map.38.part_ref = f32[4,4,128,1024]{3,2,1,0:T(8,128)} custom-call(bf16[4,4,128,1024]{3,2,1,0:T(8,128)(2,1)S(1)} %copy-done, bf16[4,4,128,1024]{3,2,1,0:T(8,128)(2,1)S(1)} %copy-done, bf16[4,4,128,1024]{3,2,1,0:T(8,128)(2,1)S(1)} %copy-done, bf16[4,4,128,1024]{3,2,1,0:T(8,128)(2,1)S(1)} %copy-done, ...), custom_call_target="tpu_custom_call" | custom-call | flops 8589934592 | bytes 16777216 | tf_op jit(solution)/shard_map/pallas_call | solution.py:181
  52.7 1.5 slice.15
  54.2 0.0 all-to-all-done
  54.2 7.8 %all-to-all-start.2 = ((bf16[8,128,1024]{2,1,0:T(8,128)(2,1)}), bf16[8,128,1024]{2,1,0:T(8,128)(2,1)}, u32[]{:S(2)}, u32[]{:S(2)}) async-start(bf16[8,128,1024]{2,1,0:T(8,128)(2,1)} %bitcast.17), calls=%async_computation.2 | async-start | bytes 4194304 | tf_op jit(solution)/shard_map/all_to_all | solution.py:298
  62.0 0.0 copy-start.2
  62.0 2.3 %copy-done.2 = bf16[256,8960]{1,0:T(8,128)(2,1)S(1)} copy-done((bf16[256,8960]{1,0:T(8,128)(2,1)S(1)}, bf16[256,8960]{1,0:T(8,128)(2,1)}, u32[]{:S(2)}) %copy-start.2) | copy-done | bytes 4587544
  64.3 0.0 copy-start.5
  64.3 2.3 %copy-done.5 = bf16[256,8960]{1,0:T(8,128)(2,1)S(1)} copy-done((bf16[256,8960]{1,0:T(8,128)(2,1)S(1)}, bf16[256,8960]{1,0:T(8,128)(2,1)}, u32[]{:S(2)}) %copy-start.5) | copy-done | bytes 4587544
  66.6 31.8 %shard_map.39 = bf16[1024,1024]{1,0:T(8,128)(2,1)} custom-call(s32[1]{0:T(128)} %bitcast.me_ref, bf16[1024,1024]{1,0:T(8,128)(2,1)S(1)} %bitcast.14, bf16[256,8960]{1,0:T(8,128)(2,1)S(1)} %copy-done.2, bf16[256,8960]{1,0:T(8,128)(2,1)S(1)} %copy-done.5), custom_call_target="tpu_custom_call" | custom-call | flops 30064771072 | bytes 13369344 | tf_op jit(solution)/shard_map/pallas_call | solution.py:120
  98.5 9.1 %all-to-all-done.2 = bf16[8,128,1024]{2,1,0:T(8,128)(2,1)} async-done(((bf16[8,128,1024]{2,1,0:T(8,128)(2,1)}), bf16[8,128,1024]{2,1,0:T(8,128)(2,1)}, u32[]{:S(2)}, u32[]{:S(2)}) %all-to-all-start.2) | async-done | bytes 2097184 | tf_op jit(solution)/shard_map/all_to_all | solution.py:298
  107.5 7.2 %all-to-all-start.1 = ((bf16[8,128,1024]{2,1,0:T(8,128)(2,1)}), bf16[8,128,1024]{2,1,0:T(8,128)(2,1)S(1)}, u32[]{:S(2)}, u32[]{:S(2)}) async-start(bf16[8,128,1024]{2,1,0:T(8,128)(2,1)} %bitcast.4), calls=%async_computation.1 | async-start | bytes 4194304 | tf_op jit(solution)/shard_map/all_to_all | solution.py:298
  114.7 0.0 copy-start.3
  114.7 2.3 %copy-done.3 = bf16[256,8960]{1,0:T(8,128)(2,1)S(1)} copy-done((bf16[256,8960]{1,0:T(8,128)(2,1)S(1)}, bf16[256,8960]{1,0:T(8,128)(2,1)}, u32[]{:S(2)}) %copy-start.3) | copy-done | bytes 4587544
  117.0 0.0 copy-start.6
  117.0 2.3 %copy-done.6 = bf16[256,8960]{1,0:T(8,128)(2,1)S(1)} copy-done((bf16[256,8960]{1,0:T(8,128)(2,1)S(1)}, bf16[256,8960]{1,0:T(8,128)(2,1)}, u32[]{:S(2)}) %copy-start.6) | copy-done | bytes 4587544
  119.3 33.0 %shard_map.41 = (bf16[128,1024]{1,0:T(8,128)(2,1)S(1)}, bf16[128,1024]{1,0:T(8,128)(2,1)S(1)}, bf16[128,1024]{1,0:T(8,128)(2,1)S(1)}, bf16[128,1024]{1,0:T(8,128...) custom-call(s32[1]{0:T(128)} %bitcast.me_ref, ...), custom_call_target="tpu_custom_call" | custom-call | flops 30064771072 | bytes 13369344 | tf_op jit(solution)/shard_map/pallas_call | solution.py:120
  152.4 0.0 copy-start.7
  152.4 0.7 copy-done.7
  153.1 2.1 collective-permute-start.2
  155.2 0.8 collective-permute-start.3
  156.0 1.8 collective-permute-start.4
  157.8 0.3 collective-permute-start.5
  158.1 1.2 collective-permute-start.6
  159.3 26.1 %collective-permute-done.2.refs_1_ = bf16[128,1024]{1,0:T(8,128)(2,1)S(1)} collective-permute-done((bf16[128,1024]{1,0:T(8,128)(2,1)S(1)}, bf16[128,1024]{1,0:T(8,128)(2,1)S(1)}, u32[]{:S(2)}, u32[]{:S(2)}) %collective-permute-start.2) | collective-permute-done | bytes 262176 | tf_op jit(solution)/shard_map/ppermute | solution.py:301
  185.4 0.0 copy-start.9
  185.4 0.5 collective-permute-start.7
  185.9 0.0 collective-permute-done.3.refs_2_
  185.9 0.0 copy-start.10
  185.9 0.2 copy-done.9
  186.1 0.5 copy-done.10
  186.6 7.3 %collective-permute-start.8 = (bf16[128,1024]{1,0:T(8,128)(2,1)S(1)}, bf16[128,1024]{1,0:T(8,128)(2,1)}, u32[]{:S(2)}, u32[]{:S(2)}) collective-permute-start(bf16[128,1024]{1,0:T(8,128)(2,1)S(1)} %get-tuple-element.28), channel_id=1, source_target_pairs={{0,4},{4,8},{8,12},{12,16},{16,20},{20,24},{24,28},{28,0},{1,5},{5... | collective-permute-start | bytes 786440 | tf_op jit(solution)/shard_map/ppermute | solution.py:301
  193.9 0.0 all-to-all-done.1
  193.9 0.0 copy-start.8
  193.9 1.3 copy-done.8
  195.3 7.5 %shard_map.40 = f32[4,4,128,1024]{3,2,1,0:T(8,128)} custom-call(f32[4,4,128,1024]{3,2,1,0:T(8,128)} %shard_map.38.part_ref, bf16[4,4,128,1024]{3,2,1,0:T(8,128)(2,1)} %u_ref.3, bf16[2,4,128,1024]{3,2,1,0:T(8,128)(2,1)} %bitcast.18), custom_call_target="tpu_custom_call", output_to_operand_aliasing={{}: (0, {})} | custom-call | flops 2097152 | bytes 12582912 | tf_op jit(solution)/shard_map/pallas_call | solution.py:212
  202.7 0.0 collective-permute-done.4.refs_3_
  202.8 4.4 %shard_map.42.part_ref = f32[2048,1024]{1,0:T(8,128)} custom-call(s32[1]{0:T(128)} %bitcast.me_ref, f32[2048,1024]{1,0:T(8,128)} %bitcast.15, bf16[2048,1024]{1,0:T(8,128)(2,1)} %bitcast.11, bf16[128,1024]{1,0:T(8,128)(2,1)} %copy-done.7, bf16[128,1024]{1,0:T(8,128)(2,1)} %copy-done.9, bf16[128,1024]{1,0:T(8,128)(2,1)} %copy-done.10, ...), custom_call_target="tpu_custom_call", output_to_operand_aliasing={{}: (1, {})} | custom-call | flops 1048576 | bytes 6291456 | tf_op jit(solution)/shard_map/pallas_call | solution.py:250
  207.1 0.0 collective-permute-done.5.refs_0_
  207.1 0.0 collective-permute-done.6.refs_1_
  207.1 2.4 %shard_map.43.part_ref = f32[2048,1024]{1,0:T(8,128)} custom-call(s32[1]{0:T(128)} %bitcast.me_ref, f32[2048,1024]{1,0:T(8,128)} %shard_map.42.part_ref, bf16[2048,1024]{1,0:T(8,128)(2,1)} %bitcast.12, bf16[128,1024]{1,0:T(8,128)(2,1)} %collective-permute-done.5.refs_0_, bf16[128,1024]{1,0:T(8,128)(2,1)} %collective-permute-done.6.refs_1_), custom_call_target="tpu_custom_call", output_to_operand_aliasing={{}: (1, {})} | custom-call | flops 524288 | bytes 3145728 | tf_op jit(solution)/shard_map/pallas_call | solution.py:250
  209.5 0.0 collective-permute-done.7.refs_0_
  209.5 0.0 collective-permute-done.8.refs_1_
  209.5 2.4 %shard_map.44 = f32[2048,1024]{1,0:T(8,128)} custom-call(s32[1]{0:T(128)} %bitcast.me_ref, f32[2048,1024]{1,0:T(8,128)} %shard_map.43.part_ref, bf16[2048,1024]{1,0:T(8,128)(2,1)} %bitcast.13, bf16[128,1024]{1,0:T(8,128)(2,1)} %collective-permute-done.7.refs_0_, bf16[128,1024]{1,0:T(8,128)(2,1)} %collective-permute-done.8.refs_1_), custom_call_target="tpu_custom_call", output_to_operand_aliasing={{}: (1, {})} | custom-call | flops 524288 | bytes 3145728 | tf_op jit(solution)/shard_map/pallas_call | solution.py:250
Async XLA Ops:
  0.0 14.3 %copy-start.11 = (f32[128]{0:T(128)S(1)}, f32[128]{0:T(128)}, u32[]{:S(2)}) copy-start(f32[128]{0:T(128)} %param.4) | copy-start | bytes 1540
  3.1 51.1 %all-to-all-start = ((bf16[8,128,1024]{2,1,0:T(8,128)(2,1)}), bf16[8,128,1024]{2,1,0:T(8,128)(2,1)S(1)}, u32[]{:S(2)}, u32[]{:S(2)}) async-start(bf16[8,128,1024]{2,1,0:T(8,128)(2,1)} %bitcast.16), calls=%async_computation | async-start | bytes 4194304 | tf_op jit(solution)/shard_map/all_to_all | solution.py:298
  9.9 14.4 %collective-permute-start = (bf16[4,4,4,1024]{3,2,1,0:T(4,128)(2,1)S(1)}, bf16[4,4,4,1024]{3,2,1,0:T(4,128)(2,1)S(1)}, u32[]{:S(2)}, u32[]{:S(2)}) collective-permute-start(bf16[4,4,4,1024]{3,2,1,0:T(4,128)(2,1)S(1)} %get-tuple-element.30), channel_id=1, source_target_pairs={{0,1},{1,2},{2,3},{4,5},{5,6},{6,7},{8,9},{9,10},{10,11},{12,13},{... | collective-permute-start | bytes 393224 | tf_op jit(solution)/shard_map/ppermute | solution.py:285
  13.0 11.3 %collective-permute-start.1 = (bf16[4,4,4,1024]{3,2,1,0:T(4,128)(2,1)S(1)}, bf16[4,4,4,1024]{3,2,1,0:T(4,128)(2,1)S(1)}, u32[]{:S(2)}, u32[]{:S(2)}) collective-permute-start(bf16[4,4,4,1024]{3,2,1,0:T(4,128)(2,1)S(1)} %get-tuple-element.29), channel_id=1, source_target_pairs={{1,0},{2,1},{3,2},{5,4},{6,5},{7,6},{9,8},{10,9},{11,10},{13,12},{... | collective-permute-start | bytes 393224 | tf_op jit(solution)/shard_map/ppermute | solution.py:286
  24.3 2.2 %copy-start = (bf16[4,4,128,1024]{3,2,1,0:T(8,128)(2,1)S(1)}, bf16[4,4,128,1024]{3,2,1,0:T(8,128)(2,1)}, u32[]{:S(2)}) copy-start(bf16[4,4,128,1024]{3,2,1,0:T(8,128)(2,1)} %u_ref.3) | copy-start | bytes 12582916
  26.5 2.3 %copy-start.1 = (bf16[256,8960]{1,0:T(8,128)(2,1)S(1)}, bf16[256,8960]{1,0:T(8,128)(2,1)}, u32[]{:S(2)}) copy-start(bf16[256,8960]{1,0:T(8,128)(2,1)} %get-tuple-element.17.high_ref) | copy-start | bytes 13762564
  28.8 2.3 %copy-start.4 = (bf16[256,8960]{1,0:T(8,128)(2,1)S(1)}, bf16[256,8960]{1,0:T(8,128)(2,1)}, u32[]{:S(2)}) copy-start(bf16[256,8960]{1,0:T(8,128)(2,1)} %get-tuple-element.18.low_ref) | copy-start | bytes 13762564
  54.2 53.3 %all-to-all-start.2 = ((bf16[8,128,1024]{2,1,0:T(8,128)(2,1)}), bf16[8,128,1024]{2,1,0:T(8,128)(2,1)}, u32[]{:S(2)}, u32[]{:S(2)}) async-start(bf16[8,128,1024]{2,1,0:T(8,128)(2,1)} %bitcast.17), calls=%async_computation.2 | async-start | bytes 4194304 | tf_op jit(solution)/shard_map/all_to_all | solution.py:298
  62.0 2.3 %copy-start.2 = (bf16[256,8960]{1,0:T(8,128)(2,1)S(1)}, bf16[256,8960]{1,0:T(8,128)(2,1)}, u32[]{:S(2)}) copy-start(bf16[256,8960]{1,0:T(8,128)(2,1)} %get-tuple-element.17.high_ref) | copy-start | bytes 13762564
  64.3 2.3 %copy-start.5 = (bf16[256,8960]{1,0:T(8,128)(2,1)S(1)}, bf16[256,8960]{1,0:T(8,128)(2,1)}, u32[]{:S(2)}) copy-start(bf16[256,8960]{1,0:T(8,128)(2,1)} %get-tuple-element.18.low_ref) | copy-start | bytes 13762564
  107.5 86.4 %all-to-all-start.1 = ((bf16[8,128,1024]{2,1,0:T(8,128)(2,1)}), bf16[8,128,1024]{2,1,0:T(8,128)(2,1)S(1)}, u32[]{:S(2)}, u32[]{:S(2)}) async-start(bf16[8,128,1024]{2,1,0:T(8,128)(2,1)} %bitcast.4), calls=%async_computation.1 | async-start | bytes 4194304 | tf_op jit(solution)/shard_map/all_to_all | solution.py:298
  114.7 2.3 %copy-start.3 = (bf16[256,8960]{1,0:T(8,128)(2,1)S(1)}, bf16[256,8960]{1,0:T(8,128)(2,1)}, u32[]{:S(2)}) copy-start(bf16[256,8960]{1,0:T(8,128)(2,1)} %get-tuple-element.17.high_ref) | copy-start | bytes 13762564
  117.0 2.3 %copy-start.6 = (bf16[256,8960]{1,0:T(8,128)(2,1)S(1)}, bf16[256,8960]{1,0:T(8,128)(2,1)}, u32[]{:S(2)}) copy-start(bf16[256,8960]{1,0:T(8,128)(2,1)} %get-tuple-element.18.low_ref) | copy-start | bytes 13762564
  152.4 0.7 copy-start.7
  153.1 32.3 %collective-permute-start.2 = (bf16[128,1024]{1,0:T(8,128)(2,1)S(1)}, bf16[128,1024]{1,0:T(8,128)(2,1)S(1)}, u32[]{:S(2)}, u32[]{:S(2)}) collective-permute-start(bf16[128,1024]{1,0:T(8,128)(2,1)S(1)} %get-tuple-element.22), channel_id=1, source_target_pairs={{0,16},{4,20},{8,24},{12,28},{16,0},{20,4},{24,8},{28,12},{1,17},{... | collective-permute-start | bytes 786440 | tf_op jit(solution)/shard_map/ppermute | solution.py:301
  155.2 30.7 %collective-permute-start.3 = (bf16[128,1024]{1,0:T(8,128)(2,1)S(1)}, bf16[128,1024]{1,0:T(8,128)(2,1)S(1)}, u32[]{:S(2)}, u32[]{:S(2)}) collective-permute-start(bf16[128,1024]{1,0:T(8,128)(2,1)S(1)} %get-tuple-element.23), channel_id=1, source_target_pairs={{0,20},{4,24},{8,28},{12,0},{16,4},{20,8},{24,12},{28,16},{1,21},{... | collective-permute-start | bytes 786440 | tf_op jit(solution)/shard_map/ppermute | solution.py:301
  156.0 46.8 %collective-permute-start.4 = (bf16[128,1024]{1,0:T(8,128)(2,1)S(1)}, bf16[128,1024]{1,0:T(8,128)(2,1)}, u32[]{:S(2)}, u32[]{:S(2)}) collective-permute-start(bf16[128,1024]{1,0:T(8,128)(2,1)S(1)} %get-tuple-element.24), channel_id=1, source_target_pairs={{0,12},{4,16},{8,20},{12,24},{16,28},{20,0},{24,4},{28,8},{1,13},{... | collective-permute-start | bytes 786440 | tf_op jit(solution)/shard_map/ppermute | solution.py:301
  157.8 49.3 %collective-permute-start.5 = (bf16[128,1024]{1,0:T(8,128)(2,1)S(1)}, bf16[128,1024]{1,0:T(8,128)(2,1)}, u32[]{:S(2)}, u32[]{:S(2)}) collective-permute-start(bf16[128,1024]{1,0:T(8,128)(2,1)S(1)} %get-tuple-element.25), channel_id=1, source_target_pairs={{0,24},{4,28},{8,0},{12,4},{16,8},{20,12},{24,16},{28,20},{1,25},{... | collective-permute-start | bytes 786440 | tf_op jit(solution)/shard_map/ppermute | solution.py:301
  158.1 49.0 %collective-permute-start.6 = (bf16[128,1024]{1,0:T(8,128)(2,1)S(1)}, bf16[128,1024]{1,0:T(8,128)(2,1)}, u32[]{:S(2)}, u32[]{:S(2)}) collective-permute-start(bf16[128,1024]{1,0:T(8,128)(2,1)S(1)} %get-tuple-element.26), channel_id=1, source_target_pairs={{0,8},{4,12},{8,16},{12,20},{16,24},{20,28},{24,0},{28,4},{1,9},{5... | collective-permute-start | bytes 786440 | tf_op jit(solution)/shard_map/ppermute | solution.py:301
  185.4 0.7 copy-start.9
  185.4 24.1 %collective-permute-start.7 = (bf16[128,1024]{1,0:T(8,128)(2,1)S(1)}, bf16[128,1024]{1,0:T(8,128)(2,1)}, u32[]{:S(2)}, u32[]{:S(2)}) collective-permute-start(bf16[128,1024]{1,0:T(8,128)(2,1)S(1)} %get-tuple-element.27), channel_id=1, source_target_pairs={{0,28},{4,0},{8,4},{12,8},{16,12},{20,16},{24,20},{28,24},{1,29},{... | collective-permute-start | bytes 786440 | tf_op jit(solution)/shard_map/ppermute | solution.py:301
  185.9 0.7 copy-start.10
  186.6 22.9 %collective-permute-start.8 = (bf16[128,1024]{1,0:T(8,128)(2,1)S(1)}, bf16[128,1024]{1,0:T(8,128)(2,1)}, u32[]{:S(2)}, u32[]{:S(2)}) collective-permute-start(bf16[128,1024]{1,0:T(8,128)(2,1)S(1)} %get-tuple-element.28), channel_id=1, source_target_pairs={{0,4},{4,8},{8,12},{12,16},{16,20},{20,24},{24,28},{28,0},{1,5},{5... | collective-permute-start | bytes 786440 | tf_op jit(solution)/shard_map/ppermute | solution.py:301
  193.9 1.3 copy-start.8

commit v3 on v2

v3 whole, which is shorter than its diff:
```python
import functools
import math

import jax
import jax.numpy as jnp
import numpy as np
from jax import lax
from jax.experimental import pallas as pl
from jax.experimental.pallas import tpu as pltpu
from jax.sharding import PartitionSpec as P

STENCIL = (4.0 / 5.0, -1.0 / 5.0, 4.0 / 105.0, -1.0 / 280.0)
BAND = 128
COLUMNS = 256
UPDATE_VMEM = 16 * 2**20
F32 = jnp.float32
BF16 = jnp.bfloat16


def kernel_row(length):
    index = np.arange(length)
    signed = np.where(index < length // 2, index, index - length).astype(np.float64)
    angle = np.pi * np.where(signed == 0, 1.0, signed) / length
    row = np.where(index % 2 == 0, 1.0, -1.0) * (np.pi / length) / np.tan(angle)
    row = np.where((index == 0) | (index == length // 2), 0.0, row)
    return jnp.asarray(row.astype(np.float32))[None, :]


def strip_body(pad, row_ref, high_ref, low_ref, run_ref):
    rows, length = run_ref.shape

    @pl.when(pl.program_id(0) == 0)
    def _():
        wide = jnp.broadcast_to(row_ref[...], (rows, length))
        run_ref[...] = pltpu.roll(wide, pad, 1, stride=1, stride_axis=0)

    @pl.when(pl.program_id(0) > 0)
    def _():
        run_ref[...] = pltpu.roll(run_ref[...], rows, 1)

    run = run_ref[...]
    high = run.astype(BF16)
    low = (run - high.astype(F32)).astype(BF16)
    high_ref[:, :length] = high
    low_ref[:, :length] = low
    if pad:
        high_ref[:, length:] = high[:, :pad]
        low_ref[:, length:] = low[:, :pad]


def strips(length, width):
    pad = width - BAND
    rows = 16
    shape = jax.ShapeDtypeStruct((BAND, length + pad), BF16)
    spec = pl.BlockSpec((rows, length + pad), lambda i: (i, 0))
    return pl.pallas_call(
        functools.partial(strip_body, pad),
        grid=(BAND // rows,),
        in_specs=[pl.BlockSpec((1, length), lambda i: (0, 0))],
        out_specs=[spec, spec],
        out_shape=[shape, shape],
        scratch_shapes=[pltpu.VMEM((rows, length), F32)],
        compiler_params=pltpu.CompilerParams(vmem_limit_bytes=8 * 2**20),
        cost_estimate=pl.CostEstimate(
            flops=4 * BAND * length, bytes_accessed=4 * BAND * length, transcendentals=0
        ),
    )(kernel_row(length))


def panel(strip_ref, first, width, columns):
    runs = [
        strip_ref[:, pl.ds(pl.multiple_of(first + width - BAND - BAND * i, BAND), columns)]
        for i in range(width // BAND)
    ]
    return runs[0] if len(runs) == 1 else jnp.concatenate(runs, axis=0)


def dot(left, right):
    return jnp.dot(left, right, preferred_element_type=F32)


def far_sum(devices, column, columns, lines_ref, high_ref, low_ref):
    total_rows, width = lines_ref.shape
    rows = total_rows // devices
    total = None
    for step in range(1, devices):
        cut = (devices - step) * rows
        moved = jnp.concatenate([lines_ref[cut:, :], lines_ref[:cut, :]], axis=0)
        first = step * width + column
        for strip_ref in (high_ref, low_ref):
            part = dot(moved, panel(strip_ref, first, width, columns))
            total = part if total is None else total + part
    return total.astype(BF16)


def far_blocks_body(devices, me_ref, lines_ref, high_ref, low_ref, *refs):
    outs, all_ref = refs[:-1], refs[-1]
    rows, columns = outs[0].shape
    all_ref[...] = far_sum(
        devices, pl.program_id(0) * columns, columns, lines_ref, high_ref, low_ref
    )
    for k in range(devices):
        start = pl.multiple_of((me_ref[0] + devices - k) % devices * rows, rows)
        outs[k][...] = all_ref[pl.ds(start, rows), :]


def far_slopes(lines, high, low, me):
    devices, rows, width = lines.shape
    total_rows = devices * rows
    columns = COLUMNS
    whole = pl.BlockSpec((total_rows, width), lambda j, m: (0, 0))
    strip = pl.BlockSpec(memory_space=pltpu.VMEM)
    return pl.pallas_call(
        functools.partial(far_blocks_body, devices),
        grid_spec=pltpu.PrefetchScalarGridSpec(
            num_scalar_prefetch=1,
            grid=(width // columns,),
            in_specs=[whole, strip, strip],
            out_specs=[pl.BlockSpec((rows, columns), lambda j, m: (0, j))] * devices,
            scratch_shapes=[pltpu.VMEM((total_rows, columns), BF16)],
        ),
        out_shape=[jax.ShapeDtypeStruct((rows, width), BF16)] * devices,
        compiler_params=pltpu.CompilerParams(vmem_limit_bytes=20 * 2**20),
        cost_estimate=pl.CostEstimate(
            flops=4 * total_rows * (devices - 1) * width * width,
            bytes_accessed=4 * total_rows * width + 4 * high.size,
            transcendentals=0,
        ),
    )(me, lines.reshape(total_rows, width), high, low)


def local_body(base, field_ref, u_ref, w_ref, b_ref, below_ref, above_ref, strat_ref, high_ref, low_ref, out_ref, pad_ref):
    comp = base + pl.program_id(1)
    levels, width = out_ref.shape
    pad_ref[8 : 8 + levels, :] = field_ref[...].astype(F32)
    pad_ref[4:8, :] = below_ref[...].astype(F32)
    pad_ref[8 + levels : 12 + levels, :] = above_ref[...].astype(F32)
    is_w = (comp == 2).astype(F32)
    is_b = (comp == 3).astype(F32)
    strat = strat_ref[...] * is_b
    columns = COLUMNS
    for j in range(width // columns):
        here = slice(j * columns, (j + 1) * columns)
        near = dot(field_ref[...], panel(high_ref, j * columns, width, columns)) + dot(
            field_ref[...], panel(low_ref, j * columns, width, columns)
        )
        slope_z = None
        for offset in range(1, 5):
            term = STENCIL[offset - 1] * (
                pad_ref[8 + offset : 8 + offset + levels, here]
                - pad_ref[8 - offset : 8 - offset + levels, here]
            )
            slope_z = term if slope_z is None else slope_z + term
        speed_w = w_ref[:, here].astype(F32)
        out_ref[:, here] = (
            is_w * b_ref[:, here].astype(F32)
            - strat * speed_w
            - (u_ref[:, here].astype(F32) * near + speed_w * slope_z)
        )


def local_part(fields, below, above, strat_col, high, low, base, count, held):
    _, lines, levels, width = fields.shape

    def block(comp):
        return pl.BlockSpec(
            (None, None, levels, width),
            (lambda l, c: (base + c, l, 0, 0)) if comp is None else (lambda l, c: (comp, l, 0, 0)),
        )

    halo = pl.BlockSpec((None, None, 4, width), lambda l, c: (base + c, l, 0, 0))
    whole = pl.BlockSpec(memory_space=pltpu.VMEM)
    return pl.pallas_call(
        functools.partial(local_body, base),
        grid=(lines, count),
        in_specs=[
            block(None),
            block(0),
            block(2),
            block(3),
            halo,
            halo,
            pl.BlockSpec((levels, 1), lambda l, c: (0, 0)),
            whole,
            whole,
        ],
        out_specs=pl.BlockSpec((None, None, levels, width), lambda l, c: (c, l, 0, 0)),
        out_shape=jax.ShapeDtypeStruct((held, lines, levels, width), F32),
        scratch_shapes=[pltpu.VMEM((levels + 16, width), F32)],
        compiler_params=pltpu.CompilerParams(vmem_limit_bytes=20 * 2**20),
        cost_estimate=pl.CostEstimate(
            flops=4 * count * lines * levels * width * width,
            bytes_accessed=8 * count * lines * levels * width,
            transcendentals=0,
        ),
    )(fields, fields, fields, fields, below, above, strat_col, high, low)


def finish_body(count, me_ref, part_ref, u_ref, *refs):
    fars, out_ref = refs[:count], refs[-1]
    for k, far_ref in enumerate(fars):

        @pl.when(pl.program_id(0) == k)
        def _(far_ref=far_ref):
            out_ref[...] = part_ref[...] - u_ref[...].astype(F32) * far_ref[...].astype(F32)


def finish(out, part, speed_u, offsets, fars, me, total_rows):
    devices = len(fars)
    rows, width = fars[0].shape
    u_blocks = speed_u.shape[0] // rows
    base = 0 if out is None else total_rows // rows - devices
    given = [] if out is None else [out]

    def owner(i, m):
        offset = offsets[-1]
        for index in range(devices - 1):
            offset = jnp.where(i == index, offsets[index], offset)
        return (m[0] + offset) % devices

    return pl.pallas_call(
        functools.partial(finish_body, devices),
        grid_spec=pltpu.PrefetchScalarGridSpec(
            num_scalar_prefetch=1,
            grid=(devices,),
            in_specs=[
                pl.BlockSpec((rows, width), lambda i, m: (owner(i, m), 0)),
                pl.BlockSpec((rows, width), lambda i, m: (owner(i, m) % u_blocks, 0)),
            ]
            + [pl.BlockSpec((rows, width), lambda i, m: (0, 0))] * devices
            + [pl.BlockSpec(memory_space=pl.ANY)] * len(given),
            out_specs=pl.BlockSpec((rows, width), lambda i, m: (base + owner(i, m), 0)),
        ),
        out_shape=jax.ShapeDtypeStruct((total_rows, width), F32),
        input_output_aliases={3 + devices: 0} if given else {},
        compiler_params=pltpu.CompilerParams(vmem_limit_bytes=UPDATE_VMEM),
        cost_estimate=pl.CostEstimate(
            flops=2 * devices * rows * width,
            bytes_accessed=12 * devices * rows * width,
            transcendentals=0,
        ),
    )(me, part, speed_u, *fars, *given)


def order_of(devices):
    return sorted(range(1, devices), key=lambda k: abs(2 * k - devices))


def halos(fields):
    count = lax.axis_size("gz")
    forward = [(i, i + 1) for i in range(count - 1)]
    backward = [(target, source) for source, target in forward]
    levels = fields.shape[2]
    below = lax.ppermute(fields[:, :, levels - 4 :], "gz", forward)
    above = lax.ppermute(fields[:, :, :4], "gz", backward)
    return below, above


def body(fields, strat_sq):
    comps, lines, levels, width = fields.shape
    devices = lax.axis_size("gx")
    group = comps // 2
    shape = (devices, group * lines * levels // devices, width)
    me = lax.axis_index("gx").astype(jnp.int32)[None]

    def exchange(whole):
        return lax.all_to_all(whole, "gx", split_axis=0, concat_axis=0, tiled=True)

    def ahead(block, k):
        return lax.ppermute(block, "gx", [(i, (i + k) % devices) for i in range(devices)])

    first = exchange(fields[:group].reshape(shape))
    below, above = halos(fields)
    high, low = strips(devices * width, width)
    local = (fields, below, above, strat_sq[:, None], high, low)
    early = local_part(*local, 0, group, group)
    part = local_part(*local, group, group, group)
    source, early, part = lax.optimization_barrier((fields, early, part))
    speed_u = source[0].reshape(lines * levels, width)
    second = exchange(source[group:].reshape(shape))
    order = order_of(devices)
    held = group * lines * levels

    def back(outs, k):
        return ahead(outs[k], devices - k)

    outs, second = lax.optimization_barrier((far_slopes(first, high, low, me), second))
    fars = [outs[0]] + [back(outs, k) for k in order]
    later = list(far_slopes(second, high, low, me))
    last = [later[0]]
    for i, k in enumerate(order):
        later[k], fars[1 + i] = lax.optimization_barrier((later[k], fars[1 + i]))
        last.append(back(later, k))
    shape_flat = (held, width)
    out = finish(None, early.reshape(shape_flat), speed_u, [0] + order, fars, me, 2 * held)
    out = finish(out, part.reshape(shape_flat), speed_u, [0] + order, last, me, 2 * held)
    return out.reshape(fields.shape)


def solution(mesh):
    placed = (P(None, None, "gz", "gx"), P("gz"))
    return jax.shard_map(
        body, mesh=mesh, in_specs=placed, out_specs=P(None, None, "gz", "gx"), check_vma=False
    )
```

time: 216 us -> 208 us (0.963); the launches traced: 212 us -> 207 us
  Pallas kernels: 113 us -> 96.9 us
  waiting for transfers between devices: 35.2 us -> 46.7 us
  local copies, waits for them, and re-layouts: 24.5 us -> 20.3 us
  starting transfers between devices: 39.1 us -> 43.1 us
    ppermute x7 -> x14, starting transfers between devices: 14 us -> 24.3 us  [ahead(): lax.ppermute(block, 'gx', [(i, (i + k) % devices) for i in range(devices)])]
    pallas_call x7 -> x6, Pallas kernels: 103 us -> 94.4 us  [the longest x2 66.3 us: far_slopes(): pl.pallas_call(functools.partial(far_blocks_body, devices), grid_spec=plt...]
    pallas_call x1, Pallas kernels: 9.86 us -> 2.55 us  [strips(): pl.pallas_call(functools.partial(strip_body, pad), grid=(BAND // rows,),...]
    all_to_all x3 -> x2, starting transfers between devices: 20.6 us -> 13.6 us  [exchange(): return lax.all_to_all(whole, 'gx', split_axis=0, concat_axis=0, tiled=True)]
    all_to_all x3 -> x2, waiting for transfers between devices: 9.09 us -> 15.3 us  [exchange(): return lax.all_to_all(whole, 'gx', split_axis=0, concat_axis=0, tiled=True)]
    unnamed x24 -> x28, local copies, waits for them, and re-layouts: 18.7 us -> 13.1 us
    ppermute x7 -> x14, waiting for transfers between devices: 26.1 us -> 31.4 us  [ahead(): lax.ppermute(block, 'gx', [(i, (i + k) % devices) for i in range(devices)])]
  transfers between devices with their start and end apart: 12 -> 18, of which waited for: 2 -> 5; matrix products, arithmetic and copies ran while one was open for 1% -> 2% of each run, Pallas kernels for 52% -> 45%
where the time goes in v3:
time: 208 us; the launch traced here: 207 us
  Pallas kernels  96.9 us (47%)
  waiting for transfers between devices  46.7 us (22%)
  starting transfers between devices  43.1 us (21%)
  local copies, waits for them, and re-layouts  20.3 us (10%)
    pallas_call x2, Pallas kernels, far_slopes(): pl.pallas_call(functools.partial(far_blocks_body, devices), grid_spec=plt...  66.3 us
    ppermute x14, waiting for transfers between devices, ahead(): lax.ppermute(block, 'gx', [(i, (i + k) % devices) for i in range(devices)])  31.4 us
    ppermute x14, starting transfers between devices, ahead(): lax.ppermute(block, 'gx', [(i, (i + k) % devices) for i in range(devices)])  24.3 us
    pallas_call x2, Pallas kernels, local_part(): pl.pallas_call(functools.partial(local_body, base), grid=(lines, count),...  20.5 us
    all_to_all x2, waiting for transfers between devices, exchange(): return lax.all_to_all(whole, 'gx', split_axis=0, concat_axis=0, tiled=True)  15.3 us
    all_to_all x2, starting transfers between devices, exchange(): return lax.all_to_all(whole, 'gx', split_axis=0, concat_axis=0, tiled=True)  13.6 us
    unnamed x28, local copies, waits for them, and re-layouts  13.1 us
    pallas_call x2, Pallas kernels, finish(): pl.pallas_call(functools.partial(finish_body, devices), grid_spec=pltpu.P...  7.53 us
  transfers between devices with their start and end apart: 18, of which 5 were waited for; matrix products, arithmetic and copies ran while one was open for 2% of the time, Pallas kernels for 45%

profile of v3, /device:TPU:9, one launch (start us, length us, event | category | flops | bytes accessed | tf_op | source)
XLA Modules:
  0.0 207.2 jit_solution(9431210265925724392)
XLA Ops:
  0.0 3.2 %slice.18 = bf16[2,4,128,1024]{3,2,1,0:T(8,128)(2,1)} slice(bf16[4,4,128,1024]{3,2,1,0:T(8,128)(2,1)} %b_ref.3), slice={[0:2], [0:4], [0:128], [0:1024]} | slice | bytes 4194304 | tf_op jit(solution)/shard_map/slice | solution.py:272
  3.2 5.6 %all-to-all-start = ((bf16[8,128,1024]{2,1,0:T(8,128)(2,1)}), bf16[8,128,1024]{2,1,0:T(8,128)(2,1)}, u32[]{:S(2)}, u32[]{:S(2)}) async-start(bf16[8,128,1024]{2,1,0:T(8,128)(2,1)} %bitcast.4), calls=%async_computation | async-start | bytes 4194304 | tf_op jit(solution)/shard_map/all_to_all | solution.py:267
  8.8 1.1 fusion
  9.9 1.3 collective-permute-start.1
  11.2 4.0 %collective-permute-start = (bf16[4,4,4,1024]{3,2,1,0:T(4,128)(2,1)S(1)}, bf16[4,4,4,1024]{3,2,1,0:T(4,128)(2,1)S(1)}, u32[]{:S(2)}, u32[]{:S(2)}) collective-permute-start(bf16[4,4,4,1024]{3,2,1,0:T(4,128)(2,1)S(1)} %get-tuple-element.94), channel_id=1, source_target_pairs={{0,1},{1,2},{2,3},{4,5},{5,6},{6,7},{8,9},{9,10},{10,11},{12,13},{... | collective-permute-start | bytes 393224 | tf_op jit(solution)/shard_map/ppermute | solution.py:254
  15.2 0.0 copy-done.13
  15.3 0.1 copy.5.strat_ref
  15.4 0.0 copy-done.8
  15.4 2.6 %shard_map.37 = (bf16[128,9088]{1,0:T(8,128)(2,1)S(1)}, bf16[128,9088]{1,0:T(8,128)(2,1)S(1)}) custom-call(f32[1,8192]{1,0:T(1,128)S(1)} %copy-done.8), custom_call_target="tpu_custom_call" | custom-call | flops 4194304 | bytes 4194304 | tf_op jit(solution)/shard_map/pallas_call | solution.py:56
  17.9 0.0 copy-start.5
  17.9 0.0 collective-permute-done.1.above_ref
  18.0 0.0 collective-permute-done.below_ref
  18.0 0.0 copy-start
  18.0 3.0 %copy-done = bf16[4,4,128,1024]{3,2,1,0:T(8,128)(2,1)S(1)} copy-done((bf16[4,4,128,1024]{3,2,1,0:T(8,128)(2,1)S(1)}, bf16[4,4,128,1024]{3,2,1,0:T(8,128)(2,1)}, u32[]{:S(2)}) %copy-start) | copy-done | bytes 4194328
  21.0 10.3 %shard_map.39 = f32[2,4,128,1024]{3,2,1,0:T(8,128)S(1)} custom-call(bf16[4,4,128,1024]{3,2,1,0:T(8,128)(2,1)S(1)} %copy-done, bf16[4,4,128,1024]{3,2,1,0:T(8,128)(2,1)S(1)} %copy-done, bf16[4,4,128,1024]{3,2,1,0:T(8,128)(2,1)S(1)} %copy-done, bf16[4,4,128,1024]{3,2,1,0:T(8,128)(2,1)S(1)} %copy-done, ...), custom_call_target="tpu_custom_call" | custom-call | flops 4294967296 | bytes 8388608 | tf_op jit(solution)/shard_map/pallas_call | solution.py:173
  31.3 0.0 copy-done.5
  31.3 2.0 copy-done.3
  33.3 10.3 %shard_map.38 = f32[2,4,128,1024]{3,2,1,0:T(8,128)S(1)} custom-call(bf16[4,4,128,1024]{3,2,1,0:T(8,128)(2,1)S(1)} %copy-done, bf16[4,4,128,1024]{3,2,1,0:T(8,128)(2,1)S(1)} %copy-done, bf16[4,4,128,1024]{3,2,1,0:T(8,128)(2,1)S(1)} %copy-done, bf16[4,4,128,1024]{3,2,1,0:T(8,128)(2,1)S(1)} %copy-done, ...), custom_call_target="tpu_custom_call" | custom-call | flops 4294967296 | bytes 8388608 | tf_op jit(solution)/shard_map/pallas_call | solution.py:173
  43.5 0.0 copy-start.1
  43.5 2.0 copy-done.1
  45.5 1.5 slice.19
  47.0 7.3 %all-to-all-done = bf16[8,128,1024]{2,1,0:T(8,128)(2,1)} async-done(((bf16[8,128,1024]{2,1,0:T(8,128)(2,1)}), bf16[8,128,1024]{2,1,0:T(8,128)(2,1)}, u32[]{:S(2)}, u32[]{:S(2)}) %all-to-all-start) | async-done | bytes 2097184 | tf_op jit(solution)/shard_map/all_to_all | solution.py:267
  54.3 7.9 %all-to-all-start.1 = ((bf16[8,128,1024]{2,1,0:T(8,128)(2,1)}), bf16[8,128,1024]{2,1,0:T(8,128)(2,1)}, u32[]{:S(2)}, u32[]{:S(2)}) async-start(bf16[8,128,1024]{2,1,0:T(8,128)(2,1)} %bitcast.14), calls=%async_computation.1 | async-start | bytes 4194304 | tf_op jit(solution)/shard_map/all_to_all | solution.py:267
  62.2 1.7 copy-done.6
  63.9 33.1 %shard_map.40 = (bf16[128,1024]{1,0:T(8,128)(2,1)S(1)}, bf16[128,1024]{1,0:T(8,128)(2,1)S(1)}, bf16[128,1024]{1,0:T(8,128)(2,1)S(1)}, bf16[128,1024]{1,0:T(8,128...) custom-call(s32[1]{0:T(128)} %bitcast.me_ref, ...), custom_call_target="tpu_custom_call" | custom-call | flops 30064771072 | bytes 8847360 | tf_op jit(solution)/shard_map/pallas_call | solution.py:113
  97.0 0.7 copy-done.9
  97.7 0.7 copy-done.10
  98.4 0.7 copy-done.11
  99.1 0.7 copy-done.12
  99.8 8.0 %all-to-all-done.1 = bf16[8,128,1024]{2,1,0:T(8,128)(2,1)} async-done(((bf16[8,128,1024]{2,1,0:T(8,128)(2,1)}), bf16[8,128,1024]{2,1,0:T(8,128)(2,1)}, u32[]{:S(2)}, u32[]{:S(2)}) %all-to-all-start.1) | async-done | bytes 2097184 | tf_op jit(solution)/shard_map/all_to_all | solution.py:267
  107.7 3.1 %collective-permute-start.2 = (bf16[128,1024]{1,0:T(8,128)(2,1)}, bf16[128,1024]{1,0:T(8,128)(2,1)S(1)}, u32[]{:S(2)}, u32[]{:S(2)}) collective-permute-start(bf16[128,1024]{1,0:T(8,128)(2,1)} %copy-done.12), channel_id=1, source_target_pairs={{0,16},{4,20},{8,24},{12,28},{16,0},{20,4},{24,8},{28,12},{1,17},{... | collective-permute-start | bytes 786440 | tf_op jit(solution)/shard_map/ppermute | solution.py:270
  110.8 0.6 collective-permute-start.4
  111.4 2.1 %collective-permute-start.6 = (bf16[128,1024]{1,0:T(8,128)(2,1)}, bf16[128,1024]{1,0:T(8,128)(2,1)S(1)}, u32[]{:S(2)}, u32[]{:S(2)}) collective-permute-start(bf16[128,1024]{1,0:T(8,128)(2,1)} %copy-done.10), channel_id=1, source_target_pairs={{0,12},{4,16},{8,20},{12,24},{16,28},{20,0},{24,4},{28,8},{1,13},{... | collective-permute-start | bytes 786440 | tf_op jit(solution)/shard_map/ppermute | solution.py:270
  113.5 0.6 collective-permute-start.8
  114.0 0.9 collective-permute-start.10
  115.0 1.7 copy-done.7
  116.6 33.2 %shard_map.41 = (bf16[128,1024]{1,0:T(8,128)(2,1)S(1)}, bf16[128,1024]{1,0:T(8,128)(2,1)S(1)}, bf16[128,1024]{1,0:T(8,128)(2,1)S(1)}, bf16[128,1024]{1,0:T(8,128...) custom-call(s32[1]{0:T(128)} %bitcast.me_ref, ...), custom_call_target="tpu_custom_call" | custom-call | flops 30064771072 | bytes 8847360 | tf_op jit(solution)/shard_map/pallas_call | solution.py:113
  149.9 0.0 collective-permute-done.2.refs_1_
  149.9 0.4 collective-permute-start.12
  150.3 0.0 collective-permute-done.4.refs_2_
  150.3 1.4 collective-permute-start.14
  151.7 0.0 collective-permute-done.6.refs_3_
  151.7 4.1 %collective-permute-start.3 = (bf16[128,1024]{1,0:T(8,128)(2,1)S(1)}, bf16[128,1024]{1,0:T(8,128)(2,1)S(1)}, u32[]{:S(2)}, u32[]{:S(2)}) collective-permute-start(bf16[128,1024]{1,0:T(8,128)(2,1)S(1)} %get-tuple-element.65), channel_id=1, source_target_pairs={{0,16},{4,20},{8,24},{12,28},{16,0},{20,4},{24,8},{28,12},{1,17},{... | collective-permute-start | bytes 786440 | tf_op jit(solution)/shard_map/ppermute | solution.py:270
  155.8 0.0 collective-permute-done.8.refs_4_
  155.8 0.0 collective-permute-start.5
  155.8 0.0 collective-permute-done.10.refs_5_
  155.8 2.6 %collective-permute-start.7 = (bf16[128,1024]{1,0:T(8,128)(2,1)S(1)}, bf16[128,1024]{1,0:T(8,128)(2,1)S(1)}, u32[]{:S(2)}, u32[]{:S(2)}) collective-permute-start(bf16[128,1024]{1,0:T(8,128)(2,1)S(1)} %get-tuple-element.71), channel_id=1, source_target_pairs={{0,12},{4,16},{8,20},{12,24},{16,28},{20,0},{24,4},{28,8},{1,13},{... | collective-permute-start | bytes 786440 | tf_op jit(solution)/shard_map/ppermute | solution.py:270
  158.5 0.0 collective-permute-done.12.refs_6_
  158.5 0.0 collective-permute-start.9
  158.5 0.0 collective-permute-done.14.refs_7_
  158.5 2.0 collective-permute-start.11
  160.5 23.0 %collective-permute-done.3.refs_1_ = bf16[128,1024]{1,0:T(8,128)(2,1)S(1)} collective-permute-done((bf16[128,1024]{1,0:T(8,128)(2,1)S(1)}, bf16[128,1024]{1,0:T(8,128)(2,1)S(1)}, u32[]{:S(2)}, u32[]{:S(2)}) %collective-permute-start.3) | collective-permute-done | bytes 262176 | tf_op jit(solution)/shard_map/ppermute | solution.py:270
  183.5 0.0 collective-permute-start.13
  183.5 0.0 collective-permute-done.5.refs_2_
  183.5 6.5 %collective-permute-start.15 = (bf16[128,1024]{1,0:T(8,128)(2,1)S(1)}, bf16[128,1024]{1,0:T(8,128)(2,1)S(1)}, u32[]{:S(2)}, u32[]{:S(2)}) collective-permute-start(bf16[128,1024]{1,0:T(8,128)(2,1)S(1)} %get-tuple-element.83), channel_id=1, source_target_pairs={{0,4},{4,8},{8,12},{12,16},{16,20},{20,24},{24,28},{28,0},{1,5},{5... | collective-permute-start | bytes 786440 | tf_op jit(solution)/shard_map/ppermute | solution.py:270
  190.0 1.3 slice.17
  191.3 3.8 %shard_map.42.refs_8_ = f32[2048,1024]{1,0:T(8,128)} custom-call(s32[1]{0:T(128)} %bitcast.me_ref, f32[1024,1024]{1,0:T(8,128)S(1)} %bitcast.10, bf16[512,1024]{1,0:T(8,128)(2,1)S(1)} %bitcast.12, bf16[128,1024]{1,0:T(8,128)(2,1)S(1)} %get-tuple-element.85.refs_0_, bf16[128,1024]{1,0:T(8,128)(2,1)S(1)} %collective-permute-done.2.refs_1_, ...), custom_call_target="tpu_custom_call" | custom-call | flops 2097152 | bytes 12582912 | tf_op jit(solution)/shard_map/pallas_call | solution.py:221
  195.1 0.0 collective-permute-done.7.refs_3_
  195.1 7.6 %collective-permute-done.9.refs_4_ = bf16[128,1024]{1,0:T(8,128)(2,1)S(1)} collective-permute-done((bf16[128,1024]{1,0:T(8,128)(2,1)S(1)}, bf16[128,1024]{1,0:T(8,128)(2,1)S(1)}, u32[]{:S(2)}, u32[]{:S(2)}) %collective-permute-start.9) | collective-permute-done | bytes 262176 | tf_op jit(solution)/shard_map/ppermute | solution.py:270
  202.6 0.0 collective-permute-done.11.refs_5_
  202.7 0.8 collective-permute-done.13.refs_6_
  203.5 0.0 collective-permute-done.15.refs_7_
  203.5 0.0 copy-done.4
  203.5 3.7 %shard_map.43 = f32[2048,1024]{1,0:T(8,128)} custom-call(s32[1]{0:T(128)} %bitcast.me_ref, f32[1024,1024]{1,0:T(8,128)S(1)} %bitcast.11, bf16[512,1024]{1,0:T(8,128)(2,1)S(1)} %bitcast.13, bf16[128,1024]{1,0:T(8,128)(2,1)S(1)} %get-tuple-element.62.refs_0_, bf16[128,1024]{1,0:T(8,128)(2,1)S(1)} %collective-permute-done.3.refs_1_, ...), custom_call_target="tpu_custom_call", output_to_operand_aliasing={{}: (11, {})} | custom-call | flops 2097152 | bytes 12582912 | tf_op jit(solution)/shard_map/pallas_call | solution.py:221
  (12 shorter events, 0.0 us)
Async XLA Ops:
  0.0 15.4 %copy-start.8 = (f32[1,8192]{1,0:T(1,128)S(1)}, f32[1,8192]{1,0:T(1,128)}, u32[]{:S(2)}) copy-start(f32[1,8192]{1,0:T(1,128)} %constant.9.row_ref) | copy-start | bytes 98308
  0.0 15.2 %copy-start.13 = (f32[128]{0:T(128)S(1)}, f32[128]{0:T(128)}, u32[]{:S(2)}) copy-start(f32[128]{0:T(128)} %param.4) | copy-start | bytes 1540
  3.2 51.1 %all-to-all-start = ((bf16[8,128,1024]{2,1,0:T(8,128)(2,1)}), bf16[8,128,1024]{2,1,0:T(8,128)(2,1)}, u32[]{:S(2)}, u32[]{:S(2)}) async-start(bf16[8,128,1024]{2,1,0:T(8,128)(2,1)} %bitcast.4), calls=%async_computation | async-start | bytes 4194304 | tf_op jit(solution)/shard_map/all_to_all | solution.py:267
  9.9 8.0 %collective-permute-start.1 = (bf16[4,4,4,1024]{3,2,1,0:T(4,128)(2,1)S(1)}, bf16[4,4,4,1024]{3,2,1,0:T(4,128)(2,1)S(1)}, u32[]{:S(2)}, u32[]{:S(2)}) collective-permute-start(bf16[4,4,4,1024]{3,2,1,0:T(4,128)(2,1)S(1)} %get-tuple-element.93), channel_id=1, source_target_pairs={{1,0},{2,1},{3,2},{5,4},{6,5},{7,6},{9,8},{10,9},{11,10},{13,12},{... | collective-permute-start | bytes 393224 | tf_op jit(solution)/shard_map/ppermute | solution.py:255
  11.2 6.7 %collective-permute-start = (bf16[4,4,4,1024]{3,2,1,0:T(4,128)(2,1)S(1)}, bf16[4,4,4,1024]{3,2,1,0:T(4,128)(2,1)S(1)}, u32[]{:S(2)}, u32[]{:S(2)}) collective-permute-start(bf16[4,4,4,1024]{3,2,1,0:T(4,128)(2,1)S(1)} %get-tuple-element.94), channel_id=1, source_target_pairs={{0,1},{1,2},{2,3},{4,5},{5,6},{6,7},{8,9},{9,10},{10,11},{12,13},{... | collective-permute-start | bytes 393224 | tf_op jit(solution)/shard_map/ppermute | solution.py:254
  17.9 13.3 %copy-start.5 = (bf16[128,9088]{1,0:T(8,128)(2,1)}, bf16[128,9088]{1,0:T(8,128)(2,1)S(1)}, u32[]{:S(2)}) copy-start(bf16[128,9088]{1,0:T(8,128)(2,1)S(1)} %get-tuple-element.50.low_ref) | copy-start | bytes 6979588
  18.0 3.0 %copy-start = (bf16[4,4,128,1024]{3,2,1,0:T(8,128)(2,1)S(1)}, bf16[4,4,128,1024]{3,2,1,0:T(8,128)(2,1)}, u32[]{:S(2)}) copy-start(bf16[4,4,128,1024]{3,2,1,0:T(8,128)(2,1)} %b_ref.3) | copy-start | bytes 12582916
  31.3 2.0 copy-start.3
  43.5 2.0 copy-start.1
  54.3 53.4 %all-to-all-start.1 = ((bf16[8,128,1024]{2,1,0:T(8,128)(2,1)}), bf16[8,128,1024]{2,1,0:T(8,128)(2,1)}, u32[]{:S(2)}, u32[]{:S(2)}) async-start(bf16[8,128,1024]{2,1,0:T(8,128)(2,1)} %bitcast.14), calls=%async_computation.1 | async-start | bytes 4194304 | tf_op jit(solution)/shard_map/all_to_all | solution.py:267
  62.2 1.7 copy-start.6
  97.0 0.7 copy-start.9
  97.7 0.7 copy-start.10
  98.4 0.7 copy-start.11
  99.1 0.7 copy-start.12
  107.7 42.1 %collective-permute-start.2 = (bf16[128,1024]{1,0:T(8,128)(2,1)}, bf16[128,1024]{1,0:T(8,128)(2,1)S(1)}, u32[]{:S(2)}, u32[]{:S(2)}) collective-permute-start(bf16[128,1024]{1,0:T(8,128)(2,1)} %copy-done.12), channel_id=1, source_target_pairs={{0,16},{4,20},{8,24},{12,28},{16,0},{20,4},{24,8},{28,12},{1,17},{... | collective-permute-start | bytes 786440 | tf_op jit(solution)/shard_map/ppermute | solution.py:270
  110.8 39.5 %collective-permute-start.4 = (bf16[128,1024]{1,0:T(8,128)(2,1)}, bf16[128,1024]{1,0:T(8,128)(2,1)S(1)}, u32[]{:S(2)}, u32[]{:S(2)}) collective-permute-start(bf16[128,1024]{1,0:T(8,128)(2,1)} %copy-done.11), channel_id=1, source_target_pairs={{0,20},{4,24},{8,28},{12,0},{16,4},{20,8},{24,12},{28,16},{1,21},{... | collective-permute-start | bytes 786440 | tf_op jit(solution)/shard_map/ppermute | solution.py:270
  111.4 40.3 %collective-permute-start.6 = (bf16[128,1024]{1,0:T(8,128)(2,1)}, bf16[128,1024]{1,0:T(8,128)(2,1)S(1)}, u32[]{:S(2)}, u32[]{:S(2)}) collective-permute-start(bf16[128,1024]{1,0:T(8,128)(2,1)} %copy-done.10), channel_id=1, source_target_pairs={{0,12},{4,16},{8,20},{12,24},{16,28},{20,0},{24,4},{28,8},{1,13},{... | collective-permute-start | bytes 786440 | tf_op jit(solution)/shard_map/ppermute | solution.py:270
  113.5 42.3 %collective-permute-start.8 = (bf16[128,1024]{1,0:T(8,128)(2,1)}, bf16[128,1024]{1,0:T(8,128)(2,1)S(1)}, u32[]{:S(2)}, u32[]{:S(2)}) collective-permute-start(bf16[128,1024]{1,0:T(8,128)(2,1)} %copy-done.9), channel_id=1, source_target_pairs={{0,24},{4,28},{8,0},{12,4},{16,8},{20,12},{24,16},{28,20},{1,25},{... | collective-permute-start | bytes 786440 | tf_op jit(solution)/shard_map/ppermute | solution.py:270
  114.0 41.8 %collective-permute-start.10 = (bf16[128,1024]{1,0:T(8,128)(2,1)S(1)}, bf16[128,1024]{1,0:T(8,128)(2,1)S(1)}, u32[]{:S(2)}, u32[]{:S(2)}) collective-permute-start(bf16[128,1024]{1,0:T(8,128)(2,1)S(1)} %get-tuple-element.76), channel_id=1, source_target_pairs={{0,8},{4,12},{8,16},{12,20},{16,24},{20,28},{24,0},{28,4},{1,9},{5... | collective-permute-start | bytes 786440 | tf_op jit(solution)/shard_map/ppermute | solution.py:270
  115.0 1.7 copy-start.7
  116.6 74.6 %copy-start.2 = (f32[2,4,128,1024]{3,2,1,0:T(8,128)S(1)}, f32[2,4,128,1024]{3,2,1,0:T(8,128)}, u32[]{:S(2)}) copy-start(f32[2,4,128,1024]{3,2,1,0:T(8,128)} %copy-done.1) | copy-start | bytes 12582916
  149.9 8.6 %collective-permute-start.12 = (bf16[128,1024]{1,0:T(8,128)(2,1)S(1)}, bf16[128,1024]{1,0:T(8,128)(2,1)S(1)}, u32[]{:S(2)}, u32[]{:S(2)}) collective-permute-start(bf16[128,1024]{1,0:T(8,128)(2,1)S(1)} %get-tuple-element.79), channel_id=1, source_target_pairs={{0,28},{4,0},{8,4},{12,8},{16,12},{20,16},{24,20},{28,24},{1,29},{... | collective-permute-start | bytes 786440 | tf_op jit(solution)/shard_map/ppermute | solution.py:270
  150.3 8.2 %collective-permute-start.14 = (bf16[128,1024]{1,0:T(8,128)(2,1)S(1)}, bf16[128,1024]{1,0:T(8,128)(2,1)S(1)}, u32[]{:S(2)}, u32[]{:S(2)}) collective-permute-start(bf16[128,1024]{1,0:T(8,128)(2,1)S(1)} %get-tuple-element.82), channel_id=1, source_target_pairs={{0,4},{4,8},{8,12},{12,16},{16,20},{20,24},{24,28},{28,0},{1,5},{5... | collective-permute-start | bytes 786440 | tf_op jit(solution)/shard_map/ppermute | solution.py:270
  151.7 31.8 %collective-permute-start.3 = (bf16[128,1024]{1,0:T(8,128)(2,1)S(1)}, bf16[128,1024]{1,0:T(8,128)(2,1)S(1)}, u32[]{:S(2)}, u32[]{:S(2)}) collective-permute-start(bf16[128,1024]{1,0:T(8,128)(2,1)S(1)} %get-tuple-element.65), channel_id=1, source_target_pairs={{0,16},{4,20},{8,24},{12,28},{16,0},{20,4},{24,8},{28,12},{1,17},{... | collective-permute-start | bytes 786440 | tf_op jit(solution)/shard_map/ppermute | solution.py:270
  155.8 27.6 %collective-permute-start.5 = (bf16[128,1024]{1,0:T(8,128)(2,1)S(1)}, bf16[128,1024]{1,0:T(8,128)(2,1)S(1)}, u32[]{:S(2)}, u32[]{:S(2)}) collective-permute-start(bf16[128,1024]{1,0:T(8,128)(2,1)S(1)} %get-tuple-element.68), channel_id=1, source_target_pairs={{0,20},{4,24},{8,28},{12,0},{16,4},{20,8},{24,12},{28,16},{1,21},{... | collective-permute-start | bytes 786440 | tf_op jit(solution)/shard_map/ppermute | solution.py:270
  155.8 39.3 %collective-permute-start.7 = (bf16[128,1024]{1,0:T(8,128)(2,1)S(1)}, bf16[128,1024]{1,0:T(8,128)(2,1)S(1)}, u32[]{:S(2)}, u32[]{:S(2)}) collective-permute-start(bf16[128,1024]{1,0:T(8,128)(2,1)S(1)} %get-tuple-element.71), channel_id=1, source_target_pairs={{0,12},{4,16},{8,20},{12,24},{16,28},{20,0},{24,4},{28,8},{1,13},{... | collective-permute-start | bytes 786440 | tf_op jit(solution)/shard_map/ppermute | solution.py:270
  158.5 44.2 %collective-permute-start.9 = (bf16[128,1024]{1,0:T(8,128)(2,1)S(1)}, bf16[128,1024]{1,0:T(8,128)(2,1)S(1)}, u32[]{:S(2)}, u32[]{:S(2)}) collective-permute-start(bf16[128,1024]{1,0:T(8,128)(2,1)S(1)} %get-tuple-element.74), channel_id=1, source_target_pairs={{0,24},{4,28},{8,0},{12,4},{16,8},{20,12},{24,16},{28,20},{1,25},{... | collective-permute-start | bytes 786440 | tf_op jit(solution)/shard_map/ppermute | solution.py:270
  158.5 44.2 %collective-permute-start.11 = (bf16[128,1024]{1,0:T(8,128)(2,1)S(1)}, bf16[128,1024]{1,0:T(8,128)(2,1)S(1)}, u32[]{:S(2)}, u32[]{:S(2)}) collective-permute-start(bf16[128,1024]{1,0:T(8,128)(2,1)S(1)} %get-tuple-element.77), channel_id=1, source_target_pairs={{0,8},{4,12},{8,16},{12,20},{16,24},{20,28},{24,0},{28,4},{1,9},{5... | collective-permute-start | bytes 786440 | tf_op jit(solution)/shard_map/ppermute | solution.py:270
  183.5 20.0 %collective-permute-start.13 = (bf16[128,1024]{1,0:T(8,128)(2,1)S(1)}, bf16[128,1024]{1,0:T(8,128)(2,1)S(1)}, u32[]{:S(2)}, u32[]{:S(2)}) collective-permute-start(bf16[128,1024]{1,0:T(8,128)(2,1)S(1)} %get-tuple-element.80), channel_id=1, source_target_pairs={{0,28},{4,0},{8,4},{12,8},{16,12},{20,16},{24,20},{28,24},{1,29},{... | collective-permute-start | bytes 786440 | tf_op jit(solution)/shard_map/ppermute | solution.py:270
  183.5 20.0 %collective-permute-start.15 = (bf16[128,1024]{1,0:T(8,128)(2,1)S(1)}, bf16[128,1024]{1,0:T(8,128)(2,1)S(1)}, u32[]{:S(2)}, u32[]{:S(2)}) collective-permute-start(bf16[128,1024]{1,0:T(8,128)(2,1)S(1)} %get-tuple-element.83), channel_id=1, source_target_pairs={{0,4},{4,8},{8,12},{12,16},{16,20},{20,24},{24,28},{28,0},{1,5},{5... | collective-permute-start | bytes 786440 | tf_op jit(solution)/shard_map/ppermute | solution.py:270
  191.3 12.2 %copy-start.4 = (f32[2,4,128,1024]{3,2,1,0:T(8,128)S(1)}, f32[2,4,128,1024]{3,2,1,0:T(8,128)}, u32[]{:S(2)}) copy-start(f32[2,4,128,1024]{3,2,1,0:T(8,128)} %copy-done.3) | copy-start | bytes 12582916

commit v4 on v3

--- a/solution.py
+++ b/solution.py
@@ -93,7 +93,7 @@
     return total.astype(BF16)
 
 
-def far_blocks_body(devices, me_ref, lines_ref, high_ref, low_ref, *refs):
+def far_whole_body(devices, me_ref, lines_ref, high_ref, low_ref, *refs):
     outs, all_ref = refs[:-1], refs[-1]
     rows, columns = outs[0].shape
     all_ref[...] = far_sum(
@@ -104,14 +104,14 @@
         outs[k][...] = all_ref[pl.ds(start, rows), :]
 
 
-def far_slopes(lines, high, low, me):
+def far_whole(lines, high, low, me):
     devices, rows, width = lines.shape
     total_rows = devices * rows
     columns = COLUMNS
     whole = pl.BlockSpec((total_rows, width), lambda j, m: (0, 0))
     strip = pl.BlockSpec(memory_space=pltpu.VMEM)
     return pl.pallas_call(
-        functools.partial(far_blocks_body, devices),
+        functools.partial(far_whole_body, devices),
         grid_spec=pltpu.PrefetchScalarGridSpec(
             num_scalar_prefetch=1,
             grid=(width // columns,),
@@ -127,6 +127,52 @@
             transcendentals=0,
         ),
     )(me, lines.reshape(total_rows, width), high, low)
+
+
+def far_body(devices, shifts, me_ref, *refs):
+    sources = dict(zip([0] + shifts, refs[:devices]))
+    high_ref, low_ref, outs = refs[devices], refs[devices + 1], refs[devices + 2 :]
+    rows, width = sources[0].shape
+    columns = outs[0].shape[1]
+    column = pl.program_id(0) * columns
+    total = None
+    for step in range(1, devices):
+        moved = jnp.concatenate(
+            [sources[(step + target) % devices][...] for target in range(devices)], axis=0
+        )
+        first = step * width + column
+        for strip_ref in (high_ref, low_ref):
+            part = dot(moved, panel(strip_ref, first, width, columns))
+            total = part if total is None else total + part
+    for target in range(devices):
+        outs[target][...] = total[target * rows : (target + 1) * rows, :].astype(BF16)
+
+
+def far_slopes(flat, chunk, received, high, low, me):
+    devices = len(received) + 1
+    shifts = list(received)
+    rows, width = received[1].shape
+    columns = COLUMNS
+    whole = pl.BlockSpec((rows, width), lambda j, m: (0, 0))
+    strip = pl.BlockSpec(memory_space=pltpu.VMEM)
+    return pl.pallas_call(
+        functools.partial(far_body, devices, shifts),
+        grid_spec=pltpu.PrefetchScalarGridSpec(
+            num_scalar_prefetch=1,
+            grid=(width // columns,),
+            in_specs=[pl.BlockSpec((rows, width), lambda j, m: (chunk * devices + m[0], 0))]
+            + [whole] * (devices - 1)
+            + [strip] * 2,
+            out_specs=[pl.BlockSpec((rows, columns), lambda j, m: (0, j))] * devices,
+        ),
+        out_shape=[jax.ShapeDtypeStruct((rows, width), BF16)] * devices,
+        compiler_params=pltpu.CompilerParams(vmem_limit_bytes=20 * 2**20),
+        cost_estimate=pl.CostEstimate(
+            flops=4 * rows * devices * (devices - 1) * width * width,
+            bytes_accessed=4 * rows * devices * width + 4 * high.size,
+            transcendentals=0,
+        ),
+    )(me, flat, *received.values(), high, low)
 
 
 def local_body(base, field_ref, u_ref, w_ref, b_ref, below_ref, above_ref, strat_ref, high_ref, low_ref, out_ref, pad_ref):
@@ -256,44 +302,51 @@
     return below, above
 
 
+def after(value, *others):
+    return lax.optimization_barrier((value, others))[0]
+
+
 def body(fields, strat_sq):
     comps, lines, levels, width = fields.shape
     devices = lax.axis_size("gx")
     group = comps // 2
-    shape = (devices, group * lines * levels // devices, width)
-    me = lax.axis_index("gx").astype(jnp.int32)[None]
-
-    def exchange(whole):
-        return lax.all_to_all(whole, "gx", split_axis=0, concat_axis=0, tiled=True)
+    held = group * lines * levels
+    rows = held // devices
+    index = lax.axis_index("gx").astype(jnp.int32)
+    me = index[None]
+    flat = fields.reshape(2 * held, width)
+    order = order_of(devices)
+    shifts = range(1, devices)
 
     def ahead(block, k):
         return lax.ppermute(block, "gx", [(i, (i + k) % devices) for i in range(devices)])
 
-    first = exchange(fields[:group].reshape(shape))
+    def block_of(source, chunk, k):
+        start = (chunk * devices + (index + k) % devices) * rows
+        return lax.dynamic_slice_in_dim(source, start, rows, 0)
+
+    first = lax.all_to_all(
+        flat[:held].reshape(devices, rows, width), "gx", split_axis=0, concat_axis=0, tiled=True
+    )
     below, above = halos(fields)
     high, low = strips(devices * width, width)
     local = (fields, below, above, strat_sq[:, None], high, low)
     early = local_part(*local, 0, group, group)
     part = local_part(*local, group, group, group)
-    source, early, part = lax.optimization_barrier((fields, early, part))
-    speed_u = source[0].reshape(lines * levels, width)
-    second = exchange(source[group:].reshape(shape))
-    order = order_of(devices)
-    held = group * lines * levels
-
-    def back(outs, k):
-        return ahead(outs[k], devices - k)
-
-    outs, second = lax.optimization_barrier((far_slopes(first, high, low, me), second))
-    fars = [outs[0]] + [back(outs, k) for k in order]
-    later = list(far_slopes(second, high, low, me))
-    last = [later[0]]
-    for i, k in enumerate(order):
-        later[k], fars[1 + i] = lax.optimization_barrier((later[k], fars[1 + i]))
-        last.append(back(later, k))
-    shape_flat = (held, width)
-    out = finish(None, early.reshape(shape_flat), speed_u, [0] + order, fars, me, 2 * held)
-    out = finish(out, part.reshape(shape_flat), speed_u, [0] + order, last, me, 2 * held)
+    source, early, part, first = lax.optimization_barrier((flat, early, part, first))
+    speed_u = source[: lines * levels]
+    second = {k: ahead(block_of(source, 1, k), k) for k in order}
+    outs = far_whole(first, high, low, me)
+    outs, blocks = lax.optimization_barrier((outs, list(second.values())))
+    second = dict(zip(second, blocks))
+    later = far_slopes(flat, 1, second, high, low, me)
+    back = {k: ahead(outs[k], devices - k) for k in shifts}
+    last = {k: ahead(after(later[k], back[k]), devices - k) for k in shifts}
+    offsets = [0] + order
+    fars = [outs[0]] + [back[k] for k in order]
+    out = finish(None, early.reshape(held, width), speed_u, offsets, fars, me, 2 * held)
+    fars = [later[0]] + [last[k] for k in order]
+    out = finish(out, part.reshape(held, width), speed_u, offsets, fars, me, 2 * held)
     return out.reshape(fields.shape)
 
 

time: 208 us -> 201 us (0.966)
  starting transfers between devices: 43.1 us -> 50.8 us
  waiting for transfers between devices: 46.7 us -> 39.8 us
  local copies, waits for them, and re-layouts: 20.3 us -> 14.7 us
    ppermute x14 -> x21, starting transfers between devices: 24.3 us -> 39.9 us  [ahead(): lax.ppermute(block, 'gx', [(i, (i + k) % devices) for i in range(devices)])]
    all_to_all x2 -> x1, starting transfers between devices: 13.6 us -> 5.64 us  [body(): lax.all_to_all(flat[:held].reshape(devices, rows, width), 'gx', split_axi...]
    all_to_all x2 -> x1, waiting for transfers between devices: 15.3 us -> 8.68 us  [body(): lax.all_to_all(flat[:held].reshape(devices, rows, width), 'gx', split_axi...]
    unnamed x28 -> x22, local copies, waits for them, and re-layouts: 13.1 us -> 8.67 us
    slice x3 -> x2, local copies, waits for them, and re-layouts: 5.94 us -> 3.17 us  [the longest x1 3.1 us: body(): flat[:held].reshape(devices, rows, width)]
    ppermute x14 -> x21, waiting for transfers between devices: 31.4 us -> 31.2 us  [ahead(): lax.ppermute(block, 'gx', [(i, (i + k) % devices) for i in range(devices)])]
  transfers between devices with their start and end apart: 18 -> 24, of which waited for: 5 -> 7; matrix products, arithmetic and copies ran while one was open for 2% -> 1% of each run, Pallas kernels for 45% -> 45%
where the time goes in v4:
time: 201 us
  Pallas kernels  95.1 us (47%)
  starting transfers between devices  50.8 us (25%)
  waiting for transfers between devices  39.8 us (20%)
  local copies, waits for them, and re-layouts  14.7 us (7%)
    ppermute x21, starting transfers between devices, ahead(): lax.ppermute(block, 'gx', [(i, (i + k) % devices) for i in range(devices)])  39.9 us
    pallas_call x1, Pallas kernels, far_whole(): pl.pallas_call(functools.partial(far_whole_body, devices), grid_spec=pltp...  33.2 us
    pallas_call x1, Pallas kernels, far_slopes(): pl.pallas_call(functools.partial(far_body, devices, shifts), grid_spec=pl...  31.2 us
    ppermute x21, waiting for transfers between devices, ahead(): lax.ppermute(block, 'gx', [(i, (i + k) % devices) for i in range(devices)])  31.2 us
    pallas_call x2, Pallas kernels, local_part(): pl.pallas_call(functools.partial(local_body, base), grid=(lines, count),...  20.5 us
    all_to_all x1, waiting for transfers between devices, body(): lax.all_to_all(flat[:held].reshape(devices, rows, width), 'gx', split_axi...  8.68 us
    unnamed x22, local copies, waits for them, and re-layouts  8.67 us
    pallas_call x2, Pallas kernels, finish(): pl.pallas_call(functools.partial(finish_body, devices), grid_spec=pltpu.P...  7.57 us
  transfers between devices with their start and end apart: 24, of which 7 were waited for; matrix products, arithmetic and copies ran while one was open for 1% of the time, Pallas kernels for 45%

profile of v4, /device:TPU:9, one launch (start us, length us, event | category | flops | bytes accessed | tf_op | source)
XLA Modules:
  0.0 200.9 jit_solution(11399297071881711345)
XLA Ops:
  0.0 3.1 %slice.15 = bf16[2,4,128,1024]{3,2,1,0:T(8,128)(2,1)} slice(bf16[4,4,128,1024]{3,2,1,0:T(8,128)(2,1)} %b_ref.3), slice={[0:2], [0:4], [0:128], [0:1024]} | slice | bytes 4194304 | tf_op jit(solution)/shard_map/slice | solution.py:329
  3.1 5.6 %all-to-all-start = ((bf16[8,128,1024]{2,1,0:T(8,128)(2,1)}), bf16[8,128,1024]{2,1,0:T(8,128)(2,1)}, u32[]{:S(2)}, u32[]{:S(2)}) async-start(bf16[8,128,1024]{2,1,0:T(8,128)(2,1)} %bitcast.3), calls=%async_computation | async-start | bytes 4194304 | tf_op jit(solution)/shard_map/all_to_all | solution.py:328
  8.7 1.1 fusion
  9.9 1.3 collective-permute-start.1
  11.2 4.0 %collective-permute-start = (bf16[4,4,4,1024]{3,2,1,0:T(4,128)(2,1)S(1)}, bf16[4,4,4,1024]{3,2,1,0:T(4,128)(2,1)S(1)}, u32[]{:S(2)}, u32[]{:S(2)}) collective-permute-start(bf16[4,4,4,1024]{3,2,1,0:T(4,128)(2,1)S(1)} %get-tuple-element.101), channel_id=1, source_target_pairs={{0,1},{1,2},{2,3},{4,5},{5,6},{6,7},{8,9},{9,10},{10,11},{12,13},{... | collective-permute-start | bytes 393224 | tf_op jit(solution)/shard_map/ppermute | solution.py:300
  15.3 0.1 copy.5.strat_ref
  15.4 2.6 %shard_map.37 = (bf16[128,9088]{1,0:T(8,128)(2,1)S(1)}, bf16[128,9088]{1,0:T(8,128)(2,1)S(1)}) custom-call(f32[1,8192]{1,0:T(1,128)S(1)} %copy-done.9), custom_call_target="tpu_custom_call" | custom-call | flops 4194304 | bytes 4194304 | tf_op jit(solution)/shard_map/pallas_call | solution.py:56
  18.0 0.0 collective-permute-done.1.above_ref
  18.0 0.0 collective-permute-done.below_ref
  18.0 0.0 copy-start
  18.1 3.0 %copy-done = bf16[4,4,128,1024]{3,2,1,0:T(8,128)(2,1)S(1)} copy-done((bf16[4,4,128,1024]{3,2,1,0:T(8,128)(2,1)S(1)}, bf16[4,4,128,1024]{3,2,1,0:T(8,128)(2,1)}, u32[]{:S(2)}) %copy-start) | copy-done | bytes 4194328
  21.1 10.2 %shard_map.39 = f32[2,4,128,1024]{3,2,1,0:T(8,128)S(1)} custom-call(bf16[4,4,128,1024]{3,2,1,0:T(8,128)(2,1)S(1)} %copy-done, bf16[4,4,128,1024]{3,2,1,0:T(8,128)(2,1)S(1)} %copy-done, bf16[4,4,128,1024]{3,2,1,0:T(8,128)(2,1)S(1)} %copy-done, bf16[4,4,128,1024]{3,2,1,0:T(8,128)(2,1)S(1)} %copy-done, ...), custom_call_target="tpu_custom_call" | custom-call | flops 4294967296 | bytes 8388608 | tf_op jit(solution)/shard_map/pallas_call | solution.py:219
  31.3 2.0 copy-done.4
  33.3 10.2 %shard_map.38 = f32[2,4,128,1024]{3,2,1,0:T(8,128)S(1)} custom-call(bf16[4,4,128,1024]{3,2,1,0:T(8,128)(2,1)S(1)} %copy-done, bf16[4,4,128,1024]{3,2,1,0:T(8,128)(2,1)S(1)} %copy-done, bf16[4,4,128,1024]{3,2,1,0:T(8,128)(2,1)S(1)} %copy-done, bf16[4,4,128,1024]{3,2,1,0:T(8,128)(2,1)S(1)} %copy-done, ...), custom_call_target="tpu_custom_call" | custom-call | flops 4294967296 | bytes 8388608 | tf_op jit(solution)/shard_map/pallas_call | solution.py:219
  43.6 0.0 copy-start.2
  43.6 2.0 copy-done.2
  45.6 8.7 %all-to-all-done = bf16[8,128,1024]{2,1,0:T(8,128)(2,1)} async-done(((bf16[8,128,1024]{2,1,0:T(8,128)(2,1)}), bf16[8,128,1024]{2,1,0:T(8,128)(2,1)}, u32[]{:S(2)}, u32[]{:S(2)}) %all-to-all-start) | async-done | bytes 2097184 | tf_op jit(solution)/shard_map/all_to_all | solution.py:328
  54.3 1.6 constant_dynamic-slice_fusion
  55.9 0.5 collective-permute-start.8
  56.3 1.3 collective-permute-start.7
  57.7 2.8 %collective-permute-start.6 = (bf16[128,1024]{1,0:T(8,128)(2,1)S(1)}, bf16[128,1024]{1,0:T(8,128)(2,1)S(1)}, u32[]{:S(2)}, u32[]{:S(2)}) collective-permute-start(bf16[128,1024]{1,0:T(8,128)(2,1)S(1)} %get-tuple-element.95), channel_id=1, source_target_pairs={{0,24},{4,28},{8,0},{12,4},{16,8},{20,12},{24,16},{28,20},{1,25},{... | collective-permute-start | bytes 786440 | tf_op jit(solution)/shard_map/ppermute | solution.py:322
  60.5 0.0 collective-permute-start.5
  60.5 2.0 collective-permute-start.4
  62.5 0.6 collective-permute-done.8.refs_7_
  63.1 0.6 collective-permute-start.3
  63.7 0.0 collective-permute-done.7.refs_6_
  63.7 5.9 %collective-permute-start.2 = (bf16[128,1024]{1,0:T(8,128)(2,1)S(1)}, bf16[128,1024]{1,0:T(8,128)(2,1)S(1)}, u32[]{:S(2)}, u32[]{:S(2)}) collective-permute-start(bf16[128,1024]{1,0:T(8,128)(2,1)S(1)} %get-tuple-element.99), channel_id=1, source_target_pairs={{0,16},{4,20},{8,24},{12,28},{16,0},{20,4},{24,8},{28,12},{1,17},{... | collective-permute-start | bytes 786440 | tf_op jit(solution)/shard_map/ppermute | solution.py:322
  69.6 1.7 copy-done.7
  71.2 33.2 %shard_map.40 = (bf16[128,1024]{1,0:T(8,128)(2,1)S(1)}, bf16[128,1024]{1,0:T(8,128)(2,1)S(1)}, bf16[128,1024]{1,0:T(8,128)(2,1)S(1)}, bf16[128,1024]{1,0:T(8,128...) custom-call(s32[1]{0:T(128)} %bitcast.me_ref, ...), custom_call_target="tpu_custom_call" | custom-call | flops 30064771072 | bytes 8847360 | tf_op jit(solution)/shard_map/pallas_call | solution.py:113
  104.5 0.0 collective-permute-done.6.refs_5_
  104.5 0.0 collective-permute-done.5.refs_4_
  104.5 0.0 collective-permute-done.4.refs_3_
  104.5 0.0 collective-permute-done.3.refs_2_
  104.5 0.0 collective-permute-done.2.refs_1_
  104.5 0.1 collective-permute-start.9
  104.6 4.4 %collective-permute-start.11 = (bf16[128,1024]{1,0:T(8,128)(2,1)S(1)}, bf16[128,1024]{1,0:T(8,128)(2,1)S(1)}, u32[]{:S(2)}, u32[]{:S(2)}) collective-permute-start(bf16[128,1024]{1,0:T(8,128)(2,1)S(1)} %get-tuple-element.74), channel_id=1, source_target_pairs={{0,20},{4,24},{8,28},{12,0},{16,4},{20,8},{24,12},{28,16},{1,21},{... | collective-permute-start | bytes 786440 | tf_op jit(solution)/shard_map/ppermute | solution.py:322
  109.0 0.0 collective-permute-start.13
  109.0 0.4 collective-permute-start.15
  109.4 1.1 collective-permute-start.17
  110.5 31.2 %shard_map.41 = (bf16[128,1024]{1,0:T(8,128)(2,1)S(1)}, bf16[128,1024]{1,0:T(8,128)(2,1)S(1)}, bf16[128,1024]{1,0:T(8,128)(2,1)S(1)}, bf16[128,1024]{1,0:T(8,128...) custom-call(s32[1]{0:T(128)} %bitcast.me_ref, ...), custom_call_target="tpu_custom_call" | custom-call | flops 30064771072 | bytes 8847360 | tf_op jit(solution)/shard_map/pallas_call | solution.py:158
  141.7 0.0 collective-permute-done.9.refs_1_
  141.8 0.8 collective-permute-start.19
  142.5 0.0 collective-permute-done.11.refs_2_
  142.5 1.2 collective-permute-start.21
  143.7 0.0 collective-permute-done.13.refs_3_
  143.7 4.0 %collective-permute-start.10 = (bf16[128,1024]{1,0:T(8,128)(2,1)S(1)}, bf16[128,1024]{1,0:T(8,128)(2,1)S(1)}, u32[]{:S(2)}, u32[]{:S(2)}) collective-permute-start(bf16[128,1024]{1,0:T(8,128)(2,1)S(1)} %get-tuple-element.72), channel_id=1, source_target_pairs={{0,16},{4,20},{8,24},{12,28},{16,0},{20,4},{24,8},{28,12},{1,17},{... | collective-permute-start | bytes 786440 | tf_op jit(solution)/shard_map/ppermute | solution.py:322
  147.7 0.6 collective-permute-done.15.refs_4_
  148.3 0.0 collective-permute-start.12
  148.3 0.0 collective-permute-done.17.refs_5_
  148.3 2.6 %collective-permute-start.14 = (bf16[128,1024]{1,0:T(8,128)(2,1)S(1)}, bf16[128,1024]{1,0:T(8,128)(2,1)S(1)}, u32[]{:S(2)}, u32[]{:S(2)}) collective-permute-start(bf16[128,1024]{1,0:T(8,128)(2,1)S(1)} %get-tuple-element.78), channel_id=1, source_target_pairs={{0,12},{4,16},{8,20},{12,24},{16,28},{20,0},{24,4},{28,8},{1,13},{... | collective-permute-start | bytes 786440 | tf_op jit(solution)/shard_map/ppermute | solution.py:322
  151.0 1.1 collective-permute-done.19.refs_6_
  152.0 0.0 collective-permute-start.16
  152.0 0.0 collective-permute-done.21.refs_7_
  152.1 3.5 %collective-permute-start.18 = (bf16[128,1024]{1,0:T(8,128)(2,1)S(1)}, bf16[128,1024]{1,0:T(8,128)(2,1)S(1)}, u32[]{:S(2)}, u32[]{:S(2)}) collective-permute-start(bf16[128,1024]{1,0:T(8,128)(2,1)S(1)} %get-tuple-element.84), channel_id=1, source_target_pairs={{0,8},{4,12},{8,16},{12,20},{16,24},{20,28},{24,0},{28,4},{1,9},{5... | collective-permute-start | bytes 786440 | tf_op jit(solution)/shard_map/ppermute | solution.py:322
  155.6 19.6 %collective-permute-done.10.refs_1_ = bf16[128,1024]{1,0:T(8,128)(2,1)S(1)} collective-permute-done((bf16[128,1024]{1,0:T(8,128)(2,1)S(1)}, bf16[128,1024]{1,0:T(8,128)(2,1)S(1)}, u32[]{:S(2)}, u32[]{:S(2)}) %collective-permute-start.10) | collective-permute-done | bytes 262176 | tf_op jit(solution)/shard_map/ppermute | solution.py:322
  175.2 0.8 collective-permute-start.20
  175.9 0.0 collective-permute-done.12.refs_2_
  175.9 8.0 %collective-permute-start.22 = (bf16[128,1024]{1,0:T(8,128)(2,1)S(1)}, bf16[128,1024]{1,0:T(8,128)(2,1)S(1)}, u32[]{:S(2)}, u32[]{:S(2)}) collective-permute-start(bf16[128,1024]{1,0:T(8,128)(2,1)S(1)} %get-tuple-element.90), channel_id=1, source_target_pairs={{0,4},{4,8},{8,12},{12,16},{16,20},{20,24},{24,28},{28,0},{1,5},{5... | collective-permute-start | bytes 786440 | tf_op jit(solution)/shard_map/ppermute | solution.py:322
  183.9 0.1 slice.16.u_ref
  184.0 3.8 %shard_map.42.refs_8_ = f32[2048,1024]{1,0:T(8,128)} custom-call(s32[1]{0:T(128)} %bitcast.me_ref, f32[1024,1024]{1,0:T(8,128)S(1)} %bitcast.11, bf16[512,1024]{1,0:T(8,128)(2,1)S(1)} %slice.16.u_ref, bf16[128,1024]{1,0:T(8,128)(2,1)S(1)} %get-tuple-element.92.refs_0_, bf16[128,1024]{1,0:T(8,128)(2,1)S(1)} %collective-permute-done.9.refs_1_, ...), custom_call_target="tpu_custom_call" | custom-call | flops 2097152 | bytes 12582912 | tf_op jit(solution)/shard_map/pallas_call | solution.py:267
  187.8 0.0 collective-permute-done.14.refs_3_
  187.8 8.3 %collective-permute-done.16.refs_4_ = bf16[128,1024]{1,0:T(8,128)(2,1)S(1)} collective-permute-done((bf16[128,1024]{1,0:T(8,128)(2,1)S(1)}, bf16[128,1024]{1,0:T(8,128)(2,1)S(1)}, u32[]{:S(2)}, u32[]{:S(2)}) %collective-permute-start.16) | collective-permute-done | bytes 262176 | tf_op jit(solution)/shard_map/ppermute | solution.py:322
  196.1 1.0 collective-permute-done.20.refs_6_
  197.1 3.8 %shard_map.43 = f32[2048,1024]{1,0:T(8,128)} custom-call(s32[1]{0:T(128)} %bitcast.me_ref, f32[1024,1024]{1,0:T(8,128)S(1)} %bitcast.12, bf16[512,1024]{1,0:T(8,128)(2,1)S(1)} %slice.16.u_ref, bf16[128,1024]{1,0:T(8,128)(2,1)S(1)} %get-tuple-element.69.refs_0_, ...), custom_call_target="tpu_custom_call", output_to_operand_aliasing={{}: (11, {})} | custom-call | flops 2097152 | bytes 12582912 | tf_op jit(solution)/shard_map/pallas_call | solution.py:267
  (18 shorter events, 0.0 us)
Async XLA Ops:
  0.0 15.4 %copy-start.9 = (f32[1,8192]{1,0:T(1,128)S(1)}, f32[1,8192]{1,0:T(1,128)}, u32[]{:S(2)}) copy-start(f32[1,8192]{1,0:T(1,128)} %constant.64.row_ref) | copy-start | bytes 98308
  0.0 15.3 %copy-start.10 = (f32[128]{0:T(128)S(1)}, f32[128]{0:T(128)}, u32[]{:S(2)}) copy-start(f32[128]{0:T(128)} %param.4) | copy-start | bytes 1540
  3.1 51.1 %all-to-all-start = ((bf16[8,128,1024]{2,1,0:T(8,128)(2,1)}), bf16[8,128,1024]{2,1,0:T(8,128)(2,1)}, u32[]{:S(2)}, u32[]{:S(2)}) async-start(bf16[8,128,1024]{2,1,0:T(8,128)(2,1)} %bitcast.3), calls=%async_computation | async-start | bytes 4194304 | tf_op jit(solution)/shard_map/all_to_all | solution.py:328
  9.9 8.1 %collective-permute-start.1 = (bf16[4,4,4,1024]{3,2,1,0:T(4,128)(2,1)S(1)}, bf16[4,4,4,1024]{3,2,1,0:T(4,128)(2,1)S(1)}, u32[]{:S(2)}, u32[]{:S(2)}) collective-permute-start(bf16[4,4,4,1024]{3,2,1,0:T(4,128)(2,1)S(1)} %get-tuple-element.100), channel_id=1, source_target_pairs={{1,0},{2,1},{3,2},{5,4},{6,5},{7,6},{9,8},{10,9},{11,10},{13,12},{... | collective-permute-start | bytes 393224 | tf_op jit(solution)/shard_map/ppermute | solution.py:301
  11.2 6.9 %collective-permute-start = (bf16[4,4,4,1024]{3,2,1,0:T(4,128)(2,1)S(1)}, bf16[4,4,4,1024]{3,2,1,0:T(4,128)(2,1)S(1)}, u32[]{:S(2)}, u32[]{:S(2)}) collective-permute-start(bf16[4,4,4,1024]{3,2,1,0:T(4,128)(2,1)S(1)} %get-tuple-element.101), channel_id=1, source_target_pairs={{0,1},{1,2},{2,3},{4,5},{5,6},{6,7},{8,9},{9,10},{10,11},{12,13},{... | collective-permute-start | bytes 393224 | tf_op jit(solution)/shard_map/ppermute | solution.py:300
  18.0 13.3 %copy-start.6 = (bf16[128,9088]{1,0:T(8,128)(2,1)}, bf16[128,9088]{1,0:T(8,128)(2,1)S(1)}, u32[]{:S(2)}) copy-start(bf16[128,9088]{1,0:T(8,128)(2,1)S(1)} %get-tuple-element.50.low_ref.refs_9_) | copy-start | bytes 6979588
  18.0 3.0 %copy-start = (bf16[4,4,128,1024]{3,2,1,0:T(8,128)(2,1)S(1)}, bf16[4,4,128,1024]{3,2,1,0:T(8,128)(2,1)}, u32[]{:S(2)}) copy-start(bf16[4,4,128,1024]{3,2,1,0:T(8,128)(2,1)} %b_ref.3) | copy-start | bytes 12582916
  31.3 2.0 copy-start.4
  43.6 2.0 %copy-start.2 = (f32[2,4,128,1024]{3,2,1,0:T(8,128)}, f32[2,4,128,1024]{3,2,1,0:T(8,128)S(1)}, u32[]{:S(2)}) copy-start(f32[2,4,128,1024]{3,2,1,0:T(8,128)S(1)} %shard_map.38) | copy-start | bytes 12582916
  55.9 7.2 %collective-permute-start.8 = (bf16[128,1024]{1,0:T(8,128)(2,1)S(1)}, bf16[128,1024]{1,0:T(8,128)(2,1)S(1)}, u32[]{:S(2)}, u32[]{:S(2)}) collective-permute-start(bf16[128,1024]{1,0:T(8,128)(2,1)S(1)} %get-tuple-element.93), channel_id=1, source_target_pairs={{0,28},{4,0},{8,4},{12,8},{16,12},{20,16},{24,20},{28,24},{1,29},{... | collective-permute-start | bytes 786440 | tf_op jit(solution)/shard_map/ppermute | solution.py:322
  56.3 7.3 %collective-permute-start.7 = (bf16[128,1024]{1,0:T(8,128)(2,1)S(1)}, bf16[128,1024]{1,0:T(8,128)(2,1)S(1)}, u32[]{:S(2)}, u32[]{:S(2)}) collective-permute-start(bf16[128,1024]{1,0:T(8,128)(2,1)S(1)} %get-tuple-element.94), channel_id=1, source_target_pairs={{0,4},{4,8},{8,12},{12,16},{16,20},{20,24},{24,28},{28,0},{1,5},{5... | collective-permute-start | bytes 786440 | tf_op jit(solution)/shard_map/ppermute | solution.py:322
  57.7 46.8 %collective-permute-start.6 = (bf16[128,1024]{1,0:T(8,128)(2,1)S(1)}, bf16[128,1024]{1,0:T(8,128)(2,1)S(1)}, u32[]{:S(2)}, u32[]{:S(2)}) collective-permute-start(bf16[128,1024]{1,0:T(8,128)(2,1)S(1)} %get-tuple-element.95), channel_id=1, source_target_pairs={{0,24},{4,28},{8,0},{12,4},{16,8},{20,12},{24,16},{28,20},{1,25},{... | collective-permute-start | bytes 786440 | tf_op jit(solution)/shard_map/ppermute | solution.py:322
  60.5 44.0 %collective-permute-start.5 = (bf16[128,1024]{1,0:T(8,128)(2,1)S(1)}, bf16[128,1024]{1,0:T(8,128)(2,1)S(1)}, u32[]{:S(2)}, u32[]{:S(2)}) collective-permute-start(bf16[128,1024]{1,0:T(8,128)(2,1)S(1)} %get-tuple-element.96), channel_id=1, source_target_pairs={{0,8},{4,12},{8,16},{12,20},{16,24},{20,28},{24,0},{28,4},{1,9},{5... | collective-permute-start | bytes 786440 | tf_op jit(solution)/shard_map/ppermute | solution.py:322
  60.5 44.0 %collective-permute-start.4 = (bf16[128,1024]{1,0:T(8,128)(2,1)S(1)}, bf16[128,1024]{1,0:T(8,128)(2,1)S(1)}, u32[]{:S(2)}, u32[]{:S(2)}) collective-permute-start(bf16[128,1024]{1,0:T(8,128)(2,1)S(1)} %get-tuple-element.97), channel_id=1, source_target_pairs={{0,20},{4,24},{8,28},{12,0},{16,4},{20,8},{24,12},{28,16},{1,21},{... | collective-permute-start | bytes 786440 | tf_op jit(solution)/shard_map/ppermute | solution.py:322
  63.1 41.4 %collective-permute-start.3 = (bf16[128,1024]{1,0:T(8,128)(2,1)S(1)}, bf16[128,1024]{1,0:T(8,128)(2,1)S(1)}, u32[]{:S(2)}, u32[]{:S(2)}) collective-permute-start(bf16[128,1024]{1,0:T(8,128)(2,1)S(1)} %get-tuple-element.98), channel_id=1, source_target_pairs={{0,12},{4,16},{8,20},{12,24},{16,28},{20,0},{24,4},{28,8},{1,13},{... | collective-permute-start | bytes 786440 | tf_op jit(solution)/shard_map/ppermute | solution.py:322
  63.7 40.8 %collective-permute-start.2 = (bf16[128,1024]{1,0:T(8,128)(2,1)S(1)}, bf16[128,1024]{1,0:T(8,128)(2,1)S(1)}, u32[]{:S(2)}, u32[]{:S(2)}) collective-permute-start(bf16[128,1024]{1,0:T(8,128)(2,1)S(1)} %get-tuple-element.99), channel_id=1, source_target_pairs={{0,16},{4,20},{8,24},{12,28},{16,0},{20,4},{24,8},{28,12},{1,17},{... | collective-permute-start | bytes 786440 | tf_op jit(solution)/shard_map/ppermute | solution.py:322
  69.6 1.7 copy-start.7
  71.2 39.3 %copy-start.1 = (bf16[4,4,128,1024]{3,2,1,0:T(8,128)(2,1)S(1)}, bf16[4,4,128,1024]{3,2,1,0:T(8,128)(2,1)}, u32[]{:S(2)}) copy-start(bf16[4,4,128,1024]{3,2,1,0:T(8,128)(2,1)} %b_ref.3) | copy-start | bytes 12582916
  71.2 39.3 %copy-start.8 = (bf16[128,9088]{1,0:T(8,128)(2,1)S(1)}, bf16[128,9088]{1,0:T(8,128)(2,1)}, u32[]{:S(2)}) copy-start(bf16[128,9088]{1,0:T(8,128)(2,1)} %copy-done.6) | copy-start | bytes 6979588
  104.5 37.2 %collective-permute-start.9 = (bf16[128,1024]{1,0:T(8,128)(2,1)S(1)}, bf16[128,1024]{1,0:T(8,128)(2,1)S(1)}, u32[]{:S(2)}, u32[]{:S(2)}) collective-permute-start(bf16[128,1024]{1,0:T(8,128)(2,1)S(1)} %get-tuple-element.71), channel_id=1, source_target_pairs={{0,16},{4,20},{8,24},{12,28},{16,0},{20,4},{24,8},{28,12},{1,17},{... | collective-permute-start | bytes 786440 | tf_op jit(solution)/shard_map/ppermute | solution.py:322
  104.6 37.9 %collective-permute-start.11 = (bf16[128,1024]{1,0:T(8,128)(2,1)S(1)}, bf16[128,1024]{1,0:T(8,128)(2,1)S(1)}, u32[]{:S(2)}, u32[]{:S(2)}) collective-permute-start(bf16[128,1024]{1,0:T(8,128)(2,1)S(1)} %get-tuple-element.74), channel_id=1, source_target_pairs={{0,20},{4,24},{8,28},{12,0},{16,4},{20,8},{24,12},{28,16},{1,21},{... | collective-permute-start | bytes 786440 | tf_op jit(solution)/shard_map/ppermute | solution.py:322
  109.0 34.7 %collective-permute-start.13 = (bf16[128,1024]{1,0:T(8,128)(2,1)S(1)}, bf16[128,1024]{1,0:T(8,128)(2,1)S(1)}, u32[]{:S(2)}, u32[]{:S(2)}) collective-permute-start(bf16[128,1024]{1,0:T(8,128)(2,1)S(1)} %get-tuple-element.77), channel_id=1, source_target_pairs={{0,12},{4,16},{8,20},{12,24},{16,28},{20,0},{24,4},{28,8},{1,13},{... | collective-permute-start | bytes 786440 | tf_op jit(solution)/shard_map/ppermute | solution.py:322
  109.0 39.3 %collective-permute-start.15 = (bf16[128,1024]{1,0:T(8,128)(2,1)S(1)}, bf16[128,1024]{1,0:T(8,128)(2,1)S(1)}, u32[]{:S(2)}, u32[]{:S(2)}) collective-permute-start(bf16[128,1024]{1,0:T(8,128)(2,1)S(1)} %get-tuple-element.80), channel_id=1, source_target_pairs={{0,24},{4,28},{8,0},{12,4},{16,8},{20,12},{24,16},{28,20},{1,25},{... | collective-permute-start | bytes 786440 | tf_op jit(solution)/shard_map/ppermute | solution.py:322
  109.4 38.9 %collective-permute-start.17 = (bf16[128,1024]{1,0:T(8,128)(2,1)S(1)}, bf16[128,1024]{1,0:T(8,128)(2,1)S(1)}, u32[]{:S(2)}, u32[]{:S(2)}) collective-permute-start(bf16[128,1024]{1,0:T(8,128)(2,1)S(1)} %get-tuple-element.83), channel_id=1, source_target_pairs={{0,8},{4,12},{8,16},{12,20},{16,24},{20,28},{24,0},{28,4},{1,9},{5... | collective-permute-start | bytes 786440 | tf_op jit(solution)/shard_map/ppermute | solution.py:322
  110.5 73.5 %copy-start.3 = (f32[2,4,128,1024]{3,2,1,0:T(8,128)S(1)}, f32[2,4,128,1024]{3,2,1,0:T(8,128)}, u32[]{:S(2)}) copy-start(f32[2,4,128,1024]{3,2,1,0:T(8,128)} %copy-done.2) | copy-start | bytes 12582916
  141.8 10.3 %collective-permute-start.19 = (bf16[128,1024]{1,0:T(8,128)(2,1)S(1)}, bf16[128,1024]{1,0:T(8,128)(2,1)S(1)}, u32[]{:S(2)}, u32[]{:S(2)}) collective-permute-start(bf16[128,1024]{1,0:T(8,128)(2,1)S(1)} %get-tuple-element.86), channel_id=1, source_target_pairs={{0,28},{4,0},{8,4},{12,8},{16,12},{20,16},{24,20},{28,24},{1,29},{... | collective-permute-start | bytes 786440 | tf_op jit(solution)/shard_map/ppermute | solution.py:322
  142.5 9.5 %collective-permute-start.21 = (bf16[128,1024]{1,0:T(8,128)(2,1)S(1)}, bf16[128,1024]{1,0:T(8,128)(2,1)S(1)}, u32[]{:S(2)}, u32[]{:S(2)}) collective-permute-start(bf16[128,1024]{1,0:T(8,128)(2,1)S(1)} %get-tuple-element.89), channel_id=1, source_target_pairs={{0,4},{4,8},{8,12},{12,16},{16,20},{20,24},{24,28},{28,0},{1,5},{5... | collective-permute-start | bytes 786440 | tf_op jit(solution)/shard_map/ppermute | solution.py:322
  143.7 31.5 %collective-permute-start.10 = (bf16[128,1024]{1,0:T(8,128)(2,1)S(1)}, bf16[128,1024]{1,0:T(8,128)(2,1)S(1)}, u32[]{:S(2)}, u32[]{:S(2)}) collective-permute-start(bf16[128,1024]{1,0:T(8,128)(2,1)S(1)} %get-tuple-element.72), channel_id=1, source_target_pairs={{0,16},{4,20},{8,24},{12,28},{16,0},{20,4},{24,8},{28,12},{1,17},{... | collective-permute-start | bytes 786440 | tf_op jit(solution)/shard_map/ppermute | solution.py:322
  148.3 27.6 %collective-permute-start.12 = (bf16[128,1024]{1,0:T(8,128)(2,1)S(1)}, bf16[128,1024]{1,0:T(8,128)(2,1)S(1)}, u32[]{:S(2)}, u32[]{:S(2)}) collective-permute-start(bf16[128,1024]{1,0:T(8,128)(2,1)S(1)} %get-tuple-element.75), channel_id=1, source_target_pairs={{0,20},{4,24},{8,28},{12,0},{16,4},{20,8},{24,12},{28,16},{1,21},{... | collective-permute-start | bytes 786440 | tf_op jit(solution)/shard_map/ppermute | solution.py:322
  148.3 39.5 %collective-permute-start.14 = (bf16[128,1024]{1,0:T(8,128)(2,1)S(1)}, bf16[128,1024]{1,0:T(8,128)(2,1)S(1)}, u32[]{:S(2)}, u32[]{:S(2)}) collective-permute-start(bf16[128,1024]{1,0:T(8,128)(2,1)S(1)} %get-tuple-element.78), channel_id=1, source_target_pairs={{0,12},{4,16},{8,20},{12,24},{16,28},{20,0},{24,4},{28,8},{1,13},{... | collective-permute-start | bytes 786440 | tf_op jit(solution)/shard_map/ppermute | solution.py:322
  152.0 44.0 %collective-permute-start.16 = (bf16[128,1024]{1,0:T(8,128)(2,1)S(1)}, bf16[128,1024]{1,0:T(8,128)(2,1)S(1)}, u32[]{:S(2)}, u32[]{:S(2)}) collective-permute-start(bf16[128,1024]{1,0:T(8,128)(2,1)S(1)} %get-tuple-element.81), channel_id=1, source_target_pairs={{0,24},{4,28},{8,0},{12,4},{16,8},{20,12},{24,16},{28,20},{1,25},{... | collective-permute-start | bytes 786440 | tf_op jit(solution)/shard_map/ppermute | solution.py:322
  152.1 44.0 %collective-permute-start.18 = (bf16[128,1024]{1,0:T(8,128)(2,1)S(1)}, bf16[128,1024]{1,0:T(8,128)(2,1)S(1)}, u32[]{:S(2)}, u32[]{:S(2)}) collective-permute-start(bf16[128,1024]{1,0:T(8,128)(2,1)S(1)} %get-tuple-element.84), channel_id=1, source_target_pairs={{0,8},{4,12},{8,16},{12,20},{16,24},{20,28},{24,0},{28,4},{1,9},{5... | collective-permute-start | bytes 786440 | tf_op jit(solution)/shard_map/ppermute | solution.py:322
  175.2 21.9 %collective-permute-start.20 = (bf16[128,1024]{1,0:T(8,128)(2,1)S(1)}, bf16[128,1024]{1,0:T(8,128)(2,1)S(1)}, u32[]{:S(2)}, u32[]{:S(2)}) collective-permute-start(bf16[128,1024]{1,0:T(8,128)(2,1)S(1)} %get-tuple-element.87), channel_id=1, source_target_pairs={{0,28},{4,0},{8,4},{12,8},{16,12},{20,16},{24,20},{28,24},{1,29},{... | collective-permute-start | bytes 786440 | tf_op jit(solution)/shard_map/ppermute | solution.py:322
  175.9 21.2 %collective-permute-start.22 = (bf16[128,1024]{1,0:T(8,128)(2,1)S(1)}, bf16[128,1024]{1,0:T(8,128)(2,1)S(1)}, u32[]{:S(2)}, u32[]{:S(2)}) collective-permute-start(bf16[128,1024]{1,0:T(8,128)(2,1)S(1)} %get-tuple-element.90), channel_id=1, source_target_pairs={{0,4},{4,8},{8,12},{12,16},{16,20},{20,24},{24,28},{28,0},{1,5},{5... | collective-permute-start | bytes 786440 | tf_op jit(solution)/shard_map/ppermute | solution.py:322
  184.0 13.1 %copy-start.5 = (f32[2,4,128,1024]{3,2,1,0:T(8,128)S(1)}, f32[2,4,128,1024]{3,2,1,0:T(8,128)}, u32[]{:S(2)}) copy-start(f32[2,4,128,1024]{3,2,1,0:T(8,128)} %copy-done.4) | copy-start | bytes 12582916

commit v5 on v4

--- a/solution.py
+++ b/solution.py
@@ -242,42 +242,42 @@
     )(fields, fields, fields, fields, below, above, strat_col, high, low)
 
 
-def finish_body(count, me_ref, part_ref, u_ref, *refs):
-    fars, out_ref = refs[:count], refs[-1]
-    for k, far_ref in enumerate(fars):
-
-        @pl.when(pl.program_id(0) == k)
-        def _(far_ref=far_ref):
-            out_ref[...] = part_ref[...] - u_ref[...].astype(F32) * far_ref[...].astype(F32)
+def finish_body(offsets, base, me_ref, part_ref, u_ref, *refs):
+    devices = len(offsets)
+    fars, out_ref, sum_ref, sems = refs[:devices], refs[-3], refs[-2], refs[-1]
+    rows, _ = fars[0].shape
+    u_blocks = u_ref.shape[0] // rows
+    copies = []
+    for i, (offset, far_ref) in enumerate(zip(offsets, fars)):
+        owner = (me_ref[0] + offset) % devices
+        part = part_ref[pl.ds(pl.multiple_of(owner * rows, rows), rows), :]
+        speed_u = u_ref[pl.ds(pl.multiple_of(owner % u_blocks * rows, rows), rows), :]
+        sum_ref[i] = part - speed_u.astype(F32) * far_ref[...].astype(F32)
+        target = pl.multiple_of((base + owner) * rows, rows)
+        copies.append(
+            pltpu.make_async_copy(sum_ref.at[i], out_ref.at[pl.ds(target, rows)], sems.at[i])
+        )
+        copies[-1].start()
+    for copy in copies:
+        copy.wait()
 
 
 def finish(out, part, speed_u, offsets, fars, me, total_rows):
     devices = len(fars)
     rows, width = fars[0].shape
-    u_blocks = speed_u.shape[0] // rows
     base = 0 if out is None else total_rows // rows - devices
     given = [] if out is None else [out]
-
-    def owner(i, m):
-        offset = offsets[-1]
-        for index in range(devices - 1):
-            offset = jnp.where(i == index, offsets[index], offset)
-        return (m[0] + offset) % devices
-
-    return pl.pallas_call(
-        functools.partial(finish_body, devices),
-        grid_spec=pltpu.PrefetchScalarGridSpec(
-            num_scalar_prefetch=1,
-            grid=(devices,),
-            in_specs=[
-                pl.BlockSpec((rows, width), lambda i, m: (owner(i, m), 0)),
-                pl.BlockSpec((rows, width), lambda i, m: (owner(i, m) % u_blocks, 0)),
-            ]
-            + [pl.BlockSpec((rows, width), lambda i, m: (0, 0))] * devices
-            + [pl.BlockSpec(memory_space=pl.ANY)] * len(given),
-            out_specs=pl.BlockSpec((rows, width), lambda i, m: (base + owner(i, m), 0)),
-        ),
+    return pl.pallas_call(
+        functools.partial(finish_body, offsets, base),
+        in_specs=[pl.BlockSpec(memory_space=pltpu.SMEM)]
+        + [pl.BlockSpec(memory_space=pltpu.VMEM)] * (2 + devices)
+        + [pl.BlockSpec(memory_space=pl.ANY)] * len(given),
+        out_specs=pl.BlockSpec(memory_space=pl.ANY),
         out_shape=jax.ShapeDtypeStruct((total_rows, width), F32),
+        scratch_shapes=[
+            pltpu.VMEM((devices, rows, width), F32),
+            pltpu.SemaphoreType.DMA((devices,)),
+        ],
         input_output_aliases={3 + devices: 0} if given else {},
         compiler_params=pltpu.CompilerParams(vmem_limit_bytes=UPDATE_VMEM),
         cost_estimate=pl.CostEstimate(

time: 201 us -> 200 us (level)
  Pallas kernels: 95.1 us -> 92 us
    pallas_call x2, Pallas kernels: 7.57 us -> 4.45 us  [finish(): pl.pallas_call(functools.partial(finish_body, offsets, base), in_specs=[p...]
where the time goes in v5:
time: 200 us; the launch traced here: 199 us
  Pallas kernels  92 us (46%)
  starting transfers between devices  50.8 us (25%)
  waiting for transfers between devices  41.4 us (21%)
  local copies, waits for them, and re-layouts  14.7 us (7%)
    ppermute x21, starting transfers between devices, ahead(): lax.ppermute(block, 'gx', [(i, (i + k) % devices) for i in range(devices)])  39.9 us
    pallas_call x1, Pallas kernels, far_whole(): pl.pallas_call(functools.partial(far_whole_body, devices), grid_spec=pltp...  33.2 us
    ppermute x21, waiting for transfers between devices, ahead(): lax.ppermute(block, 'gx', [(i, (i + k) % devices) for i in range(devices)])  32.7 us
    pallas_call x1, Pallas kernels, far_slopes(): pl.pallas_call(functools.partial(far_body, devices, shifts), grid_spec=pl...  31.2 us
    pallas_call x2, Pallas kernels, local_part(): pl.pallas_call(functools.partial(local_body, base), grid=(lines, count),...  20.5 us
    all_to_all x1, waiting for transfers between devices, body(): lax.all_to_all(flat[:held].reshape(devices, rows, width), 'gx', split_axi...  8.68 us
    unnamed x22, local copies, waits for them, and re-layouts  8.67 us
    all_to_all x1, starting transfers between devices, body(): lax.all_to_all(flat[:held].reshape(devices, rows, width), 'gx', split_axi...  5.64 us
  transfers between devices with their start and end apart: 24, of which 7 were waited for; matrix products, arithmetic and copies ran while one was open for 1% of the time, Pallas kernels for 45%

profile of v5, /device:TPU:9, one launch (start us, length us, event | category | flops | bytes accessed | tf_op | source)
XLA Modules:
  0.0 199.4 jit_solution(7445091491553014589)
XLA Ops:
  0.0 3.1 %slice.15 = bf16[2,4,128,1024]{3,2,1,0:T(8,128)(2,1)} slice(bf16[4,4,128,1024]{3,2,1,0:T(8,128)(2,1)} %b_ref.3), slice={[0:2], [0:4], [0:128], [0:1024]} | slice | bytes 4194304 | tf_op jit(solution)/shard_map/slice | solution.py:329
  3.1 5.6 %all-to-all-start = ((bf16[8,128,1024]{2,1,0:T(8,128)(2,1)}), bf16[8,128,1024]{2,1,0:T(8,128)(2,1)}, u32[]{:S(2)}, u32[]{:S(2)}) async-start(bf16[8,128,1024]{2,1,0:T(8,128)(2,1)} %bitcast.3), calls=%async_computation | async-start | bytes 4194304 | tf_op jit(solution)/shard_map/all_to_all | solution.py:328
  8.7 1.1 fusion
  9.9 1.3 collective-permute-start.1
  11.2 4.0 %collective-permute-start = (bf16[4,4,4,1024]{3,2,1,0:T(4,128)(2,1)S(1)}, bf16[4,4,4,1024]{3,2,1,0:T(4,128)(2,1)S(1)}, u32[]{:S(2)}, u32[]{:S(2)}) collective-permute-start(bf16[4,4,4,1024]{3,2,1,0:T(4,128)(2,1)S(1)} %get-tuple-element.101), channel_id=1, source_target_pairs={{0,1},{1,2},{2,3},{4,5},{5,6},{6,7},{8,9},{9,10},{10,11},{12,13},{... | collective-permute-start | bytes 393224 | tf_op jit(solution)/shard_map/ppermute | solution.py:300
  15.3 0.1 copy.5.strat_ref
  15.4 2.6 %shard_map.37 = (bf16[128,9088]{1,0:T(8,128)(2,1)S(1)}, bf16[128,9088]{1,0:T(8,128)(2,1)S(1)}) custom-call(f32[1,8192]{1,0:T(1,128)S(1)} %copy-done.9), custom_call_target="tpu_custom_call" | custom-call | flops 4194304 | bytes 4194304 | tf_op jit(solution)/shard_map/pallas_call | solution.py:56
  18.0 0.0 collective-permute-done.1.above_ref
  18.0 0.0 collective-permute-done.below_ref
  18.0 0.0 copy-start
  18.1 3.0 %copy-done = bf16[4,4,128,1024]{3,2,1,0:T(8,128)(2,1)S(1)} copy-done((bf16[4,4,128,1024]{3,2,1,0:T(8,128)(2,1)S(1)}, bf16[4,4,128,1024]{3,2,1,0:T(8,128)(2,1)}, u32[]{:S(2)}) %copy-start) | copy-done | bytes 4194328
  21.1 10.2 %shard_map.39 = f32[2,4,128,1024]{3,2,1,0:T(8,128)S(1)} custom-call(bf16[4,4,128,1024]{3,2,1,0:T(8,128)(2,1)S(1)} %copy-done, bf16[4,4,128,1024]{3,2,1,0:T(8,128)(2,1)S(1)} %copy-done, bf16[4,4,128,1024]{3,2,1,0:T(8,128)(2,1)S(1)} %copy-done, bf16[4,4,128,1024]{3,2,1,0:T(8,128)(2,1)S(1)} %copy-done, ...), custom_call_target="tpu_custom_call" | custom-call | flops 4294967296 | bytes 8388608 | tf_op jit(solution)/shard_map/pallas_call | solution.py:219
  31.3 2.0 copy-done.4
  33.3 10.2 %shard_map.38 = f32[2,4,128,1024]{3,2,1,0:T(8,128)S(1)} custom-call(bf16[4,4,128,1024]{3,2,1,0:T(8,128)(2,1)S(1)} %copy-done, bf16[4,4,128,1024]{3,2,1,0:T(8,128)(2,1)S(1)} %copy-done, bf16[4,4,128,1024]{3,2,1,0:T(8,128)(2,1)S(1)} %copy-done, bf16[4,4,128,1024]{3,2,1,0:T(8,128)(2,1)S(1)} %copy-done, ...), custom_call_target="tpu_custom_call" | custom-call | flops 4294967296 | bytes 8388608 | tf_op jit(solution)/shard_map/pallas_call | solution.py:219
  43.6 0.0 copy-start.2
  43.6 2.0 %copy-done.2 = f32[2,4,128,1024]{3,2,1,0:T(8,128)} copy-done((f32[2,4,128,1024]{3,2,1,0:T(8,128)}, f32[2,4,128,1024]{3,2,1,0:T(8,128)S(1)}, u32[]{:S(2)}) %copy-start.2) | copy-done | bytes 4194328
  45.6 8.7 %all-to-all-done = bf16[8,128,1024]{2,1,0:T(8,128)(2,1)} async-done(((bf16[8,128,1024]{2,1,0:T(8,128)(2,1)}), bf16[8,128,1024]{2,1,0:T(8,128)(2,1)}, u32[]{:S(2)}, u32[]{:S(2)}) %all-to-all-start) | async-done | bytes 2097184 | tf_op jit(solution)/shard_map/all_to_all | solution.py:328
  54.3 1.6 constant_dynamic-slice_fusion
  55.9 0.5 collective-permute-start.8
  56.3 1.3 collective-permute-start.7
  57.7 2.8 %collective-permute-start.6 = (bf16[128,1024]{1,0:T(8,128)(2,1)S(1)}, bf16[128,1024]{1,0:T(8,128)(2,1)S(1)}, u32[]{:S(2)}, u32[]{:S(2)}) collective-permute-start(bf16[128,1024]{1,0:T(8,128)(2,1)S(1)} %get-tuple-element.95), channel_id=1, source_target_pairs={{0,24},{4,28},{8,0},{12,4},{16,8},{20,12},{24,16},{28,20},{1,25},{... | collective-permute-start | bytes 786440 | tf_op jit(solution)/shard_map/ppermute | solution.py:322
  60.5 0.0 collective-permute-start.5
  60.5 2.0 collective-permute-start.4
  62.5 0.6 collective-permute-done.8.refs_7_
  63.1 0.6 collective-permute-start.3
  63.7 0.0 collective-permute-done.7.refs_6_
  63.7 5.9 %collective-permute-start.2 = (bf16[128,1024]{1,0:T(8,128)(2,1)S(1)}, bf16[128,1024]{1,0:T(8,128)(2,1)S(1)}, u32[]{:S(2)}, u32[]{:S(2)}) collective-permute-start(bf16[128,1024]{1,0:T(8,128)(2,1)S(1)} %get-tuple-element.99), channel_id=1, source_target_pairs={{0,16},{4,20},{8,24},{12,28},{16,0},{20,4},{24,8},{28,12},{1,17},{... | collective-permute-start | bytes 786440 | tf_op jit(solution)/shard_map/ppermute | solution.py:322
  69.6 1.7 copy-done.7
  71.2 33.2 %shard_map.40 = (bf16[128,1024]{1,0:T(8,128)(2,1)S(1)}, bf16[128,1024]{1,0:T(8,128)(2,1)S(1)}, bf16[128,1024]{1,0:T(8,128)(2,1)S(1)}, bf16[128,1024]{1,0:T(8,128...) custom-call(s32[1]{0:T(128)} %bitcast.me_ref, ...), custom_call_target="tpu_custom_call" | custom-call | flops 30064771072 | bytes 8847360 | tf_op jit(solution)/shard_map/pallas_call | solution.py:113
  104.5 0.0 collective-permute-done.6.refs_5_
  104.5 0.0 collective-permute-done.5.refs_4_
  104.5 0.0 collective-permute-done.4.refs_3_
  104.5 0.0 collective-permute-done.3.refs_2_
  104.5 0.0 collective-permute-done.2.refs_1_
  104.5 0.1 collective-permute-start.9
  104.6 4.4 %collective-permute-start.11 = (bf16[128,1024]{1,0:T(8,128)(2,1)S(1)}, bf16[128,1024]{1,0:T(8,128)(2,1)S(1)}, u32[]{:S(2)}, u32[]{:S(2)}) collective-permute-start(bf16[128,1024]{1,0:T(8,128)(2,1)S(1)} %get-tuple-element.74), channel_id=1, source_target_pairs={{0,20},{4,24},{8,28},{12,0},{16,4},{20,8},{24,12},{28,16},{1,21},{... | collective-permute-start | bytes 786440 | tf_op jit(solution)/shard_map/ppermute | solution.py:322
  109.0 0.0 collective-permute-start.13
  109.0 0.4 collective-permute-start.15
  109.4 1.1 collective-permute-start.17
  110.5 31.2 %shard_map.41 = (bf16[128,1024]{1,0:T(8,128)(2,1)S(1)}, bf16[128,1024]{1,0:T(8,128)(2,1)S(1)}, bf16[128,1024]{1,0:T(8,128)(2,1)S(1)}, bf16[128,1024]{1,0:T(8,128...) custom-call(s32[1]{0:T(128)} %bitcast.me_ref, ...), custom_call_target="tpu_custom_call" | custom-call | flops 30064771072 | bytes 8847360 | tf_op jit(solution)/shard_map/pallas_call | solution.py:158
  141.7 0.0 collective-permute-done.9.refs_1_
  141.8 0.8 collective-permute-start.19
  142.5 0.0 collective-permute-done.11.refs_2_
  142.5 1.2 collective-permute-start.21
  143.7 0.0 collective-permute-done.13.refs_3_
  143.7 4.0 %collective-permute-start.10 = (bf16[128,1024]{1,0:T(8,128)(2,1)S(1)}, bf16[128,1024]{1,0:T(8,128)(2,1)S(1)}, u32[]{:S(2)}, u32[]{:S(2)}) collective-permute-start(bf16[128,1024]{1,0:T(8,128)(2,1)S(1)} %get-tuple-element.72), channel_id=1, source_target_pairs={{0,16},{4,20},{8,24},{12,28},{16,0},{20,4},{24,8},{28,12},{1,17},{... | collective-permute-start | bytes 786440 | tf_op jit(solution)/shard_map/ppermute | solution.py:322
  147.7 0.6 collective-permute-done.15.refs_4_
  148.3 0.0 collective-permute-start.12
  148.3 0.0 collective-permute-done.17.refs_5_
  148.3 2.6 %collective-permute-start.14 = (bf16[128,1024]{1,0:T(8,128)(2,1)S(1)}, bf16[128,1024]{1,0:T(8,128)(2,1)S(1)}, u32[]{:S(2)}, u32[]{:S(2)}) collective-permute-start(bf16[128,1024]{1,0:T(8,128)(2,1)S(1)} %get-tuple-element.78), channel_id=1, source_target_pairs={{0,12},{4,16},{8,20},{12,24},{16,28},{20,0},{24,4},{28,8},{1,13},{... | collective-permute-start | bytes 786440 | tf_op jit(solution)/shard_map/ppermute | solution.py:322
  151.0 1.1 collective-permute-done.19.refs_6_
  152.0 0.0 collective-permute-start.16
  152.0 0.0 collective-permute-done.21.refs_7_
  152.1 3.5 %collective-permute-start.18 = (bf16[128,1024]{1,0:T(8,128)(2,1)S(1)}, bf16[128,1024]{1,0:T(8,128)(2,1)S(1)}, u32[]{:S(2)}, u32[]{:S(2)}) collective-permute-start(bf16[128,1024]{1,0:T(8,128)(2,1)S(1)} %get-tuple-element.84), channel_id=1, source_target_pairs={{0,8},{4,12},{8,16},{12,20},{16,24},{20,28},{24,0},{28,4},{1,9},{5... | collective-permute-start | bytes 786440 | tf_op jit(solution)/shard_map/ppermute | solution.py:322
  155.6 19.6 %collective-permute-done.10.refs_1_ = bf16[128,1024]{1,0:T(8,128)(2,1)S(1)} collective-permute-done((bf16[128,1024]{1,0:T(8,128)(2,1)S(1)}, bf16[128,1024]{1,0:T(8,128)(2,1)S(1)}, u32[]{:S(2)}, u32[]{:S(2)}) %collective-permute-start.10) | collective-permute-done | bytes 262176 | tf_op jit(solution)/shard_map/ppermute | solution.py:322
  175.2 0.8 collective-permute-start.20
  175.9 8.0 %collective-permute-start.22 = (bf16[128,1024]{1,0:T(8,128)(2,1)S(1)}, bf16[128,1024]{1,0:T(8,128)(2,1)S(1)}, u32[]{:S(2)}, u32[]{:S(2)}) collective-permute-start(bf16[128,1024]{1,0:T(8,128)(2,1)S(1)} %get-tuple-element.90), channel_id=1, source_target_pairs={{0,4},{4,8},{8,12},{12,16},{16,20},{20,24},{24,28},{28,0},{1,5},{5... | collective-permute-start | bytes 786440 | tf_op jit(solution)/shard_map/ppermute | solution.py:322
  183.9 0.1 slice.16.u_ref
  184.0 2.3 %shard_map.42.refs_8_ = f32[2048,1024]{1,0:T(8,128)} custom-call(s32[1]{0:T(128)} %bitcast.me_ref, f32[1024,1024]{1,0:T(8,128)S(1)} %bitcast.11, bf16[512,1024]{1,0:T(8,128)(2,1)S(1)} %slice.16.u_ref, bf16[128,1024]{1,0:T(8,128)(2,1)S(1)} %get-tuple-element.92.refs_0_, bf16[128,1024]{1,0:T(8,128)(2,1)S(1)} %collective-permute-done.9.refs_1_, ...), custom_call_target="tpu_custom_call" | custom-call | flops 2097152 | bytes 12582912 | tf_op jit(solution)/shard_map/pallas_call | solution.py:270
  186.3 9.8 %collective-permute-done.16.refs_4_ = bf16[128,1024]{1,0:T(8,128)(2,1)S(1)} collective-permute-done((bf16[128,1024]{1,0:T(8,128)(2,1)S(1)}, bf16[128,1024]{1,0:T(8,128)(2,1)S(1)}, u32[]{:S(2)}, u32[]{:S(2)}) %collective-permute-start.16) | collective-permute-done | bytes 262176 | tf_op jit(solution)/shard_map/ppermute | solution.py:322
  196.1 0.0 collective-permute-done.18.refs_5_
  196.1 1.0 collective-permute-done.20.refs_6_
  197.1 0.0 collective-permute-done.22.refs_7_
  197.1 2.2 %shard_map.43 = f32[2048,1024]{1,0:T(8,128)} custom-call(s32[1]{0:T(128)} %bitcast.me_ref, f32[1024,1024]{1,0:T(8,128)S(1)} %bitcast.12, bf16[512,1024]{1,0:T(8,128)(2,1)S(1)} %slice.16.u_ref, bf16[128,1024]{1,0:T(8,128)(2,1)S(1)} %get-tuple-element.69.refs_0_, ...), custom_call_target="tpu_custom_call", output_to_operand_aliasing={{}: (11, {})} | custom-call | flops 2097152 | bytes 12582912 | tf_op jit(solution)/shard_map/pallas_call | solution.py:270
  (18 shorter events, 0.0 us)
Async XLA Ops:
  0.0 15.4 %copy-start.9 = (f32[1,8192]{1,0:T(1,128)S(1)}, f32[1,8192]{1,0:T(1,128)}, u32[]{:S(2)}) copy-start(f32[1,8192]{1,0:T(1,128)} %constant.64.row_ref) | copy-start | bytes 98308
  0.0 15.3 %copy-start.10 = (f32[128]{0:T(128)S(1)}, f32[128]{0:T(128)}, u32[]{:S(2)}) copy-start(f32[128]{0:T(128)} %param.4) | copy-start | bytes 1540
  3.1 51.1 %all-to-all-start = ((bf16[8,128,1024]{2,1,0:T(8,128)(2,1)}), bf16[8,128,1024]{2,1,0:T(8,128)(2,1)}, u32[]{:S(2)}, u32[]{:S(2)}) async-start(bf16[8,128,1024]{2,1,0:T(8,128)(2,1)} %bitcast.3), calls=%async_computation | async-start | bytes 4194304 | tf_op jit(solution)/shard_map/all_to_all | solution.py:328
  9.9 8.1 %collective-permute-start.1 = (bf16[4,4,4,1024]{3,2,1,0:T(4,128)(2,1)S(1)}, bf16[4,4,4,1024]{3,2,1,0:T(4,128)(2,1)S(1)}, u32[]{:S(2)}, u32[]{:S(2)}) collective-permute-start(bf16[4,4,4,1024]{3,2,1,0:T(4,128)(2,1)S(1)} %get-tuple-element.100), channel_id=1, source_target_pairs={{1,0},{2,1},{3,2},{5,4},{6,5},{7,6},{9,8},{10,9},{11,10},{13,12},{... | collective-permute-start | bytes 393224 | tf_op jit(solution)/shard_map/ppermute | solution.py:301
  11.2 6.9 %collective-permute-start = (bf16[4,4,4,1024]{3,2,1,0:T(4,128)(2,1)S(1)}, bf16[4,4,4,1024]{3,2,1,0:T(4,128)(2,1)S(1)}, u32[]{:S(2)}, u32[]{:S(2)}) collective-permute-start(bf16[4,4,4,1024]{3,2,1,0:T(4,128)(2,1)S(1)} %get-tuple-element.101), channel_id=1, source_target_pairs={{0,1},{1,2},{2,3},{4,5},{5,6},{6,7},{8,9},{9,10},{10,11},{12,13},{... | collective-permute-start | bytes 393224 | tf_op jit(solution)/shard_map/ppermute | solution.py:300
  18.0 13.3 %copy-start.6 = (bf16[128,9088]{1,0:T(8,128)(2,1)}, bf16[128,9088]{1,0:T(8,128)(2,1)S(1)}, u32[]{:S(2)}) copy-start(bf16[128,9088]{1,0:T(8,128)(2,1)S(1)} %get-tuple-element.50.low_ref.refs_9_) | copy-start | bytes 6979588
  18.0 3.0 %copy-start = (bf16[4,4,128,1024]{3,2,1,0:T(8,128)(2,1)S(1)}, bf16[4,4,128,1024]{3,2,1,0:T(8,128)(2,1)}, u32[]{:S(2)}) copy-start(bf16[4,4,128,1024]{3,2,1,0:T(8,128)(2,1)} %b_ref.3) | copy-start | bytes 12582916
  31.3 2.0 copy-start.4
  43.6 2.0 %copy-start.2 = (f32[2,4,128,1024]{3,2,1,0:T(8,128)}, f32[2,4,128,1024]{3,2,1,0:T(8,128)S(1)}, u32[]{:S(2)}) copy-start(f32[2,4,128,1024]{3,2,1,0:T(8,128)S(1)} %shard_map.38) | copy-start | bytes 12582916
  55.9 7.2 %collective-permute-start.8 = (bf16[128,1024]{1,0:T(8,128)(2,1)S(1)}, bf16[128,1024]{1,0:T(8,128)(2,1)S(1)}, u32[]{:S(2)}, u32[]{:S(2)}) collective-permute-start(bf16[128,1024]{1,0:T(8,128)(2,1)S(1)} %get-tuple-element.93), channel_id=1, source_target_pairs={{0,28},{4,0},{8,4},{12,8},{16,12},{20,16},{24,20},{28,24},{1,29},{... | collective-permute-start | bytes 786440 | tf_op jit(solution)/shard_map/ppermute | solution.py:322
  56.3 7.3 %collective-permute-start.7 = (bf16[128,1024]{1,0:T(8,128)(2,1)S(1)}, bf16[128,1024]{1,0:T(8,128)(2,1)S(1)}, u32[]{:S(2)}, u32[]{:S(2)}) collective-permute-start(bf16[128,1024]{1,0:T(8,128)(2,1)S(1)} %get-tuple-element.94), channel_id=1, source_target_pairs={{0,4},{4,8},{8,12},{12,16},{16,20},{20,24},{24,28},{28,0},{1,5},{5... | collective-permute-start | bytes 786440 | tf_op jit(solution)/shard_map/ppermute | solution.py:322
  57.7 46.8 %collective-permute-start.6 = (bf16[128,1024]{1,0:T(8,128)(2,1)S(1)}, bf16[128,1024]{1,0:T(8,128)(2,1)S(1)}, u32[]{:S(2)}, u32[]{:S(2)}) collective-permute-start(bf16[128,1024]{1,0:T(8,128)(2,1)S(1)} %get-tuple-element.95), channel_id=1, source_target_pairs={{0,24},{4,28},{8,0},{12,4},{16,8},{20,12},{24,16},{28,20},{1,25},{... | collective-permute-start | bytes 786440 | tf_op jit(solution)/shard_map/ppermute | solution.py:322
  60.5 44.0 %collective-permute-start.5 = (bf16[128,1024]{1,0:T(8,128)(2,1)S(1)}, bf16[128,1024]{1,0:T(8,128)(2,1)S(1)}, u32[]{:S(2)}, u32[]{:S(2)}) collective-permute-start(bf16[128,1024]{1,0:T(8,128)(2,1)S(1)} %get-tuple-element.96), channel_id=1, source_target_pairs={{0,8},{4,12},{8,16},{12,20},{16,24},{20,28},{24,0},{28,4},{1,9},{5... | collective-permute-start | bytes 786440 | tf_op jit(solution)/shard_map/ppermute | solution.py:322
  60.5 44.0 %collective-permute-start.4 = (bf16[128,1024]{1,0:T(8,128)(2,1)S(1)}, bf16[128,1024]{1,0:T(8,128)(2,1)S(1)}, u32[]{:S(2)}, u32[]{:S(2)}) collective-permute-start(bf16[128,1024]{1,0:T(8,128)(2,1)S(1)} %get-tuple-element.97), channel_id=1, source_target_pairs={{0,20},{4,24},{8,28},{12,0},{16,4},{20,8},{24,12},{28,16},{1,21},{... | collective-permute-start | bytes 786440 | tf_op jit(solution)/shard_map/ppermute | solution.py:322
  63.1 41.4 %collective-permute-start.3 = (bf16[128,1024]{1,0:T(8,128)(2,1)S(1)}, bf16[128,1024]{1,0:T(8,128)(2,1)S(1)}, u32[]{:S(2)}, u32[]{:S(2)}) collective-permute-start(bf16[128,1024]{1,0:T(8,128)(2,1)S(1)} %get-tuple-element.98), channel_id=1, source_target_pairs={{0,12},{4,16},{8,20},{12,24},{16,28},{20,0},{24,4},{28,8},{1,13},{... | collective-permute-start | bytes 786440 | tf_op jit(solution)/shard_map/ppermute | solution.py:322
  63.7 40.8 %collective-permute-start.2 = (bf16[128,1024]{1,0:T(8,128)(2,1)S(1)}, bf16[128,1024]{1,0:T(8,128)(2,1)S(1)}, u32[]{:S(2)}, u32[]{:S(2)}) collective-permute-start(bf16[128,1024]{1,0:T(8,128)(2,1)S(1)} %get-tuple-element.99), channel_id=1, source_target_pairs={{0,16},{4,20},{8,24},{12,28},{16,0},{20,4},{24,8},{28,12},{1,17},{... | collective-permute-start | bytes 786440 | tf_op jit(solution)/shard_map/ppermute | solution.py:322
  69.6 1.7 copy-start.7
  71.2 39.3 %copy-start.1 = (bf16[4,4,128,1024]{3,2,1,0:T(8,128)(2,1)S(1)}, bf16[4,4,128,1024]{3,2,1,0:T(8,128)(2,1)}, u32[]{:S(2)}) copy-start(bf16[4,4,128,1024]{3,2,1,0:T(8,128)(2,1)} %b_ref.3) | copy-start | bytes 12582916
  71.2 39.3 %copy-start.8 = (bf16[128,9088]{1,0:T(8,128)(2,1)S(1)}, bf16[128,9088]{1,0:T(8,128)(2,1)}, u32[]{:S(2)}) copy-start(bf16[128,9088]{1,0:T(8,128)(2,1)} %copy-done.6) | copy-start | bytes 6979588
  104.5 37.2 %collective-permute-start.9 = (bf16[128,1024]{1,0:T(8,128)(2,1)S(1)}, bf16[128,1024]{1,0:T(8,128)(2,1)S(1)}, u32[]{:S(2)}, u32[]{:S(2)}) collective-permute-start(bf16[128,1024]{1,0:T(8,128)(2,1)S(1)} %get-tuple-element.71), channel_id=1, source_target_pairs={{0,16},{4,20},{8,24},{12,28},{16,0},{20,4},{24,8},{28,12},{1,17},{... | collective-permute-start | bytes 786440 | tf_op jit(solution)/shard_map/ppermute | solution.py:322
  104.6 37.9 %collective-permute-start.11 = (bf16[128,1024]{1,0:T(8,128)(2,1)S(1)}, bf16[128,1024]{1,0:T(8,128)(2,1)S(1)}, u32[]{:S(2)}, u32[]{:S(2)}) collective-permute-start(bf16[128,1024]{1,0:T(8,128)(2,1)S(1)} %get-tuple-element.74), channel_id=1, source_target_pairs={{0,20},{4,24},{8,28},{12,0},{16,4},{20,8},{24,12},{28,16},{1,21},{... | collective-permute-start | bytes 786440 | tf_op jit(solution)/shard_map/ppermute | solution.py:322
  109.0 34.7 %collective-permute-start.13 = (bf16[128,1024]{1,0:T(8,128)(2,1)S(1)}, bf16[128,1024]{1,0:T(8,128)(2,1)S(1)}, u32[]{:S(2)}, u32[]{:S(2)}) collective-permute-start(bf16[128,1024]{1,0:T(8,128)(2,1)S(1)} %get-tuple-element.77), channel_id=1, source_target_pairs={{0,12},{4,16},{8,20},{12,24},{16,28},{20,0},{24,4},{28,8},{1,13},{... | collective-permute-start | bytes 786440 | tf_op jit(solution)/shard_map/ppermute | solution.py:322
  109.0 39.3 %collective-permute-start.15 = (bf16[128,1024]{1,0:T(8,128)(2,1)S(1)}, bf16[128,1024]{1,0:T(8,128)(2,1)S(1)}, u32[]{:S(2)}, u32[]{:S(2)}) collective-permute-start(bf16[128,1024]{1,0:T(8,128)(2,1)S(1)} %get-tuple-element.80), channel_id=1, source_target_pairs={{0,24},{4,28},{8,0},{12,4},{16,8},{20,12},{24,16},{28,20},{1,25},{... | collective-permute-start | bytes 786440 | tf_op jit(solution)/shard_map/ppermute | solution.py:322
  109.4 38.9 %collective-permute-start.17 = (bf16[128,1024]{1,0:T(8,128)(2,1)S(1)}, bf16[128,1024]{1,0:T(8,128)(2,1)S(1)}, u32[]{:S(2)}, u32[]{:S(2)}) collective-permute-start(bf16[128,1024]{1,0:T(8,128)(2,1)S(1)} %get-tuple-element.83), channel_id=1, source_target_pairs={{0,8},{4,12},{8,16},{12,20},{16,24},{20,28},{24,0},{28,4},{1,9},{5... | collective-permute-start | bytes 786440 | tf_op jit(solution)/shard_map/ppermute | solution.py:322
  110.5 73.5 %copy-start.3 = (f32[2,4,128,1024]{3,2,1,0:T(8,128)S(1)}, f32[2,4,128,1024]{3,2,1,0:T(8,128)}, u32[]{:S(2)}) copy-start(f32[2,4,128,1024]{3,2,1,0:T(8,128)} %copy-done.2) | copy-start | bytes 12582916
  141.8 10.3 %collective-permute-start.19 = (bf16[128,1024]{1,0:T(8,128)(2,1)S(1)}, bf16[128,1024]{1,0:T(8,128)(2,1)S(1)}, u32[]{:S(2)}, u32[]{:S(2)}) collective-permute-start(bf16[128,1024]{1,0:T(8,128)(2,1)S(1)} %get-tuple-element.86), channel_id=1, source_target_pairs={{0,28},{4,0},{8,4},{12,8},{16,12},{20,16},{24,20},{28,24},{1,29},{... | collective-permute-start | bytes 786440 | tf_op jit(solution)/shard_map/ppermute | solution.py:322
  142.5 9.5 %collective-permute-start.21 = (bf16[128,1024]{1,0:T(8,128)(2,1)S(1)}, bf16[128,1024]{1,0:T(8,128)(2,1)S(1)}, u32[]{:S(2)}, u32[]{:S(2)}) collective-permute-start(bf16[128,1024]{1,0:T(8,128)(2,1)S(1)} %get-tuple-element.89), channel_id=1, source_target_pairs={{0,4},{4,8},{8,12},{12,16},{16,20},{20,24},{24,28},{28,0},{1,5},{5... | collective-permute-start | bytes 786440 | tf_op jit(solution)/shard_map/ppermute | solution.py:322
  143.7 31.5 %collective-permute-start.10 = (bf16[128,1024]{1,0:T(8,128)(2,1)S(1)}, bf16[128,1024]{1,0:T(8,128)(2,1)S(1)}, u32[]{:S(2)}, u32[]{:S(2)}) collective-permute-start(bf16[128,1024]{1,0:T(8,128)(2,1)S(1)} %get-tuple-element.72), channel_id=1, source_target_pairs={{0,16},{4,20},{8,24},{12,28},{16,0},{20,4},{24,8},{28,12},{1,17},{... | collective-permute-start | bytes 786440 | tf_op jit(solution)/shard_map/ppermute | solution.py:322
  148.3 27.6 %collective-permute-start.12 = (bf16[128,1024]{1,0:T(8,128)(2,1)S(1)}, bf16[128,1024]{1,0:T(8,128)(2,1)S(1)}, u32[]{:S(2)}, u32[]{:S(2)}) collective-permute-start(bf16[128,1024]{1,0:T(8,128)(2,1)S(1)} %get-tuple-element.75), channel_id=1, source_target_pairs={{0,20},{4,24},{8,28},{12,0},{16,4},{20,8},{24,12},{28,16},{1,21},{... | collective-permute-start | bytes 786440 | tf_op jit(solution)/shard_map/ppermute | solution.py:322
  148.3 38.0 %collective-permute-start.14 = (bf16[128,1024]{1,0:T(8,128)(2,1)S(1)}, bf16[128,1024]{1,0:T(8,128)(2,1)S(1)}, u32[]{:S(2)}, u32[]{:S(2)}) collective-permute-start(bf16[128,1024]{1,0:T(8,128)(2,1)S(1)} %get-tuple-element.78), channel_id=1, source_target_pairs={{0,12},{4,16},{8,20},{12,24},{16,28},{20,0},{24,4},{28,8},{1,13},{... | collective-permute-start | bytes 786440 | tf_op jit(solution)/shard_map/ppermute | solution.py:322
  152.0 44.0 %collective-permute-start.16 = (bf16[128,1024]{1,0:T(8,128)(2,1)S(1)}, bf16[128,1024]{1,0:T(8,128)(2,1)S(1)}, u32[]{:S(2)}, u32[]{:S(2)}) collective-permute-start(bf16[128,1024]{1,0:T(8,128)(2,1)S(1)} %get-tuple-element.81), channel_id=1, source_target_pairs={{0,24},{4,28},{8,0},{12,4},{16,8},{20,12},{24,16},{28,20},{1,25},{... | collective-permute-start | bytes 786440 | tf_op jit(solution)/shard_map/ppermute | solution.py:322
  152.1 44.0 %collective-permute-start.18 = (bf16[128,1024]{1,0:T(8,128)(2,1)S(1)}, bf16[128,1024]{1,0:T(8,128)(2,1)S(1)}, u32[]{:S(2)}, u32[]{:S(2)}) collective-permute-start(bf16[128,1024]{1,0:T(8,128)(2,1)S(1)} %get-tuple-element.84), channel_id=1, source_target_pairs={{0,8},{4,12},{8,16},{12,20},{16,24},{20,28},{24,0},{28,4},{1,9},{5... | collective-permute-start | bytes 786440 | tf_op jit(solution)/shard_map/ppermute | solution.py:322
  175.2 21.9 %collective-permute-start.20 = (bf16[128,1024]{1,0:T(8,128)(2,1)S(1)}, bf16[128,1024]{1,0:T(8,128)(2,1)S(1)}, u32[]{:S(2)}, u32[]{:S(2)}) collective-permute-start(bf16[128,1024]{1,0:T(8,128)(2,1)S(1)} %get-tuple-element.87), channel_id=1, source_target_pairs={{0,28},{4,0},{8,4},{12,8},{16,12},{20,16},{24,20},{28,24},{1,29},{... | collective-permute-start | bytes 786440 | tf_op jit(solution)/shard_map/ppermute | solution.py:322
  175.9 21.2 %collective-permute-start.22 = (bf16[128,1024]{1,0:T(8,128)(2,1)S(1)}, bf16[128,1024]{1,0:T(8,128)(2,1)S(1)}, u32[]{:S(2)}, u32[]{:S(2)}) collective-permute-start(bf16[128,1024]{1,0:T(8,128)(2,1)S(1)} %get-tuple-element.90), channel_id=1, source_target_pairs={{0,4},{4,8},{8,12},{12,16},{16,20},{20,24},{24,28},{28,0},{1,5},{5... | collective-permute-start | bytes 786440 | tf_op jit(solution)/shard_map/ppermute | solution.py:322
  184.0 13.1 %copy-start.5 = (f32[2,4,128,1024]{3,2,1,0:T(8,128)S(1)}, f32[2,4,128,1024]{3,2,1,0:T(8,128)}, u32[]{:S(2)}) copy-start(f32[2,4,128,1024]{3,2,1,0:T(8,128)} %copy-done.4) | copy-start | bytes 12582916

commit v6 on v5

--- a/solution.py
+++ b/solution.py
@@ -333,9 +333,12 @@
     local = (fields, below, above, strat_sq[:, None], high, low)
     early = local_part(*local, 0, group, group)
     part = local_part(*local, group, group, group)
-    source, early, part, first = lax.optimization_barrier((flat, early, part, first))
+    source, early, part = lax.optimization_barrier((flat, early, part))
     speed_u = source[: lines * levels]
-    second = {k: ahead(block_of(source, 1, k), k) for k in order}
+    near_first = order[::-1]
+    cut = [block_of(source, 1, k) for k in near_first]
+    cut, first = lax.optimization_barrier((cut, first))
+    second = {k: ahead(block, k) for k, block in zip(near_first, cut)}
     outs = far_whole(first, high, low, me)
     outs, blocks = lax.optimization_barrier((outs, list(second.values())))
     second = dict(zip(second, blocks))

time: 200 us -> 198 us (0.990)
  no operation moved by 1% of the time
where the time goes in v6:
time: 198 us
  Pallas kernels  92 us (46%)
  starting transfers between devices  50.9 us (26%)
  waiting for transfers between devices  40.5 us (20%)
  local copies, waits for them, and re-layouts  14.1 us (7%)
    ppermute x21, starting transfers between devices, ahead(): lax.ppermute(block, 'gx', [(i, (i + k) % devices) for i in range(devices)])  39.9 us
    pallas_call x1, Pallas kernels, far_whole(): pl.pallas_call(functools.partial(far_whole_body, devices), grid_spec=pltp...  33.2 us
    ppermute x21, waiting for transfers between devices, ahead(): lax.ppermute(block, 'gx', [(i, (i + k) % devices) for i in range(devices)])  32.8 us
    pallas_call x1, Pallas kernels, far_slopes(): pl.pallas_call(functools.partial(far_body, devices, shifts), grid_spec=pl...  31.2 us
    pallas_call x2, Pallas kernels, local_part(): pl.pallas_call(functools.partial(local_body, base), grid=(lines, count),...  20.5 us
    unnamed x22, local copies, waits for them, and re-layouts  8.67 us
    all_to_all x1, waiting for transfers between devices, body(): lax.all_to_all(flat[:held].reshape(devices, rows, width), 'gx', split_axi...  7.69 us
    all_to_all x1, starting transfers between devices, body(): lax.all_to_all(flat[:held].reshape(devices, rows, width), 'gx', split_axi...  5.64 us
  transfers between devices with their start and end apart: 24, of which 7 were waited for; matrix products, arithmetic and copies ran while one was open for 1% of the time, Pallas kernels for 45%

profile of v6, /device:TPU:9, one launch (start us, length us, event | category | flops | bytes accessed | tf_op | source)
XLA Modules:
  0.0 197.9 jit_solution(3508146797864353811)
XLA Ops:
  0.0 3.1 %slice.16 = bf16[2,4,128,1024]{3,2,1,0:T(8,128)(2,1)} slice(bf16[4,4,128,1024]{3,2,1,0:T(8,128)(2,1)} %b_ref.3), slice={[0:2], [0:4], [0:128], [0:1024]} | slice | bytes 4194304 | tf_op jit(solution)/shard_map/slice | solution.py:329
  3.1 5.6 %all-to-all-start = ((bf16[8,128,1024]{2,1,0:T(8,128)(2,1)}), bf16[8,128,1024]{2,1,0:T(8,128)(2,1)}, u32[]{:S(2)}, u32[]{:S(2)}) async-start(bf16[8,128,1024]{2,1,0:T(8,128)(2,1)} %bitcast.4), calls=%async_computation | async-start | bytes 4194304 | tf_op jit(solution)/shard_map/all_to_all | solution.py:328
  8.7 1.1 fusion
  9.9 1.3 collective-permute-start.1
  11.2 4.0 %collective-permute-start = (bf16[4,4,4,1024]{3,2,1,0:T(4,128)(2,1)S(1)}, bf16[4,4,4,1024]{3,2,1,0:T(4,128)(2,1)S(1)}, u32[]{:S(2)}, u32[]{:S(2)}) collective-permute-start(bf16[4,4,4,1024]{3,2,1,0:T(4,128)(2,1)S(1)} %get-tuple-element.115), channel_id=1, source_target_pairs={{0,1},{1,2},{2,3},{4,5},{5,6},{6,7},{8,9},{9,10},{10,11},{12,13},{... | collective-permute-start | bytes 393224 | tf_op jit(solution)/shard_map/ppermute | solution.py:300
  15.3 0.1 copy.5.strat_ref
  15.4 2.6 %shard_map.37 = (bf16[128,9088]{1,0:T(8,128)(2,1)S(1)}, bf16[128,9088]{1,0:T(8,128)(2,1)S(1)}) custom-call(f32[1,8192]{1,0:T(1,128)S(1)} %copy-done.9), custom_call_target="tpu_custom_call" | custom-call | flops 4194304 | bytes 4194304 | tf_op jit(solution)/shard_map/pallas_call | solution.py:56
  18.0 0.0 collective-permute-done.1.above_ref
  18.0 0.0 collective-permute-done.below_ref
  18.0 0.0 copy-start
  18.1 3.0 %copy-done = bf16[4,4,128,1024]{3,2,1,0:T(8,128)(2,1)S(1)} copy-done((bf16[4,4,128,1024]{3,2,1,0:T(8,128)(2,1)S(1)}, bf16[4,4,128,1024]{3,2,1,0:T(8,128)(2,1)}, u32[]{:S(2)}) %copy-start) | copy-done | bytes 4194328
  21.1 10.2 %shard_map.39 = f32[2,4,128,1024]{3,2,1,0:T(8,128)S(1)} custom-call(bf16[4,4,128,1024]{3,2,1,0:T(8,128)(2,1)S(1)} %copy-done, bf16[4,4,128,1024]{3,2,1,0:T(8,128)(2,1)S(1)} %copy-done, bf16[4,4,128,1024]{3,2,1,0:T(8,128)(2,1)S(1)} %copy-done, bf16[4,4,128,1024]{3,2,1,0:T(8,128)(2,1)S(1)} %copy-done, ...), custom_call_target="tpu_custom_call" | custom-call | flops 4294967296 | bytes 8388608 | tf_op jit(solution)/shard_map/pallas_call | solution.py:219
  31.3 2.0 copy-done.4
  33.3 10.2 %shard_map.38 = f32[2,4,128,1024]{3,2,1,0:T(8,128)S(1)} custom-call(bf16[4,4,128,1024]{3,2,1,0:T(8,128)(2,1)S(1)} %copy-done, bf16[4,4,128,1024]{3,2,1,0:T(8,128)(2,1)S(1)} %copy-done, bf16[4,4,128,1024]{3,2,1,0:T(8,128)(2,1)S(1)} %copy-done, bf16[4,4,128,1024]{3,2,1,0:T(8,128)(2,1)S(1)} %copy-done, ...), custom_call_target="tpu_custom_call" | custom-call | flops 4294967296 | bytes 8388608 | tf_op jit(solution)/shard_map/pallas_call | solution.py:219
  43.6 0.0 copy-start.2
  43.6 2.0 %copy-done.2 = f32[2,4,128,1024]{3,2,1,0:T(8,128)} copy-done((f32[2,4,128,1024]{3,2,1,0:T(8,128)}, f32[2,4,128,1024]{3,2,1,0:T(8,128)S(1)}, u32[]{:S(2)}) %copy-start.2) | copy-done | bytes 4194328
  45.6 1.0 constant_dynamic-slice_fusion
  46.6 7.7 %all-to-all-done = bf16[8,128,1024]{2,1,0:T(8,128)(2,1)} async-done(((bf16[8,128,1024]{2,1,0:T(8,128)(2,1)}), bf16[8,128,1024]{2,1,0:T(8,128)(2,1)}, u32[]{:S(2)}, u32[]{:S(2)}) %all-to-all-start) | async-done | bytes 2097184 | tf_op jit(solution)/shard_map/all_to_all | solution.py:328
  54.3 0.4 collective-permute-start.2
  54.7 1.3 collective-permute-start.3
  56.0 2.9 %collective-permute-start.4 = (bf16[128,1024]{1,0:T(8,128)(2,1)}, bf16[128,1024]{1,0:T(8,128)(2,1)S(1)}, u32[]{:S(2)}, u32[]{:S(2)}) collective-permute-start(bf16[128,1024]{1,0:T(8,128)(2,1)} %get-tuple-element.71), channel_id=1, source_target_pairs={{0,24},{4,28},{8,0},{12,4},{16,8},{20,12},{24,16},{28,20},{1,25},{... | collective-permute-start | bytes 786440 | tf_op jit(solution)/shard_map/ppermute | solution.py:322
  58.9 0.0 collective-permute-start.5
  58.9 2.0 collective-permute-start.6
  60.8 0.8 collective-permute-done.2.refs_1_
  61.6 0.4 collective-permute-start.7
  62.0 0.0 collective-permute-done.3.refs_2_
  62.0 6.1 %collective-permute-start.8 = (bf16[128,1024]{1,0:T(8,128)(2,1)S(1)}, bf16[128,1024]{1,0:T(8,128)(2,1)S(1)}, u32[]{:S(2)}, u32[]{:S(2)}) collective-permute-start(bf16[128,1024]{1,0:T(8,128)(2,1)S(1)} %get-tuple-element.75), channel_id=1, source_target_pairs={{0,16},{4,20},{8,24},{12,28},{16,0},{20,4},{24,8},{28,12},{1,17},{... | collective-permute-start | bytes 786440 | tf_op jit(solution)/shard_map/ppermute | solution.py:322
  68.1 1.7 copy-done.7
  69.8 33.2 %shard_map.40 = (bf16[128,1024]{1,0:T(8,128)(2,1)S(1)}, bf16[128,1024]{1,0:T(8,128)(2,1)S(1)}, bf16[128,1024]{1,0:T(8,128)(2,1)S(1)}, bf16[128,1024]{1,0:T(8,128...) custom-call(s32[1]{0:T(128)} %bitcast.me_ref, ...), custom_call_target="tpu_custom_call" | custom-call | flops 30064771072 | bytes 8847360 | tf_op jit(solution)/shard_map/pallas_call | solution.py:113
  103.0 0.0 collective-permute-done.4.refs_3_
  103.0 0.0 collective-permute-done.5.refs_4_
  103.1 0.0 collective-permute-done.6.refs_5_
  103.1 0.0 collective-permute-done.7.refs_6_
  103.1 0.0 collective-permute-done.8.refs_7_
  103.1 0.1 collective-permute-start.9
  103.2 4.4 %collective-permute-start.11 = (bf16[128,1024]{1,0:T(8,128)(2,1)S(1)}, bf16[128,1024]{1,0:T(8,128)(2,1)S(1)}, u32[]{:S(2)}, u32[]{:S(2)}) collective-permute-start(bf16[128,1024]{1,0:T(8,128)(2,1)S(1)} %get-tuple-element.88), channel_id=1, source_target_pairs={{0,20},{4,24},{8,28},{12,0},{16,4},{20,8},{24,12},{28,16},{1,21},{... | collective-permute-start | bytes 786440 | tf_op jit(solution)/shard_map/ppermute | solution.py:322
  107.6 0.0 collective-permute-start.13
  107.6 0.4 collective-permute-start.15
  108.0 1.1 collective-permute-start.17
  109.1 31.2 %shard_map.41 = (bf16[128,1024]{1,0:T(8,128)(2,1)S(1)}, bf16[128,1024]{1,0:T(8,128)(2,1)S(1)}, bf16[128,1024]{1,0:T(8,128)(2,1)S(1)}, bf16[128,1024]{1,0:T(8,128...) custom-call(s32[1]{0:T(128)} %bitcast.me_ref, ...), custom_call_target="tpu_custom_call" | custom-call | flops 30064771072 | bytes 8847360 | tf_op jit(solution)/shard_map/pallas_call | solution.py:158
  140.3 0.0 collective-permute-done.9.refs_1_
  140.3 0.8 collective-permute-start.19
  141.1 0.0 collective-permute-done.11.refs_2_
  141.1 1.2 collective-permute-start.21
  142.3 0.0 collective-permute-done.13.refs_3_
  142.3 4.0 %collective-permute-start.10 = (bf16[128,1024]{1,0:T(8,128)(2,1)S(1)}, bf16[128,1024]{1,0:T(8,128)(2,1)S(1)}, u32[]{:S(2)}, u32[]{:S(2)}) collective-permute-start(bf16[128,1024]{1,0:T(8,128)(2,1)S(1)} %get-tuple-element.86), channel_id=1, source_target_pairs={{0,16},{4,20},{8,24},{12,28},{16,0},{20,4},{24,8},{28,12},{1,17},{... | collective-permute-start | bytes 786440 | tf_op jit(solution)/shard_map/ppermute | solution.py:322
  146.3 0.5 collective-permute-done.15.refs_4_
  146.8 0.0 collective-permute-start.12
  146.8 0.0 collective-permute-done.17.refs_5_
  146.8 2.6 %collective-permute-start.14 = (bf16[128,1024]{1,0:T(8,128)(2,1)S(1)}, bf16[128,1024]{1,0:T(8,128)(2,1)S(1)}, u32[]{:S(2)}, u32[]{:S(2)}) collective-permute-start(bf16[128,1024]{1,0:T(8,128)(2,1)S(1)} %get-tuple-element.92), channel_id=1, source_target_pairs={{0,12},{4,16},{8,20},{12,24},{16,28},{20,0},{24,4},{28,8},{1,13},{... | collective-permute-start | bytes 786440 | tf_op jit(solution)/shard_map/ppermute | solution.py:322
  149.5 1.0 collective-permute-done.19.refs_6_
  150.5 0.0 collective-permute-start.16
  150.5 0.0 collective-permute-done.21.refs_7_
  150.5 3.6 %collective-permute-start.18 = (bf16[128,1024]{1,0:T(8,128)(2,1)S(1)}, bf16[128,1024]{1,0:T(8,128)(2,1)S(1)}, u32[]{:S(2)}, u32[]{:S(2)}) collective-permute-start(bf16[128,1024]{1,0:T(8,128)(2,1)S(1)} %get-tuple-element.98), channel_id=1, source_target_pairs={{0,8},{4,12},{8,16},{12,20},{16,24},{20,28},{24,0},{28,4},{1,9},{5... | collective-permute-start | bytes 786440 | tf_op jit(solution)/shard_map/ppermute | solution.py:322
  154.1 19.7 %collective-permute-done.10.refs_1_ = bf16[128,1024]{1,0:T(8,128)(2,1)S(1)} collective-permute-done((bf16[128,1024]{1,0:T(8,128)(2,1)S(1)}, bf16[128,1024]{1,0:T(8,128)(2,1)S(1)}, u32[]{:S(2)}, u32[]{:S(2)}) %collective-permute-start.10) | collective-permute-done | bytes 262176 | tf_op jit(solution)/shard_map/ppermute | solution.py:322
  173.8 0.7 collective-permute-start.20
  174.5 7.9 %collective-permute-start.22 = (bf16[128,1024]{1,0:T(8,128)(2,1)S(1)}, bf16[128,1024]{1,0:T(8,128)(2,1)S(1)}, u32[]{:S(2)}, u32[]{:S(2)}) collective-permute-start(bf16[128,1024]{1,0:T(8,128)(2,1)S(1)} %get-tuple-element.104), channel_id=1, source_target_pairs={{0,4},{4,8},{8,12},{12,16},{16,20},{20,24},{24,28},{28,0},{1,5},{5... | collective-permute-start | bytes 786440 | tf_op jit(solution)/shard_map/ppermute | solution.py:322
  182.4 0.1 slice.15.u_ref
  182.5 2.3 %shard_map.42.refs_8_ = f32[2048,1024]{1,0:T(8,128)} custom-call(s32[1]{0:T(128)} %bitcast.me_ref, f32[1024,1024]{1,0:T(8,128)S(1)} %bitcast.11, bf16[512,1024]{1,0:T(8,128)(2,1)S(1)} %slice.15.u_ref, bf16[128,1024]{1,0:T(8,128)(2,1)S(1)} %get-tuple-element.106.refs_0_, bf16[128,1024]{1,0:T(8,128)(2,1)S(1)} %collective-permute-done.9.refs_1_, ...), custom_call_target="tpu_custom_call" | custom-call | flops 2097152 | bytes 12582912 | tf_op jit(solution)/shard_map/pallas_call | solution.py:270
  184.8 0.0 collective-permute-done.14.refs_3_
  184.8 9.8 %collective-permute-done.16.refs_4_ = bf16[128,1024]{1,0:T(8,128)(2,1)S(1)} collective-permute-done((bf16[128,1024]{1,0:T(8,128)(2,1)S(1)}, bf16[128,1024]{1,0:T(8,128)(2,1)S(1)}, u32[]{:S(2)}, u32[]{:S(2)}) %collective-permute-start.16) | collective-permute-done | bytes 262176 | tf_op jit(solution)/shard_map/ppermute | solution.py:322
  194.6 0.0 collective-permute-done.18.refs_5_
  194.6 1.0 collective-permute-done.20.refs_6_
  195.6 2.2 %shard_map.43 = f32[2048,1024]{1,0:T(8,128)} custom-call(s32[1]{0:T(128)} %bitcast.me_ref, f32[1024,1024]{1,0:T(8,128)S(1)} %bitcast.12, bf16[512,1024]{1,0:T(8,128)(2,1)S(1)} %slice.15.u_ref, bf16[128,1024]{1,0:T(8,128)(2,1)S(1)} %get-tuple-element.83.refs_0_, ...), custom_call_target="tpu_custom_call", output_to_operand_aliasing={{}: (11, {})} | custom-call | flops 2097152 | bytes 12582912 | tf_op jit(solution)/shard_map/pallas_call | solution.py:270
  (18 shorter events, 0.0 us)
Async XLA Ops:
  0.0 15.4 %copy-start.9 = (f32[1,8192]{1,0:T(1,128)S(1)}, f32[1,8192]{1,0:T(1,128)}, u32[]{:S(2)}) copy-start(f32[1,8192]{1,0:T(1,128)} %constant.64.row_ref) | copy-start | bytes 98308
  0.0 15.3 %copy-start.10 = (f32[128]{0:T(128)S(1)}, f32[128]{0:T(128)}, u32[]{:S(2)}) copy-start(f32[128]{0:T(128)} %param.4) | copy-start | bytes 1540
  3.1 51.1 %all-to-all-start = ((bf16[8,128,1024]{2,1,0:T(8,128)(2,1)}), bf16[8,128,1024]{2,1,0:T(8,128)(2,1)}, u32[]{:S(2)}, u32[]{:S(2)}) async-start(bf16[8,128,1024]{2,1,0:T(8,128)(2,1)} %bitcast.4), calls=%async_computation | async-start | bytes 4194304 | tf_op jit(solution)/shard_map/all_to_all | solution.py:328
  9.9 8.1 %collective-permute-start.1 = (bf16[4,4,4,1024]{3,2,1,0:T(4,128)(2,1)S(1)}, bf16[4,4,4,1024]{3,2,1,0:T(4,128)(2,1)S(1)}, u32[]{:S(2)}, u32[]{:S(2)}) collective-permute-start(bf16[4,4,4,1024]{3,2,1,0:T(4,128)(2,1)S(1)} %get-tuple-element.114), channel_id=1, source_target_pairs={{1,0},{2,1},{3,2},{5,4},{6,5},{7,6},{9,8},{10,9},{11,10},{13,12},{... | collective-permute-start | bytes 393224 | tf_op jit(solution)/shard_map/ppermute | solution.py:301
  11.2 6.9 %collective-permute-start = (bf16[4,4,4,1024]{3,2,1,0:T(4,128)(2,1)S(1)}, bf16[4,4,4,1024]{3,2,1,0:T(4,128)(2,1)S(1)}, u32[]{:S(2)}, u32[]{:S(2)}) collective-permute-start(bf16[4,4,4,1024]{3,2,1,0:T(4,128)(2,1)S(1)} %get-tuple-element.115), channel_id=1, source_target_pairs={{0,1},{1,2},{2,3},{4,5},{5,6},{6,7},{8,9},{9,10},{10,11},{12,13},{... | collective-permute-start | bytes 393224 | tf_op jit(solution)/shard_map/ppermute | solution.py:300
  18.0 13.3 %copy-start.6 = (bf16[128,9088]{1,0:T(8,128)(2,1)}, bf16[128,9088]{1,0:T(8,128)(2,1)S(1)}, u32[]{:S(2)}) copy-start(bf16[128,9088]{1,0:T(8,128)(2,1)S(1)} %get-tuple-element.57.low_ref.refs_9_) | copy-start | bytes 6979588
  18.0 3.0 %copy-start = (bf16[4,4,128,1024]{3,2,1,0:T(8,128)(2,1)S(1)}, bf16[4,4,128,1024]{3,2,1,0:T(8,128)(2,1)}, u32[]{:S(2)}) copy-start(bf16[4,4,128,1024]{3,2,1,0:T(8,128)(2,1)} %b_ref.3) | copy-start | bytes 12582916
  31.3 2.0 copy-start.4
  43.6 2.0 %copy-start.2 = (f32[2,4,128,1024]{3,2,1,0:T(8,128)}, f32[2,4,128,1024]{3,2,1,0:T(8,128)S(1)}, u32[]{:S(2)}) copy-start(f32[2,4,128,1024]{3,2,1,0:T(8,128)S(1)} %shard_map.38) | copy-start | bytes 12582916
  54.3 7.4 %collective-permute-start.2 = (bf16[128,1024]{1,0:T(8,128)(2,1)}, bf16[128,1024]{1,0:T(8,128)(2,1)S(1)}, u32[]{:S(2)}, u32[]{:S(2)}) collective-permute-start(bf16[128,1024]{1,0:T(8,128)(2,1)} %get-tuple-element.69), channel_id=1, source_target_pairs={{0,28},{4,0},{8,4},{12,8},{16,12},{20,16},{24,20},{28,24},{1,29},{... | collective-permute-start | bytes 786440 | tf_op jit(solution)/shard_map/ppermute | solution.py:322
  54.7 7.3 %collective-permute-start.3 = (bf16[128,1024]{1,0:T(8,128)(2,1)}, bf16[128,1024]{1,0:T(8,128)(2,1)S(1)}, u32[]{:S(2)}, u32[]{:S(2)}) collective-permute-start(bf16[128,1024]{1,0:T(8,128)(2,1)} %get-tuple-element.70), channel_id=1, source_target_pairs={{0,4},{4,8},{8,12},{12,16},{16,20},{20,24},{24,28},{28,0},{1,5},{5... | collective-permute-start | bytes 786440 | tf_op jit(solution)/shard_map/ppermute | solution.py:322
  56.0 47.0 %collective-permute-start.4 = (bf16[128,1024]{1,0:T(8,128)(2,1)}, bf16[128,1024]{1,0:T(8,128)(2,1)S(1)}, u32[]{:S(2)}, u32[]{:S(2)}) collective-permute-start(bf16[128,1024]{1,0:T(8,128)(2,1)} %get-tuple-element.71), channel_id=1, source_target_pairs={{0,24},{4,28},{8,0},{12,4},{16,8},{20,12},{24,16},{28,20},{1,25},{... | collective-permute-start | bytes 786440 | tf_op jit(solution)/shard_map/ppermute | solution.py:322
  58.9 44.2 %collective-permute-start.5 = (bf16[128,1024]{1,0:T(8,128)(2,1)S(1)}, bf16[128,1024]{1,0:T(8,128)(2,1)S(1)}, u32[]{:S(2)}, u32[]{:S(2)}) collective-permute-start(bf16[128,1024]{1,0:T(8,128)(2,1)S(1)} %get-tuple-element.72), channel_id=1, source_target_pairs={{0,8},{4,12},{8,16},{12,20},{16,24},{20,28},{24,0},{28,4},{1,9},{5... | collective-permute-start | bytes 786440 | tf_op jit(solution)/shard_map/ppermute | solution.py:322
  58.9 44.2 %collective-permute-start.6 = (bf16[128,1024]{1,0:T(8,128)(2,1)S(1)}, bf16[128,1024]{1,0:T(8,128)(2,1)S(1)}, u32[]{:S(2)}, u32[]{:S(2)}) collective-permute-start(bf16[128,1024]{1,0:T(8,128)(2,1)S(1)} %get-tuple-element.73), channel_id=1, source_target_pairs={{0,20},{4,24},{8,28},{12,0},{16,4},{20,8},{24,12},{28,16},{1,21},{... | collective-permute-start | bytes 786440 | tf_op jit(solution)/shard_map/ppermute | solution.py:322
  61.6 41.4 %collective-permute-start.7 = (bf16[128,1024]{1,0:T(8,128)(2,1)S(1)}, bf16[128,1024]{1,0:T(8,128)(2,1)S(1)}, u32[]{:S(2)}, u32[]{:S(2)}) collective-permute-start(bf16[128,1024]{1,0:T(8,128)(2,1)S(1)} %get-tuple-element.74), channel_id=1, source_target_pairs={{0,12},{4,16},{8,20},{12,24},{16,28},{20,0},{24,4},{28,8},{1,13},{... | collective-permute-start | bytes 786440 | tf_op jit(solution)/shard_map/ppermute | solution.py:322
  62.0 41.1 %collective-permute-start.8 = (bf16[128,1024]{1,0:T(8,128)(2,1)S(1)}, bf16[128,1024]{1,0:T(8,128)(2,1)S(1)}, u32[]{:S(2)}, u32[]{:S(2)}) collective-permute-start(bf16[128,1024]{1,0:T(8,128)(2,1)S(1)} %get-tuple-element.75), channel_id=1, source_target_pairs={{0,16},{4,20},{8,24},{12,28},{16,0},{20,4},{24,8},{28,12},{1,17},{... | collective-permute-start | bytes 786440 | tf_op jit(solution)/shard_map/ppermute | solution.py:322
  68.1 1.7 copy-start.7
  69.8 39.3 %copy-start.1 = (bf16[4,4,128,1024]{3,2,1,0:T(8,128)(2,1)S(1)}, bf16[4,4,128,1024]{3,2,1,0:T(8,128)(2,1)}, u32[]{:S(2)}) copy-start(bf16[4,4,128,1024]{3,2,1,0:T(8,128)(2,1)} %b_ref.3) | copy-start | bytes 12582916
  69.8 39.3 %copy-start.8 = (bf16[128,9088]{1,0:T(8,128)(2,1)S(1)}, bf16[128,9088]{1,0:T(8,128)(2,1)}, u32[]{:S(2)}) copy-start(bf16[128,9088]{1,0:T(8,128)(2,1)} %copy-done.6) | copy-start | bytes 6979588
  103.1 37.2 %collective-permute-start.9 = (bf16[128,1024]{1,0:T(8,128)(2,1)S(1)}, bf16[128,1024]{1,0:T(8,128)(2,1)S(1)}, u32[]{:S(2)}, u32[]{:S(2)}) collective-permute-start(bf16[128,1024]{1,0:T(8,128)(2,1)S(1)} %get-tuple-element.85), channel_id=1, source_target_pairs={{0,16},{4,20},{8,24},{12,28},{16,0},{20,4},{24,8},{28,12},{1,17},{... | collective-permute-start | bytes 786440 | tf_op jit(solution)/shard_map/ppermute | solution.py:322
  103.2 37.9 %collective-permute-start.11 = (bf16[128,1024]{1,0:T(8,128)(2,1)S(1)}, bf16[128,1024]{1,0:T(8,128)(2,1)S(1)}, u32[]{:S(2)}, u32[]{:S(2)}) collective-permute-start(bf16[128,1024]{1,0:T(8,128)(2,1)S(1)} %get-tuple-element.88), channel_id=1, source_target_pairs={{0,20},{4,24},{8,28},{12,0},{16,4},{20,8},{24,12},{28,16},{1,21},{... | collective-permute-start | bytes 786440 | tf_op jit(solution)/shard_map/ppermute | solution.py:322
  107.6 34.7 %collective-permute-start.13 = (bf16[128,1024]{1,0:T(8,128)(2,1)S(1)}, bf16[128,1024]{1,0:T(8,128)(2,1)S(1)}, u32[]{:S(2)}, u32[]{:S(2)}) collective-permute-start(bf16[128,1024]{1,0:T(8,128)(2,1)S(1)} %get-tuple-element.91), channel_id=1, source_target_pairs={{0,12},{4,16},{8,20},{12,24},{16,28},{20,0},{24,4},{28,8},{1,13},{... | collective-permute-start | bytes 786440 | tf_op jit(solution)/shard_map/ppermute | solution.py:322
  107.6 39.2 %collective-permute-start.15 = (bf16[128,1024]{1,0:T(8,128)(2,1)S(1)}, bf16[128,1024]{1,0:T(8,128)(2,1)S(1)}, u32[]{:S(2)}, u32[]{:S(2)}) collective-permute-start(bf16[128,1024]{1,0:T(8,128)(2,1)S(1)} %get-tuple-element.94), channel_id=1, source_target_pairs={{0,24},{4,28},{8,0},{12,4},{16,8},{20,12},{24,16},{28,20},{1,25},{... | collective-permute-start | bytes 786440 | tf_op jit(solution)/shard_map/ppermute | solution.py:322
  108.0 38.8 %collective-permute-start.17 = (bf16[128,1024]{1,0:T(8,128)(2,1)S(1)}, bf16[128,1024]{1,0:T(8,128)(2,1)S(1)}, u32[]{:S(2)}, u32[]{:S(2)}) collective-permute-start(bf16[128,1024]{1,0:T(8,128)(2,1)S(1)} %get-tuple-element.97), channel_id=1, source_target_pairs={{0,8},{4,12},{8,16},{12,20},{16,24},{20,28},{24,0},{28,4},{1,9},{5... | collective-permute-start | bytes 786440 | tf_op jit(solution)/shard_map/ppermute | solution.py:322
  109.1 73.4 %copy-start.3 = (f32[2,4,128,1024]{3,2,1,0:T(8,128)S(1)}, f32[2,4,128,1024]{3,2,1,0:T(8,128)}, u32[]{:S(2)}) copy-start(f32[2,4,128,1024]{3,2,1,0:T(8,128)} %copy-done.2) | copy-start | bytes 12582916
  140.3 10.2 %collective-permute-start.19 = (bf16[128,1024]{1,0:T(8,128)(2,1)S(1)}, bf16[128,1024]{1,0:T(8,128)(2,1)S(1)}, u32[]{:S(2)}, u32[]{:S(2)}) collective-permute-start(bf16[128,1024]{1,0:T(8,128)(2,1)S(1)} %get-tuple-element.100), channel_id=1, source_target_pairs={{0,28},{4,0},{8,4},{12,8},{16,12},{20,16},{24,20},{28,24},{1,29},{... | collective-permute-start | bytes 786440 | tf_op jit(solution)/shard_map/ppermute | solution.py:322
  141.1 9.4 %collective-permute-start.21 = (bf16[128,1024]{1,0:T(8,128)(2,1)S(1)}, bf16[128,1024]{1,0:T(8,128)(2,1)S(1)}, u32[]{:S(2)}, u32[]{:S(2)}) collective-permute-start(bf16[128,1024]{1,0:T(8,128)(2,1)S(1)} %get-tuple-element.103), channel_id=1, source_target_pairs={{0,4},{4,8},{8,12},{12,16},{16,20},{20,24},{24,28},{28,0},{1,5},{5... | collective-permute-start | bytes 786440 | tf_op jit(solution)/shard_map/ppermute | solution.py:322
  142.3 31.5 %collective-permute-start.10 = (bf16[128,1024]{1,0:T(8,128)(2,1)S(1)}, bf16[128,1024]{1,0:T(8,128)(2,1)S(1)}, u32[]{:S(2)}, u32[]{:S(2)}) collective-permute-start(bf16[128,1024]{1,0:T(8,128)(2,1)S(1)} %get-tuple-element.86), channel_id=1, source_target_pairs={{0,16},{4,20},{8,24},{12,28},{16,0},{20,4},{24,8},{28,12},{1,17},{... | collective-permute-start | bytes 786440 | tf_op jit(solution)/shard_map/ppermute | solution.py:322
  146.8 27.7 %collective-permute-start.12 = (bf16[128,1024]{1,0:T(8,128)(2,1)S(1)}, bf16[128,1024]{1,0:T(8,128)(2,1)S(1)}, u32[]{:S(2)}, u32[]{:S(2)}) collective-permute-start(bf16[128,1024]{1,0:T(8,128)(2,1)S(1)} %get-tuple-element.89), channel_id=1, source_target_pairs={{0,20},{4,24},{8,28},{12,0},{16,4},{20,8},{24,12},{28,16},{1,21},{... | collective-permute-start | bytes 786440 | tf_op jit(solution)/shard_map/ppermute | solution.py:322
  146.8 38.0 %collective-permute-start.14 = (bf16[128,1024]{1,0:T(8,128)(2,1)S(1)}, bf16[128,1024]{1,0:T(8,128)(2,1)S(1)}, u32[]{:S(2)}, u32[]{:S(2)}) collective-permute-start(bf16[128,1024]{1,0:T(8,128)(2,1)S(1)} %get-tuple-element.92), channel_id=1, source_target_pairs={{0,12},{4,16},{8,20},{12,24},{16,28},{20,0},{24,4},{28,8},{1,13},{... | collective-permute-start | bytes 786440 | tf_op jit(solution)/shard_map/ppermute | solution.py:322
  150.5 44.2 %collective-permute-start.16 = (bf16[128,1024]{1,0:T(8,128)(2,1)S(1)}, bf16[128,1024]{1,0:T(8,128)(2,1)S(1)}, u32[]{:S(2)}, u32[]{:S(2)}) collective-permute-start(bf16[128,1024]{1,0:T(8,128)(2,1)S(1)} %get-tuple-element.95), channel_id=1, source_target_pairs={{0,24},{4,28},{8,0},{12,4},{16,8},{20,12},{24,16},{28,20},{1,25},{... | collective-permute-start | bytes 786440 | tf_op jit(solution)/shard_map/ppermute | solution.py:322
  150.5 44.2 %collective-permute-start.18 = (bf16[128,1024]{1,0:T(8,128)(2,1)S(1)}, bf16[128,1024]{1,0:T(8,128)(2,1)S(1)}, u32[]{:S(2)}, u32[]{:S(2)}) collective-permute-start(bf16[128,1024]{1,0:T(8,128)(2,1)S(1)} %get-tuple-element.98), channel_id=1, source_target_pairs={{0,8},{4,12},{8,16},{12,20},{16,24},{20,28},{24,0},{28,4},{1,9},{5... | collective-permute-start | bytes 786440 | tf_op jit(solution)/shard_map/ppermute | solution.py:322
  173.8 21.9 %collective-permute-start.20 = (bf16[128,1024]{1,0:T(8,128)(2,1)S(1)}, bf16[128,1024]{1,0:T(8,128)(2,1)S(1)}, u32[]{:S(2)}, u32[]{:S(2)}) collective-permute-start(bf16[128,1024]{1,0:T(8,128)(2,1)S(1)} %get-tuple-element.101), channel_id=1, source_target_pairs={{0,28},{4,0},{8,4},{12,8},{16,12},{20,16},{24,20},{28,24},{1,29},{... | collective-permute-start | bytes 786440 | tf_op jit(solution)/shard_map/ppermute | solution.py:322
  174.5 21.1 %collective-permute-start.22 = (bf16[128,1024]{1,0:T(8,128)(2,1)S(1)}, bf16[128,1024]{1,0:T(8,128)(2,1)S(1)}, u32[]{:S(2)}, u32[]{:S(2)}) collective-permute-start(bf16[128,1024]{1,0:T(8,128)(2,1)S(1)} %get-tuple-element.104), channel_id=1, source_target_pairs={{0,4},{4,8},{8,12},{12,16},{16,20},{20,24},{24,28},{28,0},{1,5},{5... | collective-permute-start | bytes 786440 | tf_op jit(solution)/shard_map/ppermute | solution.py:322
  182.5 13.1 %copy-start.5 = (f32[2,4,128,1024]{3,2,1,0:T(8,128)S(1)}, f32[2,4,128,1024]{3,2,1,0:T(8,128)}, u32[]{:S(2)}) copy-start(f32[2,4,128,1024]{3,2,1,0:T(8,128)} %copy-done.4) | copy-start | bytes 12582916
